TPU v7x, 1024 devices: a whole 8x8x8 slice. The times are simulated.
1024 devices in a mesh: dp: 8 (over x), group: 8 (over y), local: 16 (over z, core).
Axes of the slice: x: 8, y: 8, z: 8, core: 2. Of those that a mesh axis runs over, the one named last changes fastest.
Arguments:
- tokens: bfloat16 [16384, 1024], P(('dp', 'group', 'local')), may hold values from -6 to 6
- cotangent: bfloat16 [16384, 1024], P(('dp', 'group', 'local')), may hold values from -6 to 6
- expert_ids: int32 [16384, 8], P(('dp', 'group', 'local')), may hold values from 0 to 127, as said below
- router_weights: bfloat16 [16384, 8], P(('dp', 'group', 'local')), may hold values from 0.049804688 to 1
- gate_weight: bfloat16 [128, 1024, 384], P(('group', 'local'), 'dp'), may hold values from -0.1875 to 0.1875
- up_weight: bfloat16 [128, 1024, 384], P(('group', 'local'), 'dp'), may hold values from -0.1875 to 0.1875
- down_weight: bfloat16 [128, 384, 1024], P(('group', 'local'), None, 'dp'), may hold values from -0.3125 to 0.3125
Outputs:
- layer_output: bfloat16 [16384, 1024], P(('dp', 'group', 'local'))
- token_grads: bfloat16 [16384, 1024], P(('dp', 'group', 'local'))
- router_grads: bfloat16 [16384, 8], P(('dp', 'group', 'local'))
- gate_grad: bfloat16 [128, 1024, 384], P(('group', 'local'), 'dp')
- up_grad: bfloat16 [128, 1024, 384], P(('group', 'local'), 'dp')
- down_grad: bfloat16 [128, 384, 1024], P(('group', 'local'), None, 'dp')
Inputs may be any that keep to these rules, and one draw needn't show every extreme that they name: `expert_ids`: expert e belongs to group e // 16. Columns 2j and 2j+1 of a token name two different experts of one group, and the 4 column pairs of a token name 4 different groups. Every device sends exactly 8 of its tokens to each group. For every dp index and group, one expert of the group is named by exactly 3 of the tokens that each device of that dp index sends to the group, and every other expert of the group by fewer; so at most 24 tokens reach one expert from the devices of one dp index and one local index, and that many reach the busiest one.
All inputs are finite; a program needn't handle non-finite values.
Results may differ from a plain program's by a relative error of at most 0.013.
Values may be sent and summed in bfloat16 or wider, within the bound.
No kernel may reach another device: no remote copies, remote signals or barrier semaphores. Data moves between devices by JAX's collectives and lax.ppermute only.
A program may use at most 32 MiB of HBM per device.

v0:
```python
import jax
import jax.numpy as jnp
from jax import lax
from jax.sharding import PartitionSpec as P


def gather_turned(arrays, axis, dims):
    turned = [jnp.moveaxis(a, dim, 0) for a, dim in zip(arrays, dims)]
    both = jnp.concatenate([t.reshape(len(t), -1) for t in turned], axis=1)
    out, at, gathered = (lax.all_gather(both, axis, axis=0, tiled=True), 0, [])
    for t, dim in zip(turned, dims):
        slab = out[:, at : at + t[0].size].reshape(-1, *t.shape[1:])
        gathered.append(jnp.moveaxis(slab, 0, dim))
        at += t[0].size
    return tuple(gathered)


def side_by_side(arrays, axis, split_dim, concat_dim, along):
    both = jnp.concatenate(arrays, axis=along)
    out, at, gathered = (
        lax.all_to_all(both, axis, split_axis=split_dim, concat_axis=concat_dim, tiled=True),
        0,
        [],
    )
    for a in arrays:
        gathered.append(lax.slice_in_dim(out, at, at + a.shape[along], axis=along))
        at += a.shape[along]
    return tuple(gathered)


def cut_along(value, dim, peers):
    dims = value.shape
    blocks = value.reshape(*dims[:dim], peers, dims[dim] // peers, *dims[dim + 1 :])
    return jnp.moveaxis(blocks, dim, 0)


def one_scatter(arrays, axis, dims):
    peers = lax.axis_size(axis)
    blocks = [cut_along(a, dim, peers) for a, dim in zip(arrays, dims)]
    lines = jnp.concatenate([b.reshape(peers, -1) for b in blocks], axis=1)
    rows = max(16, -(-lines.shape[1] // 1024) * 8)
    lines = jnp.pad(lines, ((0, 0), (0, rows * 128 - lines.shape[1]))).reshape(-1, 128)
    vector, at, gathered = (lax.psum_scatter(lines, axis, tiled=True).reshape(-1), 0, [])
    for b in blocks:
        part = b[0]
        gathered.append(vector[at : at + part.size].reshape(part.shape))
        at += part.size
    return tuple(gathered)


def slot_matrix(labels, bin_count, capacity):
    onehot = (labels[:, None] == jnp.arange(bin_count, dtype=jnp.int32)[None, :]).astype(jnp.int32)
    earlier = jnp.cumsum(onehot, axis=0) - onehot
    slot_rank = jnp.sum(earlier * onehot, axis=1)
    target = labels * capacity + slot_rank
    return jnp.arange(bin_count * capacity, dtype=jnp.int32)[:, None] == target[None, :]


def select_rows(chooser, row_block):
    return jnp.dot(chooser.astype(jnp.bfloat16), row_block, preferred_element_type=jnp.float32)


def expert_forward(rows_in, gate_full, up_full, down_full):
    gate_pre = jnp.dot(rows_in, gate_full, preferred_element_type=jnp.float32)
    up_pre = jnp.dot(rows_in, up_full, preferred_element_type=jnp.float32)
    sigmoid_gate = jax.nn.sigmoid(gate_pre)
    hidden = (gate_pre * sigmoid_gate * up_pre).astype(jnp.bfloat16)
    expert_out = jnp.dot(hidden, down_full, preferred_element_type=jnp.float32).astype(jnp.bfloat16)
    return ((gate_pre, up_pre, sigmoid_gate, hidden), expert_out)


def expert_backward(rows_in, grad_out, saved_state, gate_full, up_full, down_full):
    gate_pre, up_pre, sigmoid_gate, hidden = saved_state
    hidden_grad = jnp.dot(grad_out, down_full.T, preferred_element_type=jnp.float32)
    gate_pre_grad = (
        hidden_grad * up_pre * sigmoid_gate * (1.0 + gate_pre * (1.0 - sigmoid_gate))
    ).astype(jnp.bfloat16)
    up_pre_grad = (hidden_grad * gate_pre * sigmoid_gate).astype(jnp.bfloat16)
    expert_in_grad = (
        jnp.dot(gate_pre_grad, gate_full.T, preferred_element_type=jnp.float32)
        + jnp.dot(up_pre_grad, up_full.T, preferred_element_type=jnp.float32)
    ).astype(jnp.bfloat16)
    gate_term = jnp.dot(rows_in.T, gate_pre_grad, preferred_element_type=jnp.float32)
    up_term = jnp.dot(rows_in.T, up_pre_grad, preferred_element_type=jnp.float32)
    down_term = jnp.dot(hidden.T, grad_out, preferred_element_type=jnp.float32)
    return (expert_in_grad, (gate_term, up_term, down_term))


def local(tokens, cotangent, expert_ids, router_weights, gate_weight, up_weight, down_weight):
    group_count = lax.axis_size("group")
    local_count = lax.axis_size("local")
    token_count, feature_count = tokens.shape
    pair_count = expert_ids.shape[1] // 2
    per_group = token_count * pair_count // group_count
    hot_count = min(per_group, 6 * per_group // local_count)
    owner_cap = group_count * hot_count
    rows_first = group_count * per_group
    rows_second = local_count * owner_cap
    first_ids = expert_ids[:, 0::2]
    second_ids = expert_ids[:, 1::2]
    to_group = slot_matrix((first_ids // local_count).reshape(-1), group_count, per_group)
    token_pick = jnp.any(to_group.reshape(rows_first, token_count, pair_count), axis=2)
    send_rows = (
        select_rows(token_pick, tokens)
        .astype(jnp.bfloat16)
        .reshape(group_count, per_group, feature_count)
    )
    send_grads = (
        select_rows(token_pick, cotangent)
        .astype(jnp.bfloat16)
        .reshape(group_count, per_group, feature_count)
    )
    route_table = jnp.stack(
        [
            (first_ids % local_count).astype(jnp.float32),
            (second_ids % local_count).astype(jnp.float32),
            router_weights[:, 0::2].astype(jnp.float32),
            router_weights[:, 1::2].astype(jnp.float32),
        ],
        axis=2,
    )
    send_info = jnp.dot(
        to_group.astype(jnp.float32), route_table.reshape(-1, 4), precision=lax.Precision.HIGHEST
    )
    send_info = send_info.astype(jnp.bfloat16).reshape(group_count, per_group, 4)
    gate_full, up_full, down_full = gather_turned(
        (gate_weight[0], up_weight[0], down_weight[0]), "dp", (0, 0, 1)
    )

    def both_parts(first_pick, second_pick, result_block):
        result_flat = result_block.reshape(rows_second, feature_count)
        return (select_rows(first_pick, result_flat), select_rows(second_pick, result_flat))

    recv_rows, recv_grads, recv_info = side_by_side(
        (send_rows, send_grads, send_info), "group", 0, 0, 2
    )
    route_info = recv_info.reshape(rows_first, 4).astype(jnp.float32)
    labels = route_info[:, 0:2].astype(jnp.int32).reshape(-1)
    to_owner = slot_matrix(labels, local_count, owner_cap)
    paired = to_owner.reshape(rows_second, rows_first, 2)
    owner_pick = jnp.any(paired, axis=2)
    slot_scale = jnp.sum(jnp.where(to_owner, route_info[:, 2:4].reshape(-1)[None, :], 0.0), axis=1)
    owner_pick, slot_scale, first_pick, second_pick, scales = (
        owner_pick,
        slot_scale,
        paired[:, :, 0].T,
        paired[:, :, 1].T,
        route_info[:, 2:4],
    )
    picked = select_rows(owner_pick, recv_rows.reshape(rows_first, feature_count))
    owner_picked = select_rows(owner_pick, recv_grads.reshape(rows_first, feature_count))
    expert_in, grad_in = side_by_side(
        (
            picked.astype(jnp.bfloat16).reshape(local_count, owner_cap, feature_count),
            (owner_picked * slot_scale[:, None])
            .astype(jnp.bfloat16)
            .reshape(local_count, owner_cap, feature_count),
        ),
        "local",
        0,
        0,
        1,
    )
    expert_in = expert_in.reshape(rows_second, feature_count)
    grad_in = grad_in.reshape(rows_second, feature_count)
    saved_state, expert_out = expert_forward(expert_in, gate_full, up_full, down_full)
    expert_in_grad, weight_terms = expert_backward(
        expert_in, grad_in, saved_state, gate_full, up_full, down_full
    )
    returned, returned_grads = side_by_side(
        (
            expert_out.reshape(local_count, owner_cap, feature_count),
            expert_in_grad.reshape(local_count, owner_cap, feature_count),
        ),
        "local",
        0,
        0,
        1,
    )
    first_out, second_out = both_parts(first_pick, second_pick, returned)
    first_grad, second_grad = both_parts(first_pick, second_pick, returned_grads)
    summed_part = scales[:, 0:1] * first_out + scales[:, 1:2] * second_out
    grad_rows = recv_grads.reshape(rows_first, feature_count).astype(jnp.float32)
    both = jnp.stack(
        [jnp.sum(grad_rows * first_out, axis=1), jnp.sum(grad_rows * second_out, axis=1)], axis=1
    )
    summed, summed_grads, router_back = side_by_side(
        (
            summed_part.astype(jnp.bfloat16).reshape(group_count, per_group, feature_count),
            (first_grad + second_grad)
            .astype(jnp.bfloat16)
            .reshape(group_count, per_group, feature_count),
            both.astype(jnp.bfloat16).reshape(group_count, per_group, 2),
        ),
        "group",
        0,
        0,
        2,
    )
    back_pick = token_pick.T
    layer_output = select_rows(back_pick, summed.reshape(rows_first, feature_count)).astype(
        jnp.bfloat16
    )
    token_grads = select_rows(back_pick, summed_grads.reshape(rows_first, feature_count)).astype(
        jnp.bfloat16
    )
    router_grads = jnp.dot(
        to_group.T.astype(jnp.float32),
        router_back.reshape(rows_first, 2).astype(jnp.float32),
        precision=lax.Precision.HIGHEST,
    )
    router_grads = router_grads.reshape(token_count, 2 * pair_count).astype(jnp.bfloat16)
    gate_sum, up_sum, down_sum = tuple(
        (
            part.astype(jnp.float32)
            for part in one_scatter(
                (
                    weight_terms[0].astype(jnp.bfloat16),
                    weight_terms[1].astype(jnp.bfloat16),
                    weight_terms[2].astype(jnp.bfloat16),
                ),
                "dp",
                (0, 0, 1),
            )
        )
    )
    return (
        layer_output,
        token_grads,
        router_grads,
        gate_sum.astype(jnp.bfloat16)[None],
        up_sum.astype(jnp.bfloat16)[None],
        down_sum.astype(jnp.bfloat16)[None],
    )


def solution(mesh):
    placed = (
        P(("dp", "group", "local"), None),
        P(("dp", "group", "local"), None),
        P(("dp", "group", "local"), None),
        P(("dp", "group", "local"), None),
        P(("group", "local"), "dp", None),
        P(("group", "local"), "dp", None),
        P(("group", "local"), None, "dp"),
    )
    return jax.shard_map(
        local,
        mesh=mesh,
        in_specs=placed,
        out_specs=(
            P(("dp", "group", "local"), None),
            P(("dp", "group", "local"), None),
            P(("dp", "group", "local"), None),
            P(("group", "local"), "dp", None),
            P(("group", "local"), "dp", None),
            P(("group", "local"), None, "dp"),
        ),
        check_vma=False,
    )
```

profile of v0, /device:TPU:1, one launch (start us, length us, event | category | flops | bytes accessed | tf_op | source)
XLA Modules:
  0.0 182.6 jit_solution(9759481322171231475)
XLA Ops:
  7.2 0.7 slice.84
  8.1 0.1 reduce_window_sum.22
  8.2 0.2 select_reduce_fusion.2
  8.5 0.7 slice.87
  9.2 0.7 slice.86
  9.9 0.7 slice.85
  11.5 0.1 convolution_convert_fusion.9
  11.6 0.1 copy.64
  11.8 0.2 fusion.3
  12.0 1.0 fusion.2
  13.0 0.7 pad_maximum_fusion.4
  13.7 8.1 %all-to-all-start = ((bf16[8,8,2052]{2,1,0:T(8,128)(2,1)}), bf16[8,8,2052]{2,1,0:T(8,128)(2,1)S(1)}, u32[]{:S(2)}, u32[]{:S(2)}) async-start(bf16[8,8,2052]{2,1,0:T(8,128)(2,1)} %pad_maximum_fusion.4), calls=%async_computation | async-start | bytes 557056 | tf_op jit(solution)/shard_map/all_to_all | solution.py:21
  21.9 1.0 copy.58
  22.9 1.0 copy.57
  23.9 1.6 pad_maximum_fusion.3
  25.5 5.8 %all-to-all-done = bf16[8,8,2052]{2,1,0:T(8,128)(2,1)S(1)} async-done(((bf16[8,8,2052]{2,1,0:T(8,128)(2,1)}), bf16[8,8,2052]{2,1,0:T(8,128)(2,1)S(1)}, u32[]{:S(2)}, u32[]{:S(2)}) %all-to-all-start) | async-done | bytes 262688 | tf_op jit(solution)/shard_map/all_to_all | solution.py:21
  31.4 0.1 eq.84
  31.6 0.2 reduce_window_sum.23
  31.8 0.2 select_reduce_fusion.1
  32.0 0.1 reduce_sum.52
  32.2 0.1 broadcast_in_dim.30
  32.3 0.1 select_reduce_fusion
  32.5 0.1 iota_compare_fusion.1
  32.6 0.4 convolution_convert_fusion
  33.1 0.4 multiply_convert_fusion
  33.5 0.2 pad_maximum_fusion.1
  33.7 59.8 %all_to_all.20 = bf16[16,48,1024]{2,1,0:T(8,128)(2,1)S(1)} all-to-all(bf16[16,48,1024]{2,1,0:T(8,128)(2,1)S(1)} %pad_maximum_fusion.1), channel_id=1, replica_groups=mesh['dp'=8,'group'=8,'local'=16] {'local'}, dimensions={0} | all-to-all | bytes 3145728 | tf_op jit(solution)/shard_map/all_to_all | solution.py:21
  93.5 0.1 fusion.42
  93.7 1.9 %fusion.13 = f32[384,384]{1,0:T(8,128)S(1)} fusion(bf16[384,1024]{1,0:T(8,128)(2,1)S(1)} %bitcast.99, bf16[1024,1152]{0,1:T(8,128)(2,1)} %all-gather.2.cloned.1.call-done), kind=kOutput, calls=%fused_computation.30 | convolution fusion | flops 301989888 | bytes 2162688 | tf_op jit(solution)/shard_map/dot_general | solution.py:64
  95.6 1.7 fusion.5
  97.3 0.7 multiply_convert_fusion.3
  98.0 0.6 fusion
  98.6 0.7 convolution_convert_fusion.2
  99.3 0.7 convolution_convert_fusion.3
  100.0 0.6 fusion.11
  100.6 0.6 convolution_convert_fusion.4
  101.2 0.6 add_convert_fusion
  101.8 1.3 pad_maximum_fusion.2
  103.1 6.3 %all-to-all-start.2 = ((bf16[16,48,1024]{2,1,0:T(8,128)(2,1)}), bf16[16,48,1024]{2,1,0:T(8,128)(2,1)}, u32[]{:S(2)}, u32[]{:S(2)}) async-start(bf16[16,48,1024]{2,1,0:T(8,128)(2,1)} %pad_maximum_fusion.2), calls=%async_computation.2 | async-start | bytes 3145728 | tf_op jit(solution)/shard_map/all_to_all | solution.py:21
  109.4 0.2 reduce-scatter.2.cloned.1.call-start
  109.6 0.2 copy.68
  109.8 1.2 reshape_reshape.7
  111.1 1.3 reshape_reshape.6
  112.3 6.7 %pad_maximum_fusion = bf16[8,147456]{1,0:T(8,128)(2,1)S(1)} fusion(bf16[8,49152]{1,0:T(8,128)(2,1)S(1)} %bitcast.93, bf16[8,49152]{1,0:T(8,128)(2,1)} %reshape_reshape.7, bf16[8,49152]{1,0:T(8,128)(2,1)} %reshape_reshape.6), kind=kLoop, calls=%fused_computation | loop fusion | flops 7077888 | bytes 4718592 | tf_op jit(solution)/shard_map/concatenate | solution.py:40
  119.0 2.5 %reshape.174 = bf16[9216,128]{1,0:T(8,128)(2,1)} reshape(bf16[8,147456]{1,0:T(8,128)(2,1)S(1)} %pad_maximum_fusion) | data formatting | bytes 4718592 | tf_op jit(solution)/shard_map/reshape | solution.py:42
  121.5 0.2 slice_reduce_fusion.1
  121.7 26.4 %all-to-all-done.2 = bf16[16,48,1024]{2,1,0:T(8,128)(2,1)} async-done(((bf16[16,48,1024]{2,1,0:T(8,128)(2,1)}), bf16[16,48,1024]{2,1,0:T(8,128)(2,1)}, u32[]{:S(2)}, u32[]{:S(2)}) %all-to-all-start.2) | async-done | bytes 1572896 | tf_op jit(solution)/shard_map/all_to_all | solution.py:21
  148.0 1.5 fusion.41
  149.6 0.3 fusion.19
  149.8 0.4 fusion.16
  150.2 0.2 stack.37
  150.4 0.2 stack.38
  150.5 0.3 fusion.18
  150.8 0.3 fusion.4
  151.1 0.1 concatenate.26
  151.2 19.0 %all_to_all.21 = bf16[8,8,2050]{2,1,0:T(8,128)(2,1)S(1)} all-to-all(bf16[8,8,2050]{2,1,0:T(8,128)(2,1)S(1)} %concatenate.26), channel_id=1, replica_groups=mesh['dp'=8,'group'=8,'local'=16] {'group'}, dimensions={0} | all-to-all | bytes 524800 | tf_op jit(solution)/shard_map/all_to_all | solution.py:21
  170.2 0.2 convolution_convert_fusion.10
  170.4 0.1 copy.62
  170.6 0.7 copy.63
  171.3 0.7 convolution_convert_fusion.8
  172.0 0.7 convolution_convert_fusion.7
  172.8 1.6 slice_bitcast_fusion.8
  174.4 0.7 broadcast_in_dim.33
  175.1 0.7 broadcast_in_dim.34
  (33 shorter events, 1.6 us)
Async XLA Ops:
  7.2 4.6 %copy-start = (bf16[16,1024]{1,0:T(8,128)(2,1)S(1)}, bf16[16,1024]{1,0:T(8,128)(2,1)}, u32[]{:S(2)}) copy-start(bf16[16,1024]{1,0:T(8,128)(2,1)} %param.8) | copy-start | bytes 98308
  13.7 17.6 %all-to-all-start = ((bf16[8,8,2052]{2,1,0:T(8,128)(2,1)}), bf16[8,8,2052]{2,1,0:T(8,128)(2,1)S(1)}, u32[]{:S(2)}, u32[]{:S(2)}) async-start(bf16[8,8,2052]{2,1,0:T(8,128)(2,1)} %pad_maximum_fusion.4), calls=%async_computation | async-start | bytes 557056 | tf_op jit(solution)/shard_map/all_to_all | solution.py:21
  21.8 71.9 %all-gather.2.cloned.1.call-start = ((), (), s32[]{:S(2)}) async-start(), calls=%async_computation.5 | async-start | bytes 2654208 | tf_op jit(solution)/shard_map/all_gather | solution.py:10
  93.7 3.6 %copy-start.1 = (bf16[1024,1152]{0,1:T(8,128)(2,1)S(1)}, bf16[1024,1152]{0,1:T(8,128)(2,1)}, u32[]{:S(2)}) copy-start(bf16[1024,1152]{0,1:T(8,128)(2,1)} %all-gather.2.cloned.1.call-done) | copy-start | bytes 7077892
  103.1 45.0 %all-to-all-start.2 = ((bf16[16,48,1024]{2,1,0:T(8,128)(2,1)}), bf16[16,48,1024]{2,1,0:T(8,128)(2,1)}, u32[]{:S(2)}, u32[]{:S(2)}) async-start(bf16[16,48,1024]{2,1,0:T(8,128)(2,1)} %pad_maximum_fusion.2), calls=%async_computation.2 | async-start | bytes 3145728 | tf_op jit(solution)/shard_map/all_to_all | solution.py:21
  109.4 63.4 %reduce-scatter.2.cloned.1.call-start = ((), (), s32[]{:S(2)}) async-start(), calls=%async_computation.6 | async-start | bytes 2654208 | tf_op jit(solution)/shard_map/reduce_scatter | solution.py:43
Sparse Core Ops, SparseCore 0:
  25.7 61.4 all-gather.1
  121.6 43.0 reduce-scatter.1
where the time goes:
time: 183 us
  blocking collectives  78.9 us (43%)
  waiting for transfers between devices  32.2 us (18%)
  local copies, waits for them, and re-layouts  17.7 us (10%)
  starting transfers between devices  14.7 us (8%)
  between operations  14.4 us (8%)
  matrix products  13 us (7%)
  other arithmetic  11.8 us (6%)
    all_to_all x2, blocking collectives, side_by_side(): lax.all_to_all(both, axis, split_axis=split_dim, concat_axis=concat_dim,...  78.9 us
    all_to_all x2, waiting for transfers between devices, side_by_side(): lax.all_to_all(both, axis, split_axis=split_dim, concat_axis=concat_dim,...  32.1 us
    all_to_all x2, starting transfers between devices, side_by_side(): lax.all_to_all(both, axis, split_axis=split_dim, concat_axis=concat_dim,...  14.4 us
    concatenate x1, other arithmetic, one_scatter(): lines = jnp.concatenate([b.reshape(peers, -1) for b in blocks], axis=1)  6.67 us
    dot_general x10, matrix products, select_rows(): jnp.dot(chooser.astype(jnp.bfloat16), row_block, preferred_element_type=j...  4.72 us
  transfers between devices with their start and end apart: 4, of which 2 were waited for; matrix products, arithmetic and copies ran while one was open for 13% of the time, Pallas kernels for 0%

commit v1 on v0

v1 whole, which is shorter than its diff:
```python
import jax
import jax.numpy as jnp
from jax import lax
from jax.experimental import pallas as pl
from jax.experimental.pallas import tpu as pltpu
from jax.sharding import PartitionSpec as P

INTERPRET = False
BF16 = jnp.bfloat16
F32 = jnp.float32
LANES = 128
CAP = 3


def vmem():
    return pl.BlockSpec(memory_space=pltpu.VMEM)


def dot(a, b, dims=((1,), (0,))):
    return lax.dot_general(a, b, (dims, ((), ())), preferred_element_type=F32)


def spread_rows(wide, rows, first, blocks):
    n, features = wide.shape
    per = features // LANES
    for c in range(per):
        rows[pl.ds(first + c, n, stride=blocks), :] = wide[:, c * LANES : (c + 1) * LANES]


def gather_rows(rows, n, first, blocks, per):
    return jnp.concatenate(
        [rows[pl.ds(first + c, n, stride=blocks), :] for c in range(per)], axis=1
    )


def token_ranks(ids, experts):
    tokens, columns = ids.shape
    lane = lax.broadcasted_iota(jnp.int32, (tokens, experts), 1)
    matches = [ids[:, k : k + 1] == lane for k in range(columns)]
    named = jnp.zeros((tokens, experts), F32)
    for match in matches:
        named = named + match.astype(F32)
    row = lax.broadcasted_iota(jnp.int32, (tokens, tokens), 0)
    column = lax.broadcasted_iota(jnp.int32, (tokens, tokens), 1)
    earlier = (column < row).astype(F32).astype(BF16)
    return matches, named, dot(earlier, named.astype(BF16))


def pack_kernel(gate, up, down, out):
    features, hidden = gate.shape
    for i, weight in enumerate((gate, up)):
        for c in range(hidden // LANES):
            at = i * hidden + c * LANES
            out[at : at + features, :] = weight[:, c * LANES : (c + 1) * LANES]
    out[2 * hidden :, :] = down[...]


def send_kernel(tokens, cotangent, ids, weights, out, rows):
    experts = out.shape[0] // (2 * CAP * tokens.shape[1] // LANES)
    per = tokens.shape[1] // LANES
    blocks = 2 * CAP * per
    matches, named, rank = token_ranks(ids[...], experts)
    scale = jnp.zeros(named.shape, F32)
    values = weights[...].astype(F32)
    for k, match in enumerate(matches):
        scale = scale + jnp.where(match, values[:, k : k + 1], 0.0)
    for r in range(CAP):
        here = (named > 0.0) & (rank == float(r))
        pick = jnp.where(here, 1.0, 0.0).astype(BF16)
        scaled = jnp.where(here, scale, 0.0).astype(BF16)
        spread_rows(dot(pick, tokens[...], ((0,), (0,))), rows, r * per, blocks)
        spread_rows(dot(scaled, cotangent[...], ((0,), (0,))), rows, (CAP + r) * per, blocks)
    out[...] = rows[...].astype(BF16)


def expert_kernel(recv, gathered, back, terms, rows, gate_up, down, sems):
    peers = gathered.shape[0]
    features = gate_up.shape[0] // peers
    hidden = down.shape[0]
    width = gate_up.shape[0]
    per = width // LANES
    blocks = 2 * CAP * per
    sources = recv.shape[0] // blocks
    copies = []
    for d in range(peers):
        for i in range(2 * hidden // LANES):
            copies.append(
                pltpu.make_async_copy(
                    gathered.at[d, pl.ds(i * LANES, LANES), :],
                    gate_up.at[pl.ds(d * features, features), pl.ds(i * LANES, LANES)],
                    sems.at[0, d * (2 * hidden // LANES) + i],
                )
            )
    late = [
        pltpu.make_async_copy(
            gathered.at[d, pl.ds(2 * hidden, hidden), :],
            down.at[:, pl.ds(d * features, features)],
            sems.at[1, d],
        )
        for d in range(peers)
    ]
    for copy in copies + late:
        copy.start()
    rows[...] = recv[...].astype(F32)
    x = jnp.concatenate(
        [gather_rows(rows, sources, r * per, blocks, per).astype(BF16) for r in range(CAP)], axis=0
    )
    g = jnp.concatenate(
        [gather_rows(rows, sources, (CAP + r) * per, blocks, per).astype(BF16) for r in range(CAP)],
        axis=0,
    )
    for copy in copies:
        copy.wait()
    pre = dot(x, gate_up[...])
    gate_pre, up_pre = pre[:, :hidden], pre[:, hidden:]
    sigmoid = 1.0 / (1.0 + jnp.exp(-gate_pre))
    inner = (gate_pre * sigmoid * up_pre).astype(BF16)
    for copy in late:
        copy.wait()
    hidden_grad = dot(g, down[...], ((1,), (1,)))
    out = dot(inner, down[...])
    for r in range(CAP):
        spread_rows(out[r * sources : (r + 1) * sources], rows, r * per, blocks)
    gate_grad = (hidden_grad * up_pre * sigmoid * (1.0 + gate_pre * (1.0 - sigmoid))).astype(BF16)
    up_grad = (hidden_grad * gate_pre * sigmoid).astype(BF16)
    both = jnp.concatenate([gate_grad, up_grad], axis=1)
    back_grad = dot(both, gate_up[...], ((1,), (1,)))
    for r in range(CAP):
        spread_rows(back_grad[r * sources : (r + 1) * sources], rows, (CAP + r) * per, blocks)
    back[...] = rows[...].astype(BF16)
    down_term = dot(inner, g, ((0,), (0,))).astype(BF16)
    for d in range(peers):
        terms[d, 2 * hidden :, :] = down_term[:, d * features : (d + 1) * features]
    term = dot(x, both, ((0,), (0,))).astype(BF16)
    for d in range(peers):
        for i in range(2 * hidden // LANES):
            terms[d, i * LANES : (i + 1) * LANES, :] = term[
                d * features : (d + 1) * features, i * LANES : (i + 1) * LANES
            ]


def combine_kernel(back, cotangent, ids, weights, layer, token_grads, router_grads, rows):
    tokens, width = cotangent.shape
    columns = ids.shape[1]
    per = width // LANES
    blocks = 2 * CAP * per
    experts = back.shape[0] // blocks
    rows[...] = back[...].astype(F32)
    matches, named, rank = token_ranks(ids[...], experts)
    ranks = [rank == float(r) for r in range(CAP)]
    pick = jnp.concatenate(
        [
            jnp.concatenate(
                [jnp.where(match & at, 1.0, 0.0) for at in ranks],
                axis=1,
            )
            for match in matches
        ],
        axis=0,
    ).astype(BF16)
    outs = jnp.concatenate(
        [gather_rows(rows, experts, r * per, blocks, per).astype(BF16) for r in range(CAP)], axis=0
    )
    grads = jnp.concatenate(
        [
            gather_rows(rows, experts, (CAP + r) * per, blocks, per).astype(BF16)
            for r in range(CAP)
        ],
        axis=0,
    )
    out = dot(pick, outs)
    grad = dot(pick, grads)
    values = weights[...].astype(F32)
    cot = cotangent[...].astype(F32)
    lane = lax.broadcasted_iota(jnp.int32, (tokens, columns), 1)
    total = jnp.zeros((tokens, width), F32)
    total_grad = jnp.zeros((tokens, width), F32)
    routed = jnp.zeros((tokens, columns), F32)
    for j in range(columns // 2):
        a, b = 2 * j, 2 * j + 1
        first, second = out[a * tokens : (a + 1) * tokens], out[b * tokens : (b + 1) * tokens]
        pair = values[:, a : a + 1] * first + values[:, b : b + 1] * second
        total = total + pair.astype(BF16).astype(F32)
        pair = grad[a * tokens : (a + 1) * tokens] + grad[b * tokens : (b + 1) * tokens]
        total_grad = total_grad + pair.astype(BF16).astype(F32)
        routed = jnp.where(lane == a, jnp.sum(cot * first, axis=1, keepdims=True), routed)
        routed = jnp.where(lane == b, jnp.sum(cot * second, axis=1, keepdims=True), routed)
    layer[...] = total.astype(BF16)
    token_grads[...] = total_grad.astype(BF16)
    router_grads[...] = routed.astype(BF16)


def unpack_kernel(lines, gate, up, down):
    features, hidden = gate.shape
    for i, weight in enumerate((gate, up)):
        for c in range(hidden // LANES):
            at = i * hidden + c * LANES
            weight[:, c * LANES : (c + 1) * LANES] = lines[at : at + features, :]
    down[...] = lines[2 * hidden :, :]


def call(kernel, outs, scratch=(), in_specs=None, name=None):
    shapes = [jax.ShapeDtypeStruct(shape, BF16) for shape in outs]
    single = len(shapes) == 1
    return pl.pallas_call(
        kernel,
        out_shape=shapes[0] if single else shapes,
        in_specs=in_specs,
        out_specs=vmem() if single else [vmem() for _ in shapes],
        scratch_shapes=list(scratch),
        interpret=INTERPRET,
        name=name,
    )


def pack_weights(gate, up, down):
    hidden = gate.shape[1]
    return call(pack_kernel, [(3 * hidden, LANES)], in_specs=[vmem()] * 3, name="pack_weights")(
        gate, up, down
    )


def send_rows(tokens, cotangent, ids, weights, experts):
    lines = experts * 2 * CAP * tokens.shape[1] // LANES
    return call(
        send_kernel,
        [(lines, LANES)],
        scratch=[pltpu.VMEM((lines, LANES), F32)],
        in_specs=[vmem()] * 4,
        name="send_rows",
    )(tokens, cotangent, ids, weights)


def expert(recv, gathered, hidden, width):
    peers = gathered.shape[0]
    return call(
        expert_kernel,
        [recv.shape, gathered.shape],
        scratch=[
            pltpu.VMEM(recv.shape, F32),
            pltpu.VMEM((width, 2 * hidden), BF16),
            pltpu.VMEM((hidden, width), BF16),
            pltpu.SemaphoreType.DMA((2, peers * 2 * hidden // LANES)),
        ],
        in_specs=[vmem(), pl.BlockSpec(memory_space=pl.ANY)],
        name="expert",
    )(recv, gathered)


def combine(back, cotangent, ids, weights):
    return call(
        combine_kernel,
        [cotangent.shape, cotangent.shape, ids.shape],
        scratch=[pltpu.VMEM(back.shape, F32)],
        in_specs=[vmem()] * 4,
        name="combine",
    )(back, cotangent, ids, weights)


def unpack_grads(lines, features, hidden):
    return call(
        unpack_kernel,
        [(features, hidden), (features, hidden), (hidden, LANES)],
        in_specs=[vmem()],
        name="unpack_grads",
    )(lines)


def exchange(lines, peers):
    out = lax.all_to_all(
        lines.reshape(peers, -1, LANES), ("group", "local"), split_axis=0, concat_axis=0, tiled=True
    )
    return out.reshape(lines.shape)


def local(tokens, cotangent, expert_ids, router_weights, gate_weight, up_weight, down_weight):
    experts = lax.axis_size("group") * lax.axis_size("local")
    peers = lax.axis_size("dp")
    features, hidden = gate_weight.shape[1:]
    width = tokens.shape[1]
    packed = pack_weights(gate_weight[0], up_weight[0], down_weight[0])
    gathered = lax.all_gather(packed, "dp", axis=0, tiled=True).reshape(peers, -1, LANES)
    sent = send_rows(tokens, cotangent, expert_ids, router_weights, experts)
    recv = exchange(sent, experts)
    back, terms = expert(recv, gathered, hidden, width)
    scattered = lax.psum_scatter(terms.reshape(-1, LANES), "dp", tiled=True)
    returned = exchange(back, experts)
    layer, token_grads, router_grads = combine(returned, cotangent, expert_ids, router_weights)
    gate, up, down = unpack_grads(scattered, features, hidden)
    return layer, token_grads, router_grads, gate[None], up[None], down[None]


def solution(mesh):
    tokens = P(("dp", "group", "local"), None)
    rows = P(("group", "local"), "dp", None)
    columns = P(("group", "local"), None, "dp")
    return jax.shard_map(
        local,
        mesh=mesh,
        in_specs=(tokens, tokens, tokens, tokens, rows, rows, columns),
        out_specs=(tokens, tokens, tokens, rows, rows, columns),
        check_vma=False,
    )
```

time: 183 us -> 155 us (0.85)
  blocking collectives: 78.9 us -> 115 us
  waiting for transfers between devices: 32.2 us -> 0.04 us
  Pallas kernels: 0 us -> 20.1 us
  starting transfers between devices: 14.7 us -> 0.08 us
  matrix products: 13 us -> 0 us
  local copies, waits for them, and re-layouts: 17.7 us -> 5.41 us
  other arithmetic: 11.8 us -> 0 us
    all_to_all x2, blocking collectives: 78.9 us -> 115 us  [exchange(): lax.all_to_all(lines.reshape(peers, -1, LANES), ('group', 'local'), split...]
    all_to_all x2 -> x0, waiting for transfers between devices: 32.1 us -> none  [side_by_side(): lax.all_to_all(both, axis, split_axis=split_dim, concat_axis=concat_dim,...]
    pallas_call x0 -> x5, Pallas kernels: none -> 20.1 us  [the longest x1 9.75 us: expert(): call(expert_kernel, [recv.shape, gathered.shape], scratch=[pltpu.VMEM(rec...]
    all_to_all x2 -> x0, starting transfers between devices: 14.4 us -> none  [side_by_side(): lax.all_to_all(both, axis, split_axis=split_dim, concat_axis=concat_dim,...]
    dot_general x21 -> x0, matrix products: 13 us -> none  [the longest x10 4.72 us: select_rows(): jnp.dot(chooser.astype(jnp.bfloat16), row_block, preferred_element_type=j...]
    concatenate x5 -> x0, other arithmetic: 10.5 us -> none  [the longest x1 6.67 us: one_scatter(): lines = jnp.concatenate([b.reshape(peers, -1) for b in blocks], axis=1)]
    slice x7 -> x0, local copies, waits for them, and re-layouts: 4.64 us -> none  [the longest x2 1.65 us: side_by_side(): gathered.append(lax.slice_in_dim(out, at, at + a.shape[along], axis=along))]
    another operation x10 -> x0, local copies, waits for them, and re-layouts: 3.35 us -> none  [the longest x2 2.51 us: one_scatter(): lines = jnp.concatenate([b.reshape(peers, -1) for b in blocks], axis=1)]
  transfers between devices with their start and end apart: 4 -> 2, of which waited for: 2 -> 0; matrix products, arithmetic and copies ran while one was open for 13% -> 3% of each run, Pallas kernels for 0% -> 4%
where the time goes in v1:
time: 155 us
  blocking collectives  115 us (74%)
  Pallas kernels  20.1 us (13%)
  between operations  14.1 us (9%)
  local copies, waits for them, and re-layouts  5.41 us (3%)
    all_to_all x2, blocking collectives, exchange(): lax.all_to_all(lines.reshape(peers, -1, LANES), ('group', 'local'), split...  115 us
    pallas_call x1, Pallas kernels, expert(): call(expert_kernel, [recv.shape, gathered.shape], scratch=[pltpu.VMEM(rec...  9.75 us
    unnamed x5, local copies, waits for them, and re-layouts  5.41 us
    pallas_call x1, Pallas kernels, send_rows(): call(send_kernel, [(lines, LANES)], scratch=[pltpu.VMEM((lines, LANES), F...  3.48 us
    pallas_call x1, Pallas kernels, combine(): call(combine_kernel, [cotangent.shape, cotangent.shape, ids.shape], scrat...  3.42 us
  transfers between devices with their start and end apart: 2, of which 0 were waited for; matrix products, arithmetic and copies ran while one was open for 3% of the time, Pallas kernels for 4%

profile of v1, /device:TPU:1, one launch (start us, length us, event | category | flops | bytes accessed | tf_op | source)
XLA Modules:
  0.0 154.7 jit_solution(298331946377684514)
XLA Ops:
  7.2 0.0 all-gather.2.cloned.1.call-start
  7.2 1.7 %pack_weights.1 = bf16[1152,128]{1,0:T(8,128)(2,1)} custom-call(bf16[128,384]{1,0:T(8,128)(2,1)} %bitcast.18, bf16[128,384]{1,0:T(8,128)(2,1)} %bitcast.19, bf16[384,128]{1,0:T(8,128)(2,1)} %bitcast.20), custom_call_target="tpu_custom_call" | custom-call | tf_op jit(solution)/shard_map/pack_weights/pallas_call | solution.py:218
  8.9 0.0 all-gather.2.cloned.1.call-update
  9.0 0.0 reduce-scatter.2.cloned.1.call-start
  9.0 1.3 copy.14.weights
  10.4 1.4 copy.13.ids
  11.7 3.5 %send_rows.1 = bf16[6144,128]{1,0:T(8,128)(2,1)} custom-call(bf16[16,1024]{1,0:T(8,128)(2,1)} %tokens.1, bf16[16,1024]{1,0:T(8,128)(2,1)} %cotangent.3, s32[16,8]{1,0:T(8,128)} %copy.13.ids, bf16[16,8]{1,0:T(8,128)(2,1)} %copy.14.weights), custom_call_target="tpu_custom_call" | custom-call | tf_op jit(solution)/shard_map/send_rows/pallas_call | solution.py:225
  15.2 66.5 %all_to_all.10 = bf16[128,48,128]{2,1,0:T(8,128)(2,1)} all-to-all(bf16[128,48,128]{2,1,0:T(8,128)(2,1)} %bitcast.13), channel_id=1, replica_groups=mesh['dp'=8,'group'=8,'local'=16] {'group','local'}, dimensions={0} | all-to-all | bytes 3145728 | tf_op jit(solution)/shard_map/all_to_all | solution.py:270
  81.7 0.0 all-gather.2.cloned.1.call-done
  81.7 9.8 %expert.1 = (bf16[6144,128]{1,0:T(8,128)(2,1)}, bf16[8,1152,128]{2,1,0:T(8,128)(2,1)}) custom-call(bf16[6144,128]{1,0:T(8,128)(2,1)} %bitcast.14, bf16[8,1152,128]{2,1,0:T(8,128)(2,1)} %bitcast.16), custom_call_target="tpu_custom_call" | custom-call | tf_op jit(solution)/shard_map/expert/pallas_call | solution.py:236
  91.4 0.0 copy-start
  91.4 0.0 reduce-scatter.2.cloned.1.call-update
  91.5 1.4 copy-done
  92.8 48.6 %all_to_all.11 = bf16[128,48,128]{2,1,0:T(8,128)(2,1)} all-to-all(bf16[128,48,128]{2,1,0:T(8,128)(2,1)S(1)} %bitcast.17), channel_id=1, replica_groups=mesh['dp'=8,'group'=8,'local'=16] {'group','local'}, dimensions={0} | all-to-all | bytes 3145728 | tf_op jit(solution)/shard_map/all_to_all | solution.py:270
  141.4 3.4 %combine.1 = (bf16[16,1024]{1,0:T(8,128)(2,1)}, bf16[16,1024]{1,0:T(8,128)(2,1)}, bf16[16,8]{1,0:T(8,128)(2,1)}) custom-call(bf16[6144,128]{1,0:T(8,128)(2,1)} %bitcast.12, bf16[16,1024]{1,0:T(8,128)(2,1)} %cotangent.3, s32[16,8]{1,0:T(8,128)} %copy.13.ids, bf16[16,8]{1,0:T(8,128)(2,1)} %copy.14.weights), custom_call_target="tpu_custom_call" | custom-call | tf_op jit(solution)/shard_map/combine/pallas_call | solution.py:251
  144.8 1.3 copy.17
  146.2 0.0 reduce-scatter.2.cloned.1.call-done.lines
  146.2 1.7 %unpack_grads.1 = (bf16[128,384]{1,0:T(8,128)(2,1)}, bf16[128,384]{1,0:T(8,128)(2,1)}, bf16[384,128]{1,0:T(8,128)(2,1)}) custom-call(bf16[1152,128]{1,0:T(8,128)(2,1)} %reduce-scatter.2.cloned.1.call-done.lines), custom_call_target="tpu_custom_call" | custom-call | tf_op jit(solution)/shard_map/unpack_grads/pallas_call | solution.py:261
Async XLA Ops:
  7.2 74.5 %all-gather.2.cloned.1.call-start = ((), (), s32[]{:S(2)}) async-start(), calls=%async_computation.3 | async-start | bytes 2654208 | tf_op jit(solution)/shard_map/all_gather | solution.py:282
  9.0 137.2 %reduce-scatter.2.cloned.1.call-start = ((), (), s32[]{:S(2)}) async-start(), calls=%async_computation.4 | async-start | bytes 2654208 | tf_op jit(solution)/shard_map/reduce_scatter | solution.py:286
  91.4 1.4 copy-start
Sparse Core Ops, SparseCore 0:
  10.6 54.5 all-gather.1
  91.6 38.9 reduce-scatter.1

commit v2 on v1

v2 whole, which is shorter than its diff:
```python
import jax
import jax.numpy as jnp
from jax import lax
from jax.experimental import pallas as pl
from jax.experimental.pallas import tpu as pltpu
from jax.sharding import PartitionSpec as P

INTERPRET = False
BF16 = jnp.bfloat16
F32 = jnp.float32
LANES = 128
CAP = 3


def vmem():
    return pl.BlockSpec(memory_space=pltpu.VMEM)


def dot(a, b, dims=((1,), (0,))):
    return lax.dot_general(a, b, (dims, ((), ())), preferred_element_type=F32)


def spread_rows(wide, rows, first, blocks):
    n, features = wide.shape
    per = features // LANES
    for c in range(per):
        rows[pl.ds(first + c, n, stride=blocks), :] = wide[:, c * LANES : (c + 1) * LANES]


def gather_rows(rows, n, first, blocks, per):
    return jnp.concatenate(
        [rows[pl.ds(first + c, n, stride=blocks), :] for c in range(per)], axis=1
    )


def token_ranks(ids, experts):
    columns, tokens = ids.shape
    expert_at = lax.broadcasted_iota(jnp.int32, (experts, tokens), 0)
    matches = [ids[k : k + 1, :] == expert_at for k in range(columns)]
    named = jnp.zeros((experts, tokens), F32)
    for match in matches:
        named = named + match.astype(F32)
    row = lax.broadcasted_iota(jnp.int32, (tokens, tokens), 0)
    column = lax.broadcasted_iota(jnp.int32, (tokens, tokens), 1)
    earlier = (row < column).astype(F32).astype(BF16)
    return matches, named, dot(named.astype(BF16), earlier)


def identity(size):
    row = lax.broadcasted_iota(jnp.int32, (size, size), 0)
    column = lax.broadcasted_iota(jnp.int32, (size, size), 1)
    return (row == column).astype(F32).astype(BF16)


def prepare_kernel(tokens, cotangent, ids, weights, gate, up, down, out, packed, rows):
    features, hidden = gate.shape
    for i, weight in enumerate((gate, up)):
        for c in range(hidden // LANES):
            at = i * hidden + c * LANES
            packed[at : at + features, :] = weight[:, c * LANES : (c + 1) * LANES]
    packed[2 * hidden :, :] = down[...]
    per = tokens.shape[1] // LANES
    blocks = 2 * CAP * per
    experts = out.shape[0] // blocks
    matches, named, rank = token_ranks(ids[...], experts)
    scale = jnp.zeros(named.shape, F32)
    values = weights[...].astype(F32)
    for k, match in enumerate(matches):
        scale = scale + jnp.where(match, values[k : k + 1, :], 0.0)
    for r in range(CAP):
        here = (named > 0.0) & (rank == float(r))
        pick = jnp.where(here, 1.0, 0.0).astype(BF16)
        scaled = jnp.where(here, scale, 0.0).astype(BF16)
        spread_rows(dot(pick, tokens[...]), rows, r * per, blocks)
        spread_rows(dot(scaled, cotangent[...]), rows, (CAP + r) * per, blocks)
    out[...] = rows[...].astype(BF16)


def expert_kernel(place, recv, *refs):
    pieces, outs, scratch = refs[:9], refs[9:19], refs[19:]
    back, terms = outs[0], outs[1:]
    rows, gate_up, down, term, down_term, sems = scratch
    peers, features, _ = gate_up.shape
    hidden = down.shape[1]
    width = peers * features
    per = width // LANES
    blocks = 2 * CAP * per
    sources = recv.shape[0] // blocks
    me = place[0]
    tiles = 2 * hidden // LANES
    early, late = [], []
    starts = [0, -1, -2, -3, 1, 2, 3, 4, 4]
    for n, (piece, offset) in enumerate(zip(pieces, starts)):
        d = lax.rem(me + offset + peers, peers)
        first = pieces[7].shape[0] if n == 8 else 0
        for i in range(piece.shape[0] // LANES):
            at = first // LANES + i
            if at < tiles:
                target = gate_up.at[d, :, pl.ds(at * LANES, LANES)]
            else:
                target = down.at[d, pl.ds((at - tiles) * LANES, LANES), :]
            copy = pltpu.make_async_copy(
                piece.at[pl.ds(i * LANES, LANES), :], target, sems.at[n, i]
            )
            (early if at < tiles else late).append(copy)
    for copy in early + late:
        copy.start()
    rows[...] = recv[...].astype(F32)
    x = jnp.concatenate(
        [gather_rows(rows, sources, r * per, blocks, per).astype(BF16) for r in range(CAP)], axis=0
    )
    g = jnp.concatenate(
        [gather_rows(rows, sources, (CAP + r) * per, blocks, per).astype(BF16) for r in range(CAP)],
        axis=0,
    )
    for copy in early:
        copy.wait()
    wide = gate_up[...].reshape(width, 2 * hidden)
    pre = dot(x, wide)
    gate_pre, up_pre = pre[:, :hidden], pre[:, hidden:]
    sigmoid = 1.0 / (1.0 + jnp.exp(-gate_pre))
    inner = (gate_pre * sigmoid * up_pre).astype(BF16)
    for copy in late:
        copy.wait()
    narrow = jnp.concatenate([down[d] for d in range(peers)], axis=1)
    hidden_grad = dot(g, narrow, ((1,), (1,)))
    out = dot(inner, narrow)
    for r in range(CAP):
        spread_rows(out[r * sources : (r + 1) * sources], rows, r * per, blocks)
    gate_grad = (hidden_grad * up_pre * sigmoid * (1.0 + gate_pre * (1.0 - sigmoid))).astype(BF16)
    up_grad = (hidden_grad * gate_pre * sigmoid).astype(BF16)
    both = jnp.concatenate([gate_grad, up_grad], axis=1)
    back_grad = dot(both, wide, ((1,), (1,)))
    for r in range(CAP):
        spread_rows(back_grad[r * sources : (r + 1) * sources], rows, (CAP + r) * per, blocks)
    back[...] = rows[...].astype(BF16)
    term[...] = dot(x, both, ((0,), (0,))).astype(BF16).reshape(term.shape)
    down_full = dot(inner, g, ((0,), (0,))).astype(BF16)
    for d in range(peers):
        down_term[d] = down_full[:, d * features : (d + 1) * features]
    for n, (ref, offset) in enumerate(zip(terms, [0, 1, 2, 3, 5, 6, 7, 4, 4])):
        d = lax.rem(me + offset, peers)
        first = terms[7].shape[0] if n == 8 else 0
        for i in range(ref.shape[0] // LANES):
            at = first // LANES + i
            if at < tiles:
                ref[i * LANES : (i + 1) * LANES, :] = term[d, :, at * LANES : (at + 1) * LANES]
            else:
                ref[i * LANES : (i + 1) * LANES, :] = down_term[
                    d, (at - tiles) * LANES : (at - tiles + 1) * LANES, :
                ]


def combine_kernel(back, cotangent, ids, weights, layer, token_grads, router_grads, rows):
    tokens, width = cotangent.shape
    columns = ids.shape[0]
    per = width // LANES
    blocks = 2 * CAP * per
    experts = back.shape[0] // blocks
    rows[...] = back[...].astype(F32)
    matches, named, rank = token_ranks(ids[...], experts)
    ranks = [rank == float(r) for r in range(CAP)]
    pick = jnp.concatenate(
        [
            jnp.concatenate([jnp.where(match & at, 1.0, 0.0) for match in matches], axis=1)
            for at in ranks
        ],
        axis=0,
    ).astype(BF16)
    outs = jnp.concatenate(
        [gather_rows(rows, experts, r * per, blocks, per).astype(BF16) for r in range(CAP)], axis=0
    )
    grads = jnp.concatenate(
        [
            gather_rows(rows, experts, (CAP + r) * per, blocks, per).astype(BF16)
            for r in range(CAP)
        ],
        axis=0,
    )
    out = dot(pick, outs, ((0,), (0,)))
    grad = dot(pick, grads, ((0,), (0,)))
    eye = identity(tokens)
    values = dot(eye, weights[...], ((1,), (1,)))
    cot = cotangent[...].astype(F32)
    lane = lax.broadcasted_iota(jnp.int32, (tokens, columns), 1)
    total = jnp.zeros((tokens, width), F32)
    total_grad = jnp.zeros((tokens, width), F32)
    routed = jnp.zeros((tokens, columns), F32)
    for j in range(columns // 2):
        a, b = 2 * j, 2 * j + 1
        first, second = out[a * tokens : (a + 1) * tokens], out[b * tokens : (b + 1) * tokens]
        pair = values[:, a : a + 1] * first + values[:, b : b + 1] * second
        total = total + pair.astype(BF16).astype(F32)
        pair = grad[a * tokens : (a + 1) * tokens] + grad[b * tokens : (b + 1) * tokens]
        total_grad = total_grad + pair.astype(BF16).astype(F32)
        routed = jnp.where(lane == a, jnp.sum(cot * first, axis=1, keepdims=True), routed)
        routed = jnp.where(lane == b, jnp.sum(cot * second, axis=1, keepdims=True), routed)
    layer[...] = total.astype(BF16)
    token_grads[...] = total_grad.astype(BF16)
    router_grads[...] = dot(routed.astype(BF16), eye, ((0,), (0,))).astype(BF16)


def unpack_kernel(own, right, left, gate, up, down):
    features, hidden = gate.shape
    total = (own[...].astype(F32) + right[...].astype(F32) + left[...].astype(F32)).astype(BF16)
    for i, weight in enumerate((gate, up)):
        for c in range(hidden // LANES):
            at = i * hidden + c * LANES
            weight[:, c * LANES : (c + 1) * LANES] = total[at : at + features, :]
    down[...] = total[2 * hidden :, :]


def call(kernel, outs, scratch=(), in_specs=None, name=None):
    shapes = [jax.ShapeDtypeStruct(shape, BF16) for shape in outs]
    single = len(shapes) == 1
    return pl.pallas_call(
        kernel,
        out_shape=shapes[0] if single else shapes,
        in_specs=in_specs,
        out_specs=vmem() if single else [vmem() for _ in shapes],
        scratch_shapes=list(scratch),
        interpret=INTERPRET,
        name=name,
    )


def prepare(tokens, cotangent, ids, weights, gate, up, down, experts):
    lines = experts * 2 * CAP * tokens.shape[1] // LANES
    return call(
        prepare_kernel,
        [(lines, LANES), (3 * gate.shape[1], LANES)],
        scratch=[pltpu.VMEM((lines, LANES), F32)],
        in_specs=[vmem()] * 7,
        name="prepare",
    )(tokens, cotangent, ids, weights, gate, up, down)


def expert(place, recv, pieces, hidden, width):
    peers = width // LANES
    lines, half = pieces[0].shape[0], pieces[7].shape[0]
    first, second = half, lines - half
    shapes = [(lines, LANES)] * 7 + [(first, LANES), (second, LANES)]
    return call(
        expert_kernel,
        [recv.shape] + shapes,
        scratch=[
            pltpu.VMEM(recv.shape, F32),
            pltpu.VMEM((peers, LANES, 2 * hidden), BF16),
            pltpu.VMEM((peers, hidden, LANES), BF16),
            pltpu.VMEM((peers, LANES, 2 * hidden), BF16),
            pltpu.VMEM((peers, hidden, LANES), BF16),
            pltpu.SemaphoreType.DMA((9, lines // LANES)),
        ],
        in_specs=[pl.BlockSpec(memory_space=pltpu.SMEM), vmem()]
        + [pl.BlockSpec(memory_space=pl.ANY)] * 9,
        name="expert",
    )(place, recv, *pieces)


def shifted(value, by):
    peers = lax.axis_size("dp")
    return lax.ppermute(value, "dp", [(i, (i + by) % peers) for i in range(peers)])


def gather_ring(chunk):
    half = far_half(chunk.shape[0])
    right, left = [chunk], [chunk]
    for _ in range(3):
        right.append(shifted(right[-1], 1))
        left.append(shifted(left[-1], -1))
    far = [shifted(right[-1][:half], 1), shifted(left[-1][half:], -1)]
    return right + left[1:] + far


def far_half(lines):
    return lines // LANES // 2 * LANES + lines // LANES % 2 * LANES


def scatter_ring(terms):
    own, near, two, three, far3, far2, far1, first, second = terms
    half = first.shape[0]
    right, left = shifted(first, 1), shifted(second, -1)
    right = jnp.concatenate([three[:half] + right, three[half:]], axis=0)
    left = jnp.concatenate([far3[:half], far3[half:] + left], axis=0)
    right, left = shifted(right, 1), shifted(left, -1)
    right, left = shifted(two + right, 1), shifted(far2 + left, -1)
    right, left = shifted(near + right, 1), shifted(far1 + left, -1)
    return own, right, left


def combine(back, cotangent, ids, weights):
    return call(
        combine_kernel,
        [cotangent.shape, cotangent.shape, ids.shape],
        scratch=[pltpu.VMEM(back.shape, F32)],
        in_specs=[vmem()] * 4,
        name="combine",
    )(back, cotangent, ids, weights)


def unpack_grads(parts, features, hidden):
    return call(
        unpack_kernel,
        [(features, hidden), (features, hidden), (hidden, LANES)],
        in_specs=[vmem()] * 3,
        name="unpack_grads",
    )(*parts)


def exchange(lines, peers):
    out = lax.all_to_all(
        lines.reshape(peers, -1, LANES), ("group", "local"), split_axis=0, concat_axis=0, tiled=True
    )
    return out.reshape(lines.shape)


def local(tokens, cotangent, expert_ids, router_weights, gate_weight, up_weight, down_weight):
    experts = lax.axis_size("group") * lax.axis_size("local")
    features, hidden = gate_weight.shape[1:]
    width = tokens.shape[1]
    ids, weights = expert_ids.T, router_weights.T
    sent, packed = prepare(
        tokens, cotangent, ids, weights, gate_weight[0], up_weight[0], down_weight[0], experts
    )
    recv = exchange(sent, experts)
    pieces = gather_ring(packed)
    place = lax.axis_index("dp").astype(jnp.int32).reshape(1)
    back, *terms = expert(place, recv, pieces, hidden, width)
    returned = exchange(back, experts)
    parts = scatter_ring(terms)
    layer, token_grads, router_grads = combine(returned, cotangent, ids, weights)
    gate, up, down = unpack_grads(parts, features, hidden)
    return layer, token_grads, router_grads.T, gate[None], up[None], down[None]


def solution(mesh):
    tokens = P(("dp", "group", "local"), None)
    rows = P(("group", "local"), "dp", None)
    columns = P(("group", "local"), None, "dp")
    return jax.shard_map(
        local,
        mesh=mesh,
        in_specs=(tokens, tokens, tokens, tokens, rows, rows, columns),
        out_specs=(tokens, tokens, tokens, rows, rows, columns),
        check_vma=False,
    )
```

time: 155 us -> 153 us (0.987)
  the two profiles are of different devices: /device:TPU:1 before, /device:TPU:24 now
where the time goes in v2:
time: 153 us
  starting transfers between devices  97 us (63%)
  waiting for transfers between devices  30.5 us (20%)
  Pallas kernels  19 us (12%)
  local copies, waits for them, and re-layouts  4.52 us (3%)
    ppermute x16, starting transfers between devices, shifted(): lax.ppermute(value, 'dp', [(i, (i + by) % peers) for i in range(peers)])  58.9 us
    all_to_all x2, starting transfers between devices, exchange(): lax.all_to_all(lines.reshape(peers, -1, LANES), ('group', 'local'), split...  38.1 us
    ppermute x16, waiting for transfers between devices, shifted(): lax.ppermute(value, 'dp', [(i, (i + by) % peers) for i in range(peers)])  30.5 us
    pallas_call x1, Pallas kernels, expert(): call(expert_kernel, [recv.shape] + shapes, scratch=[pltpu.VMEM(recv.shape...  9.61 us
    pallas_call x1, Pallas kernels, combine(): call(combine_kernel, [cotangent.shape, cotangent.shape, ids.shape], scrat...  3.84 us
    pallas_call x1, Pallas kernels, prepare(): call(prepare_kernel, [(lines, LANES), (3 * gate.shape[1], LANES)], scratc...  3.64 us
    unnamed x40, local copies, waits for them, and re-layouts  3.09 us
  transfers between devices with their start and end apart: 18, of which 11 were waited for; matrix products, arithmetic and copies ran while one was open for 1% of the time, Pallas kernels for 1%

profile of v2, /device:TPU:24, one launch (start us, length us, event | category | flops | bytes accessed | tf_op | source)
XLA Modules:
  0.0 152.5 jit_solution(3141570248151790748)
XLA Ops:
  0.6 3.6 %prepare.1 = (bf16[6144,128]{1,0:T(8,128)(2,1)}, bf16[1152,128]{1,0:T(8,128)(2,1)}) custom-call(bf16[16,1024]{1,0:T(8,128)(2,1)} %tokens.1, bf16[16,1024]{1,0:T(8,128)(2,1)} %cotangent.3, s32[8,16]{1,0:T(8,128)} %bitcast.21, bf16[8,16]{1,0:T(8,128)(2,1)} %bitcast.23, bf16[128,384]{1,0:T(8,128)(2,1)} %bitcast.18, bf16[128,384]{1,0:T(8,128)(2,1)} %bitcast.19, ...), custom_call_target="tpu_custom_call" | custom-call | tf_op jit(solution)/shard_map/prepare/pallas_call | solution.py:229
  4.3 24.2 %all-to-all-start = ((bf16[128,48,128]{2,1,0:T(8,128)(2,1)}), bf16[128,48,128]{2,1,0:T(8,128)(2,1)S(1)}, u32[]{:S(2)}, u32[]{:S(2)}) async-start(bf16[128,48,128]{2,1,0:T(8,128)(2,1)} %bitcast.17), calls=%async_computation | async-start | bytes 3145728 | tf_op jit(solution)/shard_map/all_to_all | solution.py:311
  28.5 0.0 copy-done.4
  28.5 2.5 %collective-permute-start = (bf16[1152,128]{1,0:T(8,128)(2,1)S(1)}, bf16[1152,128]{1,0:T(8,128)(2,1)S(1)}, u32[]{:S(2)}, u32[]{:S(2)}) collective-permute-start(bf16[1152,128]{1,0:T(8,128)(2,1)S(1)} %copy-done.4), channel_id=1, source_target_pairs={{0,128},{128,256},{256,384},{384,512},{512,640},{640,768},{768,896... | collective-permute-start | bytes 884744 | tf_op jit(solution)/shard_map/ppermute | solution.py:262
  31.0 4.6 %collective-permute-start.3 = (bf16[1152,128]{1,0:T(8,128)(2,1)S(1)}, bf16[1152,128]{1,0:T(8,128)(2,1)S(1)}, u32[]{:S(2)}, u32[]{:S(2)}) collective-permute-start(bf16[1152,128]{1,0:T(8,128)(2,1)S(1)} %copy-done.4), channel_id=1, source_target_pairs={{0,896},{128,0},{256,128},{384,256},{512,384},{640,512},{768,640},... | collective-permute-start | bytes 884744 | tf_op jit(solution)/shard_map/ppermute | solution.py:262
  35.6 5.1 %collective-permute-done.refs_1_ = bf16[1152,128]{1,0:T(8,128)(2,1)S(1)} collective-permute-done((bf16[1152,128]{1,0:T(8,128)(2,1)S(1)}, bf16[1152,128]{1,0:T(8,128)(2,1)S(1)}, u32[]{:S(2)}, u32[]{:S(2)}) %collective-permute-start) | collective-permute-done | bytes 294944 | tf_op jit(solution)/shard_map/ppermute | solution.py:262
  40.6 1.9 %collective-permute-start.1 = (bf16[1152,128]{1,0:T(8,128)(2,1)S(1)}, bf16[1152,128]{1,0:T(8,128)(2,1)S(1)}, u32[]{:S(2)}, u32[]{:S(2)}) collective-permute-start(bf16[1152,128]{1,0:T(8,128)(2,1)S(1)} %collective-permute-done.refs_1_), channel_id=1, source_target_pairs={{0,128},{128,256},{256,384},{384,512},{512,640},{640,768},{768,896... | collective-permute-start | bytes 884744 | tf_op jit(solution)/shard_map/ppermute | solution.py:262
  42.6 0.0 collective-permute-done.3.refs_4_
  42.6 0.0 copy-start.6
  42.6 5.1 %collective-permute-start.4 = (bf16[1152,128]{1,0:T(8,128)(2,1)S(1)}, bf16[1152,128]{1,0:T(8,128)(2,1)S(1)}, u32[]{:S(2)}, u32[]{:S(2)}) collective-permute-start(bf16[1152,128]{1,0:T(8,128)(2,1)S(1)} %collective-permute-done.3.refs_4_), channel_id=1, source_target_pairs={{0,896},{128,0},{256,128},{384,256},{512,384},{640,512},{768,640},... | collective-permute-start | bytes 884744 | tf_op jit(solution)/shard_map/ppermute | solution.py:262
  47.7 4.2 %collective-permute-done.1.refs_2_ = bf16[1152,128]{1,0:T(8,128)(2,1)S(1)} collective-permute-done((bf16[1152,128]{1,0:T(8,128)(2,1)S(1)}, bf16[1152,128]{1,0:T(8,128)(2,1)S(1)}, u32[]{:S(2)}, u32[]{:S(2)}) %collective-permute-start.1) | collective-permute-done | bytes 294944 | tf_op jit(solution)/shard_map/ppermute | solution.py:262
  51.9 1.9 %collective-permute-start.2 = (bf16[1152,128]{1,0:T(8,128)(2,1)S(1)}, bf16[1152,128]{1,0:T(8,128)(2,1)S(1)}, u32[]{:S(2)}, u32[]{:S(2)}) collective-permute-start(bf16[1152,128]{1,0:T(8,128)(2,1)S(1)} %collective-permute-done.1.refs_2_), channel_id=1, source_target_pairs={{0,128},{128,256},{256,384},{384,512},{512,640},{640,768},{768,896... | collective-permute-start | bytes 884744 | tf_op jit(solution)/shard_map/ppermute | solution.py:262
  53.8 0.0 collective-permute-done.4.refs_5_
  53.8 0.0 copy-start.8
  53.8 5.1 %collective-permute-start.5 = (bf16[1152,128]{1,0:T(8,128)(2,1)S(1)}, bf16[1152,128]{1,0:T(8,128)(2,1)S(1)}, u32[]{:S(2)}, u32[]{:S(2)}) collective-permute-start(bf16[1152,128]{1,0:T(8,128)(2,1)S(1)} %collective-permute-done.4.refs_5_), channel_id=1, source_target_pairs={{0,896},{128,0},{256,128},{384,256},{512,384},{640,512},{768,640},... | collective-permute-start | bytes 884744 | tf_op jit(solution)/shard_map/ppermute | solution.py:262
  59.0 3.3 %collective-permute-done.2.refs_3_ = bf16[1152,128]{1,0:T(8,128)(2,1)S(1)} collective-permute-done((bf16[1152,128]{1,0:T(8,128)(2,1)S(1)}, bf16[1152,128]{1,0:T(8,128)(2,1)S(1)}, u32[]{:S(2)}, u32[]{:S(2)}) %collective-permute-start.2) | collective-permute-done | bytes 294944 | tf_op jit(solution)/shard_map/ppermute | solution.py:262
  62.3 0.7 slice.24
  63.0 1.9 %collective-permute-start.6 = (bf16[640,128]{1,0:T(8,128)(2,1)}, bf16[640,128]{1,0:T(8,128)(2,1)S(1)}, u32[]{:S(2)}, u32[]{:S(2)}) collective-permute-start(bf16[640,128]{1,0:T(8,128)(2,1)} %slice.24), channel_id=1, source_target_pairs={{0,128},{128,256},{256,384},{384,512},{512,640},{640,768},{768,896... | collective-permute-start | bytes 491528 | tf_op jit(solution)/shard_map/ppermute | solution.py:262
  64.9 0.0 collective-permute-done.5.refs_6_
  65.0 0.0 copy-start.3
  65.0 0.7 slice.25
  65.7 5.1 %collective-permute-start.7 = (bf16[512,128]{1,0:T(8,128)(2,1)}, bf16[512,128]{1,0:T(8,128)(2,1)}, u32[]{:S(2)}, u32[]{:S(2)}) collective-permute-start(bf16[512,128]{1,0:T(8,128)(2,1)} %slice.25), channel_id=1, source_target_pairs={{0,896},{128,0},{256,128},{384,256},{512,384},{640,512},{768,640},... | collective-permute-start | bytes 393224 | tf_op jit(solution)/shard_map/ppermute | solution.py:262
  70.8 2.8 %collective-permute-done.7.refs_8_ = bf16[512,128]{1,0:T(8,128)(2,1)} collective-permute-done((bf16[512,128]{1,0:T(8,128)(2,1)}, bf16[512,128]{1,0:T(8,128)(2,1)}, u32[]{:S(2)}, u32[]{:S(2)}) %collective-permute-start.7) | collective-permute-done | bytes 131104 | tf_op jit(solution)/shard_map/ppermute | solution.py:262
  73.6 0.0 collective-permute-done.6.refs_7_
  73.6 0.0 all-to-all-done
  73.6 0.0 copy-done.5
  73.6 0.0 copy-done.6
  73.6 0.0 copy-done.7
  73.7 0.0 copy-done.8
  73.7 0.0 copy-done.2
  73.7 0.0 copy-done.3
  73.7 0.6 copy-done.17
  74.3 0.6 copy-done.1
  74.8 9.6 %expert.1 = (bf16[6144,128]{1,0:T(8,128)(2,1)}, bf16[1152,128]{1,0:T(8,128)(2,1)}, bf16[1152,128]{1,0:T(8,128)(2,1)}, bf16[1152,128]{1,0:T(8,128)(2,1)}, bf16[11...) custom-call(s32[1]{0:T(128)} %bitcast.place, ...), custom_call_target="tpu_custom_call" | custom-call | tf_op jit(solution)/shard_map/expert/pallas_call | solution.py:243
  84.5 13.9 %all-to-all-start.1 = ((bf16[128,48,128]{2,1,0:T(8,128)(2,1)}), bf16[128,48,128]{2,1,0:T(8,128)(2,1)S(1)}, u32[]{:S(2)}, u32[]{:S(2)}) async-start(bf16[128,48,128]{2,1,0:T(8,128)(2,1)} %bitcast.16), calls=%async_computation.1 | async-start | bytes 3145728 | tf_op jit(solution)/shard_map/all_to_all | solution.py:311
  98.4 5.9 %collective-permute-start.12 = (bf16[512,128]{1,0:T(8,128)(2,1)S(1)}, bf16[512,128]{1,0:T(8,128)(2,1)S(1)}, u32[]{:S(2)}, u32[]{:S(2)}) collective-permute-start(bf16[512,128]{1,0:T(8,128)(2,1)S(1)} %copy-done.19), channel_id=1, source_target_pairs={{0,896},{128,0},{256,128},{384,256},{512,384},{640,512},{768,640},... | collective-permute-start | bytes 393224 | tf_op jit(solution)/shard_map/ppermute | solution.py:262
  104.3 0.0 copy-done.16
  104.3 0.0 copy-done.15
  104.3 0.0 copy-start.11
  104.4 2.1 %collective-permute-start.8 = (bf16[640,128]{1,0:T(8,128)(2,1)S(1)}, bf16[640,128]{1,0:T(8,128)(2,1)S(1)}, u32[]{:S(2)}, u32[]{:S(2)}) collective-permute-start(bf16[640,128]{1,0:T(8,128)(2,1)S(1)} %copy-done.18), channel_id=1, source_target_pairs={{0,128},{128,256},{256,384},{384,512},{512,640},{640,768},{768,896... | collective-permute-start | bytes 491528 | tf_op jit(solution)/shard_map/ppermute | solution.py:262
  106.4 0.9 collective-permute-done.12
  107.4 5.7 %collective-permute-start.13 = (bf16[1152,128]{1,0:T(8,128)(2,1)S(1)}, bf16[1152,128]{1,0:T(8,128)(2,1)S(1)}, u32[]{:S(2)}, u32[]{:S(2)}) collective-permute-start(bf16[1152,128]{1,0:T(8,128)(2,1)S(1)} %pad_maximum_fusion.1), channel_id=1, source_target_pairs={{0,896},{128,0},{256,128},{384,256},{512,384},{640,512},{768,640},... | collective-permute-start | bytes 884744 | tf_op jit(solution)/shard_map/ppermute | solution.py:262
  113.1 0.4 collective-permute-done.8
  113.6 2.1 %collective-permute-start.9 = (bf16[1152,128]{1,0:T(8,128)(2,1)S(1)}, bf16[1152,128]{1,0:T(8,128)(2,1)S(1)}, u32[]{:S(2)}, u32[]{:S(2)}) collective-permute-start(bf16[1152,128]{1,0:T(8,128)(2,1)S(1)} %pad_maximum_fusion), channel_id=1, source_target_pairs={{0,128},{128,256},{256,384},{384,512},{512,640},{640,768},{768,896... | collective-permute-start | bytes 884744 | tf_op jit(solution)/shard_map/ppermute | solution.py:262
  115.7 3.1 %collective-permute-done.13 = bf16[1152,128]{1,0:T(8,128)(2,1)S(1)} collective-permute-done((bf16[1152,128]{1,0:T(8,128)(2,1)S(1)}, bf16[1152,128]{1,0:T(8,128)(2,1)S(1)}, u32[]{:S(2)}, u32[]{:S(2)}) %collective-permute-start.13) | collective-permute-done | bytes 294944 | tf_op jit(solution)/shard_map/ppermute | solution.py:262
  118.8 0.0 copy-done.12
  118.8 0.1 add.22
  118.9 5.6 %collective-permute-start.14 = (bf16[1152,128]{1,0:T(8,128)(2,1)S(1)}, bf16[1152,128]{1,0:T(8,128)(2,1)S(1)}, u32[]{:S(2)}, u32[]{:S(2)}) collective-permute-start(bf16[1152,128]{1,0:T(8,128)(2,1)S(1)} %add.22), channel_id=1, source_target_pairs={{0,896},{128,0},{256,128},{384,256},{512,384},{640,512},{768,640},... | collective-permute-start | bytes 884744 | tf_op jit(solution)/shard_map/ppermute | solution.py:262
  124.5 0.3 collective-permute-done.9
  124.7 0.1 add.19
  124.8 1.9 %collective-permute-start.10 = (bf16[1152,128]{1,0:T(8,128)(2,1)S(1)}, bf16[1152,128]{1,0:T(8,128)(2,1)S(1)}, u32[]{:S(2)}, u32[]{:S(2)}) collective-permute-start(bf16[1152,128]{1,0:T(8,128)(2,1)S(1)} %add.19), channel_id=1, source_target_pairs={{0,128},{128,256},{256,384},{384,512},{512,640},{640,768},{768,896... | collective-permute-start | bytes 884744 | tf_op jit(solution)/shard_map/ppermute | solution.py:262
  126.8 2.5 %collective-permute-done.14 = bf16[1152,128]{1,0:T(8,128)(2,1)S(1)} collective-permute-done((bf16[1152,128]{1,0:T(8,128)(2,1)S(1)}, bf16[1152,128]{1,0:T(8,128)(2,1)S(1)}, u32[]{:S(2)}, u32[]{:S(2)}) %collective-permute-start.14) | collective-permute-done | bytes 294944 | tf_op jit(solution)/shard_map/ppermute | solution.py:262
  129.3 0.1 add.23
  129.4 5.6 %collective-permute-start.15 = (bf16[1152,128]{1,0:T(8,128)(2,1)S(1)}, bf16[1152,128]{1,0:T(8,128)(2,1)S(1)}, u32[]{:S(2)}, u32[]{:S(2)}) collective-permute-start(bf16[1152,128]{1,0:T(8,128)(2,1)S(1)} %add.23), channel_id=1, source_target_pairs={{0,896},{128,0},{256,128},{384,256},{512,384},{640,512},{768,640},... | collective-permute-start | bytes 884744 | tf_op jit(solution)/shard_map/ppermute | solution.py:262
  135.0 0.0 collective-permute-done.10
  135.0 0.1 add.20
  135.1 1.9 %collective-permute-start.11 = (bf16[1152,128]{1,0:T(8,128)(2,1)S(1)}, bf16[1152,128]{1,0:T(8,128)(2,1)S(1)}, u32[]{:S(2)}, u32[]{:S(2)}) collective-permute-start(bf16[1152,128]{1,0:T(8,128)(2,1)S(1)} %add.20), channel_id=1, source_target_pairs={{0,128},{128,256},{256,384},{384,512},{512,640},{640,768},{768,896... | collective-permute-start | bytes 884744 | tf_op jit(solution)/shard_map/ppermute | solution.py:262
  137.0 2.2 %collective-permute-done.15.left = bf16[1152,128]{1,0:T(8,128)(2,1)S(1)} collective-permute-done((bf16[1152,128]{1,0:T(8,128)(2,1)S(1)}, bf16[1152,128]{1,0:T(8,128)(2,1)S(1)}, u32[]{:S(2)}, u32[]{:S(2)}) %collective-permute-start.15) | collective-permute-done | bytes 294944 | tf_op jit(solution)/shard_map/ppermute | solution.py:262
  139.2 5.7 %collective-permute-done.11.right = bf16[1152,128]{1,0:T(8,128)(2,1)S(1)} collective-permute-done((bf16[1152,128]{1,0:T(8,128)(2,1)S(1)}, bf16[1152,128]{1,0:T(8,128)(2,1)S(1)}, u32[]{:S(2)}, u32[]{:S(2)}) %collective-permute-start.11) | collective-permute-done | bytes 294944 | tf_op jit(solution)/shard_map/ppermute | solution.py:262
  144.9 0.7 copy-done.14
  145.6 1.9 %unpack_grads.1 = (bf16[128,384]{1,0:T(8,128)(2,1)}, bf16[128,384]{1,0:T(8,128)(2,1)}, bf16[384,128]{1,0:T(8,128)(2,1)}) custom-call(bf16[1152,128]{1,0:T(8,128)(2,1)} %get-tuple-element.30.own, bf16[1152,128]{1,0:T(8,128)(2,1)} %copy-done.14, bf16[1152,128]{1,0:T(8,128)(2,1)} %copy-done.13), custom_call_target="tpu_custom_call" | custom-call | tf_op jit(solution)/shard_map/unpack_grads/pallas_call | solution.py:302
  147.5 0.0 all-to-all-done.1
  147.5 1.2 copy-done
  148.7 3.8 %combine.1 = (bf16[16,1024]{1,0:T(8,128)(2,1)}, bf16[16,1024]{1,0:T(8,128)(2,1)}, bf16[8,16]{1,0:T(8,128)(2,1)}) custom-call(bf16[6144,128]{1,0:T(8,128)(2,1)} %bitcast.14, bf16[16,1024]{1,0:T(8,128)(2,1)} %cotangent.3, s32[8,16]{1,0:T(8,128)} %bitcast.22, bf16[8,16]{1,0:T(8,128)(2,1)} %bitcast.24), custom_call_target="tpu_custom_call" | custom-call | tf_op jit(solution)/shard_map/combine/pallas_call | solution.py:292
  (28 shorter events, 0.2 us)
Async XLA Ops:
  4.3 24.2 %copy-start.4 = (bf16[1152,128]{1,0:T(8,128)(2,1)S(1)}, bf16[1152,128]{1,0:T(8,128)(2,1)}, u32[]{:S(2)}) copy-start(bf16[1152,128]{1,0:T(8,128)(2,1)} %get-tuple-element.25.refs_0_) | copy-start | bytes 884740
  4.3 69.3 %all-to-all-start = ((bf16[128,48,128]{2,1,0:T(8,128)(2,1)}), bf16[128,48,128]{2,1,0:T(8,128)(2,1)S(1)}, u32[]{:S(2)}, u32[]{:S(2)}) async-start(bf16[128,48,128]{2,1,0:T(8,128)(2,1)} %bitcast.17), calls=%async_computation | async-start | bytes 3145728 | tf_op jit(solution)/shard_map/all_to_all | solution.py:311
  28.5 12.1 %collective-permute-start = (bf16[1152,128]{1,0:T(8,128)(2,1)S(1)}, bf16[1152,128]{1,0:T(8,128)(2,1)S(1)}, u32[]{:S(2)}, u32[]{:S(2)}) collective-permute-start(bf16[1152,128]{1,0:T(8,128)(2,1)S(1)} %copy-done.4), channel_id=1, source_target_pairs={{0,128},{128,256},{256,384},{384,512},{512,640},{640,768},{768,896... | collective-permute-start | bytes 884744 | tf_op jit(solution)/shard_map/ppermute | solution.py:262
  31.0 11.5 %collective-permute-start.3 = (bf16[1152,128]{1,0:T(8,128)(2,1)S(1)}, bf16[1152,128]{1,0:T(8,128)(2,1)S(1)}, u32[]{:S(2)}, u32[]{:S(2)}) collective-permute-start(bf16[1152,128]{1,0:T(8,128)(2,1)S(1)} %copy-done.4), channel_id=1, source_target_pairs={{0,896},{128,0},{256,128},{384,256},{512,384},{640,512},{768,640},... | collective-permute-start | bytes 884744 | tf_op jit(solution)/shard_map/ppermute | solution.py:262
  40.6 33.0 %copy-start.5 = (bf16[1152,128]{1,0:T(8,128)(2,1)}, bf16[1152,128]{1,0:T(8,128)(2,1)S(1)}, u32[]{:S(2)}) copy-start(bf16[1152,128]{1,0:T(8,128)(2,1)S(1)} %collective-permute-done.refs_1_) | copy-start | bytes 884740
  40.6 11.3 %collective-permute-start.1 = (bf16[1152,128]{1,0:T(8,128)(2,1)S(1)}, bf16[1152,128]{1,0:T(8,128)(2,1)S(1)}, u32[]{:S(2)}, u32[]{:S(2)}) collective-permute-start(bf16[1152,128]{1,0:T(8,128)(2,1)S(1)} %collective-permute-done.refs_1_), channel_id=1, source_target_pairs={{0,128},{128,256},{256,384},{384,512},{512,640},{640,768},{768,896... | collective-permute-start | bytes 884744 | tf_op jit(solution)/shard_map/ppermute | solution.py:262
  42.6 31.1 %copy-start.6 = (bf16[1152,128]{1,0:T(8,128)(2,1)}, bf16[1152,128]{1,0:T(8,128)(2,1)S(1)}, u32[]{:S(2)}) copy-start(bf16[1152,128]{1,0:T(8,128)(2,1)S(1)} %collective-permute-done.3.refs_4_) | copy-start | bytes 884740
  42.6 11.2 %collective-permute-start.4 = (bf16[1152,128]{1,0:T(8,128)(2,1)S(1)}, bf16[1152,128]{1,0:T(8,128)(2,1)S(1)}, u32[]{:S(2)}, u32[]{:S(2)}) collective-permute-start(bf16[1152,128]{1,0:T(8,128)(2,1)S(1)} %collective-permute-done.3.refs_4_), channel_id=1, source_target_pairs={{0,896},{128,0},{256,128},{384,256},{512,384},{640,512},{768,640},... | collective-permute-start | bytes 884744 | tf_op jit(solution)/shard_map/ppermute | solution.py:262
  51.9 21.7 %copy-start.7 = (bf16[1152,128]{1,0:T(8,128)(2,1)}, bf16[1152,128]{1,0:T(8,128)(2,1)S(1)}, u32[]{:S(2)}) copy-start(bf16[1152,128]{1,0:T(8,128)(2,1)S(1)} %collective-permute-done.1.refs_2_) | copy-start | bytes 884740
  51.9 10.4 %collective-permute-start.2 = (bf16[1152,128]{1,0:T(8,128)(2,1)S(1)}, bf16[1152,128]{1,0:T(8,128)(2,1)S(1)}, u32[]{:S(2)}, u32[]{:S(2)}) collective-permute-start(bf16[1152,128]{1,0:T(8,128)(2,1)S(1)} %collective-permute-done.1.refs_2_), channel_id=1, source_target_pairs={{0,128},{128,256},{256,384},{384,512},{512,640},{640,768},{768,896... | collective-permute-start | bytes 884744 | tf_op jit(solution)/shard_map/ppermute | solution.py:262
  53.8 19.8 %copy-start.8 = (bf16[1152,128]{1,0:T(8,128)(2,1)}, bf16[1152,128]{1,0:T(8,128)(2,1)S(1)}, u32[]{:S(2)}) copy-start(bf16[1152,128]{1,0:T(8,128)(2,1)S(1)} %collective-permute-done.4.refs_5_) | copy-start | bytes 884740
  53.8 11.1 %collective-permute-start.5 = (bf16[1152,128]{1,0:T(8,128)(2,1)S(1)}, bf16[1152,128]{1,0:T(8,128)(2,1)S(1)}, u32[]{:S(2)}, u32[]{:S(2)}) collective-permute-start(bf16[1152,128]{1,0:T(8,128)(2,1)S(1)} %collective-permute-done.4.refs_5_), channel_id=1, source_target_pairs={{0,896},{128,0},{256,128},{384,256},{512,384},{640,512},{768,640},... | collective-permute-start | bytes 884744 | tf_op jit(solution)/shard_map/ppermute | solution.py:262
  62.3 11.3 %copy-start.2 = (bf16[1152,128]{1,0:T(8,128)(2,1)}, bf16[1152,128]{1,0:T(8,128)(2,1)S(1)}, u32[]{:S(2)}) copy-start(bf16[1152,128]{1,0:T(8,128)(2,1)S(1)} %collective-permute-done.2.refs_3_) | copy-start | bytes 884740
  63.0 10.6 %collective-permute-start.6 = (bf16[640,128]{1,0:T(8,128)(2,1)}, bf16[640,128]{1,0:T(8,128)(2,1)S(1)}, u32[]{:S(2)}, u32[]{:S(2)}) collective-permute-start(bf16[640,128]{1,0:T(8,128)(2,1)} %slice.24), channel_id=1, source_target_pairs={{0,128},{128,256},{256,384},{384,512},{512,640},{640,768},{768,896... | collective-permute-start | bytes 491528 | tf_op jit(solution)/shard_map/ppermute | solution.py:262
  65.0 8.7 %copy-start.3 = (bf16[1152,128]{1,0:T(8,128)(2,1)}, bf16[1152,128]{1,0:T(8,128)(2,1)S(1)}, u32[]{:S(2)}) copy-start(bf16[1152,128]{1,0:T(8,128)(2,1)S(1)} %collective-permute-done.5.refs_6_) | copy-start | bytes 884740
  65.7 7.9 %collective-permute-start.7 = (bf16[512,128]{1,0:T(8,128)(2,1)}, bf16[512,128]{1,0:T(8,128)(2,1)}, u32[]{:S(2)}, u32[]{:S(2)}) collective-permute-start(bf16[512,128]{1,0:T(8,128)(2,1)} %slice.25), channel_id=1, source_target_pairs={{0,896},{128,0},{256,128},{384,256},{512,384},{640,512},{768,640},... | collective-permute-start | bytes 393224 | tf_op jit(solution)/shard_map/ppermute | solution.py:262
  73.6 0.7 copy-start.17
  73.6 1.2 copy-start.1
  84.4 13.9 %copy-start.19 = (bf16[512,128]{1,0:T(8,128)(2,1)S(1)}, bf16[512,128]{1,0:T(8,128)(2,1)}, u32[]{:S(2)}) copy-start(bf16[512,128]{1,0:T(8,128)(2,1)} %get-tuple-element.38) | copy-start | bytes 393220
  84.5 19.8 %copy-start.16 = (bf16[1152,128]{1,0:T(8,128)(2,1)S(1)}, bf16[1152,128]{1,0:T(8,128)(2,1)}, u32[]{:S(2)}) copy-start(bf16[1152,128]{1,0:T(8,128)(2,1)} %get-tuple-element.33) | copy-start | bytes 884740
  84.5 19.9 %copy-start.15 = (bf16[1152,128]{1,0:T(8,128)(2,1)S(1)}, bf16[1152,128]{1,0:T(8,128)(2,1)}, u32[]{:S(2)}) copy-start(bf16[1152,128]{1,0:T(8,128)(2,1)} %get-tuple-element.37) | copy-start | bytes 884740
  84.5 19.9 %copy-start.18 = (bf16[640,128]{1,0:T(8,128)(2,1)S(1)}, bf16[640,128]{1,0:T(8,128)(2,1)}, u32[]{:S(2)}) copy-start(bf16[640,128]{1,0:T(8,128)(2,1)} %get-tuple-element.34) | copy-start | bytes 491524
  84.5 63.0 %all-to-all-start.1 = ((bf16[128,48,128]{2,1,0:T(8,128)(2,1)}), bf16[128,48,128]{2,1,0:T(8,128)(2,1)S(1)}, u32[]{:S(2)}, u32[]{:S(2)}) async-start(bf16[128,48,128]{2,1,0:T(8,128)(2,1)} %bitcast.16), calls=%async_computation.1 | async-start | bytes 3145728 | tf_op jit(solution)/shard_map/all_to_all | solution.py:311
  98.4 20.4 %copy-start.12 = (bf16[1152,128]{1,0:T(8,128)(2,1)S(1)}, bf16[1152,128]{1,0:T(8,128)(2,1)}, u32[]{:S(2)}) copy-start(bf16[1152,128]{1,0:T(8,128)(2,1)} %get-tuple-element.36) | copy-start | bytes 884740
  98.4 8.9 %collective-permute-start.12 = (bf16[512,128]{1,0:T(8,128)(2,1)S(1)}, bf16[512,128]{1,0:T(8,128)(2,1)S(1)}, u32[]{:S(2)}, u32[]{:S(2)}) collective-permute-start(bf16[512,128]{1,0:T(8,128)(2,1)S(1)} %copy-done.19), channel_id=1, source_target_pairs={{0,896},{128,0},{256,128},{384,256},{512,384},{640,512},{768,640},... | collective-permute-start | bytes 393224 | tf_op jit(solution)/shard_map/ppermute | solution.py:262
  104.3 20.4 %copy-start.11 = (bf16[1152,128]{1,0:T(8,128)(2,1)S(1)}, bf16[1152,128]{1,0:T(8,128)(2,1)}, u32[]{:S(2)}) copy-start(bf16[1152,128]{1,0:T(8,128)(2,1)} %get-tuple-element.32) | copy-start | bytes 884740
  104.4 9.2 %collective-permute-start.8 = (bf16[640,128]{1,0:T(8,128)(2,1)S(1)}, bf16[640,128]{1,0:T(8,128)(2,1)S(1)}, u32[]{:S(2)}, u32[]{:S(2)}) collective-permute-start(bf16[640,128]{1,0:T(8,128)(2,1)S(1)} %copy-done.18), channel_id=1, source_target_pairs={{0,128},{128,256},{256,384},{384,512},{512,640},{640,768},{768,896... | collective-permute-start | bytes 491528 | tf_op jit(solution)/shard_map/ppermute | solution.py:262
  107.4 21.9 %copy-start.10 = (bf16[1152,128]{1,0:T(8,128)(2,1)S(1)}, bf16[1152,128]{1,0:T(8,128)(2,1)}, u32[]{:S(2)}) copy-start(bf16[1152,128]{1,0:T(8,128)(2,1)} %get-tuple-element.35) | copy-start | bytes 884740
  107.4 11.4 %collective-permute-start.13 = (bf16[1152,128]{1,0:T(8,128)(2,1)S(1)}, bf16[1152,128]{1,0:T(8,128)(2,1)S(1)}, u32[]{:S(2)}, u32[]{:S(2)}) collective-permute-start(bf16[1152,128]{1,0:T(8,128)(2,1)S(1)} %pad_maximum_fusion.1), channel_id=1, source_target_pairs={{0,896},{128,0},{256,128},{384,256},{512,384},{640,512},{768,640},... | collective-permute-start | bytes 884744 | tf_op jit(solution)/shard_map/ppermute | solution.py:262
  113.6 21.4 %copy-start.9 = (bf16[1152,128]{1,0:T(8,128)(2,1)S(1)}, bf16[1152,128]{1,0:T(8,128)(2,1)}, u32[]{:S(2)}) copy-start(bf16[1152,128]{1,0:T(8,128)(2,1)} %get-tuple-element.31) | copy-start | bytes 884740
  113.6 11.1 %collective-permute-start.9 = (bf16[1152,128]{1,0:T(8,128)(2,1)S(1)}, bf16[1152,128]{1,0:T(8,128)(2,1)S(1)}, u32[]{:S(2)}, u32[]{:S(2)}) collective-permute-start(bf16[1152,128]{1,0:T(8,128)(2,1)S(1)} %pad_maximum_fusion), channel_id=1, source_target_pairs={{0,128},{128,256},{256,384},{384,512},{512,640},{640,768},{768,896... | collective-permute-start | bytes 884744 | tf_op jit(solution)/shard_map/ppermute | solution.py:262
  118.9 10.4 %collective-permute-start.14 = (bf16[1152,128]{1,0:T(8,128)(2,1)S(1)}, bf16[1152,128]{1,0:T(8,128)(2,1)S(1)}, u32[]{:S(2)}, u32[]{:S(2)}) collective-permute-start(bf16[1152,128]{1,0:T(8,128)(2,1)S(1)} %add.22), channel_id=1, source_target_pairs={{0,896},{128,0},{256,128},{384,256},{512,384},{640,512},{768,640},... | collective-permute-start | bytes 884744 | tf_op jit(solution)/shard_map/ppermute | solution.py:262
  124.8 10.2 %collective-permute-start.10 = (bf16[1152,128]{1,0:T(8,128)(2,1)S(1)}, bf16[1152,128]{1,0:T(8,128)(2,1)S(1)}, u32[]{:S(2)}, u32[]{:S(2)}) collective-permute-start(bf16[1152,128]{1,0:T(8,128)(2,1)S(1)} %add.19), channel_id=1, source_target_pairs={{0,128},{128,256},{256,384},{384,512},{512,640},{640,768},{768,896... | collective-permute-start | bytes 884744 | tf_op jit(solution)/shard_map/ppermute | solution.py:262
  129.4 9.8 %collective-permute-start.15 = (bf16[1152,128]{1,0:T(8,128)(2,1)S(1)}, bf16[1152,128]{1,0:T(8,128)(2,1)S(1)}, u32[]{:S(2)}, u32[]{:S(2)}) collective-permute-start(bf16[1152,128]{1,0:T(8,128)(2,1)S(1)} %add.23), channel_id=1, source_target_pairs={{0,896},{128,0},{256,128},{384,256},{512,384},{640,512},{768,640},... | collective-permute-start | bytes 884744 | tf_op jit(solution)/shard_map/ppermute | solution.py:262
  135.1 9.8 %collective-permute-start.11 = (bf16[1152,128]{1,0:T(8,128)(2,1)S(1)}, bf16[1152,128]{1,0:T(8,128)(2,1)S(1)}, u32[]{:S(2)}, u32[]{:S(2)}) collective-permute-start(bf16[1152,128]{1,0:T(8,128)(2,1)S(1)} %add.20), channel_id=1, source_target_pairs={{0,128},{128,256},{256,384},{384,512},{512,640},{640,768},{768,896... | collective-permute-start | bytes 884744 | tf_op jit(solution)/shard_map/ppermute | solution.py:262
  139.2 5.7 %copy-start.13 = (bf16[1152,128]{1,0:T(8,128)(2,1)}, bf16[1152,128]{1,0:T(8,128)(2,1)S(1)}, u32[]{:S(2)}) copy-start(bf16[1152,128]{1,0:T(8,128)(2,1)S(1)} %collective-permute-done.15.left) | copy-start | bytes 884740
  144.9 0.7 copy-start.14
  147.5 1.2 copy-start

commit v3 on v2

--- a/solution.py
+++ b/solution.py
@@ -5,10 +5,12 @@
 from jax.experimental.pallas import tpu as pltpu
 from jax.sharding import PartitionSpec as P
 
+
 INTERPRET = False
 BF16 = jnp.bfloat16
 F32 = jnp.float32
 LANES = 128
+RING = (0, 7, 6, 5, 4, 1, 2, 3)
 CAP = 3
 
 
@@ -77,9 +79,9 @@
 
 
 def expert_kernel(place, recv, *refs):
-    pieces, outs, scratch = refs[:9], refs[9:19], refs[19:]
+    pieces, outs, scratch = refs[:8], refs[8:17], refs[17:]
     back, terms = outs[0], outs[1:]
-    rows, gate_up, down, term, down_term, sems = scratch
+    rows, gate_up, down, term, down_term, leaving, in_sems, out_sems, back_sem = scratch
     peers, features, _ = gate_up.shape
     hidden = down.shape[1]
     width = peers * features
@@ -89,20 +91,21 @@
     me = place[0]
     tiles = 2 * hidden // LANES
     early, late = [], []
-    starts = [0, -1, -2, -3, 1, 2, 3, 4, 4]
-    for n, (piece, offset) in enumerate(zip(pieces, starts)):
-        d = lax.rem(me + offset + peers, peers)
-        first = pieces[7].shape[0] if n == 8 else 0
-        for i in range(piece.shape[0] // LANES):
-            at = first // LANES + i
-            if at < tiles:
-                target = gate_up.at[d, :, pl.ds(at * LANES, LANES)]
-            else:
-                target = down.at[d, pl.ds((at - tiles) * LANES, LANES), :]
-            copy = pltpu.make_async_copy(
-                piece.at[pl.ds(i * LANES, LANES), :], target, sems.at[n, i]
+    for n, (piece, offset) in enumerate(zip(pieces, RING)):
+        d = lax.rem(me + offset, peers)
+        for i in range(tiles):
+            early.append(
+                pltpu.make_async_copy(
+                    piece.at[pl.ds(i * LANES, LANES), :],
+                    gate_up.at[d, :, pl.ds(i * LANES, LANES)],
+                    in_sems.at[n, i],
+                )
             )
-            (early if at < tiles else late).append(copy)
+        late.append(
+            pltpu.make_async_copy(
+                piece.at[pl.ds(2 * hidden, hidden), :], down.at[d], in_sems.at[n, tiles]
+            )
+        )
     for copy in early + late:
         copy.start()
     rows[...] = recv[...].astype(F32)
@@ -133,22 +136,36 @@
     back_grad = dot(both, wide, ((1,), (1,)))
     for r in range(CAP):
         spread_rows(back_grad[r * sources : (r + 1) * sources], rows, (CAP + r) * per, blocks)
-    back[...] = rows[...].astype(BF16)
-    term[...] = dot(x, both, ((0,), (0,))).astype(BF16).reshape(term.shape)
+    leaving[...] = rows[...].astype(BF16)
+    send_back = pltpu.make_async_copy(leaving, back, back_sem.at[0])
+    send_back.start()
     down_full = dot(inner, g, ((0,), (0,))).astype(BF16)
     for d in range(peers):
         down_term[d] = down_full[:, d * features : (d + 1) * features]
-    for n, (ref, offset) in enumerate(zip(terms, [0, 1, 2, 3, 5, 6, 7, 4, 4])):
-        d = lax.rem(me + offset, peers)
-        first = terms[7].shape[0] if n == 8 else 0
-        for i in range(ref.shape[0] // LANES):
-            at = first // LANES + i
-            if at < tiles:
-                ref[i * LANES : (i + 1) * LANES, :] = term[d, :, at * LANES : (at + 1) * LANES]
-            else:
-                ref[i * LANES : (i + 1) * LANES, :] = down_term[
-                    d, (at - tiles) * LANES : (at - tiles + 1) * LANES, :
-                ]
+    places = [lax.rem(me + offset, peers) for offset in range(peers)]
+    copies = [
+        pltpu.make_async_copy(
+            down_term.at[d], ref.at[pl.ds(2 * hidden, hidden), :], out_sems.at[n, tiles]
+        )
+        for n, (ref, d) in enumerate(zip(terms, places))
+    ]
+    for copy in copies:
+        copy.start()
+    term[...] = dot(x, both, ((0,), (0,))).astype(BF16).reshape(term.shape)
+    lines = [
+        pltpu.make_async_copy(
+            term.at[d, :, pl.ds(i * LANES, LANES)],
+            ref.at[pl.ds(i * LANES, LANES), :],
+            out_sems.at[n, i],
+        )
+        for n, (ref, d) in enumerate(zip(terms, places))
+        for i in range(tiles)
+    ]
+    for copy in lines:
+        copy.start()
+    for copy in copies + lines:
+        copy.wait()
+    send_back.wait()
 
 
 def combine_kernel(back, cotangent, ids, weights, layer, token_grads, router_grads, rows):
@@ -158,7 +175,7 @@
     blocks = 2 * CAP * per
     experts = back.shape[0] // blocks
     rows[...] = back[...].astype(F32)
-    matches, named, rank = token_ranks(ids[...], experts)
+    matches, _, rank = token_ranks(ids[...], experts)
     ranks = [rank == float(r) for r in range(CAP)]
     pick = jnp.concatenate(
         [
@@ -210,7 +227,7 @@
     down[...] = total[2 * hidden :, :]
 
 
-def call(kernel, outs, scratch=(), in_specs=None, name=None):
+def call(kernel, outs, scratch=(), in_specs=None):
     shapes = [jax.ShapeDtypeStruct(shape, BF16) for shape in outs]
     single = len(shapes) == 1
     return pl.pallas_call(
@@ -220,7 +237,6 @@
         out_specs=vmem() if single else [vmem() for _ in shapes],
         scratch_shapes=list(scratch),
         interpret=INTERPRET,
-        name=name,
     )
 
 
@@ -231,28 +247,32 @@
         [(lines, LANES), (3 * gate.shape[1], LANES)],
         scratch=[pltpu.VMEM((lines, LANES), F32)],
         in_specs=[vmem()] * 7,
-        name="prepare",
     )(tokens, cotangent, ids, weights, gate, up, down)
 
 
 def expert(place, recv, pieces, hidden, width):
     peers = width // LANES
-    lines, half = pieces[0].shape[0], pieces[7].shape[0]
-    first, second = half, lines - half
-    shapes = [(lines, LANES)] * 7 + [(first, LANES), (second, LANES)]
-    return call(
+    lines = pieces[0].shape[0]
+    anywhere = pl.BlockSpec(memory_space=pl.ANY)
+    copies = 2 * hidden // LANES + 1
+    return pl.pallas_call(
         expert_kernel,
-        [recv.shape] + shapes,
-        scratch=[
+        out_shape=[jax.ShapeDtypeStruct(recv.shape, BF16)]
+        + [jax.ShapeDtypeStruct((lines, LANES), BF16)] * peers,
+        in_specs=[pl.BlockSpec(memory_space=pltpu.SMEM), vmem()] + [anywhere] * peers,
+        out_specs=[anywhere] * (1 + peers),
+        scratch_shapes=[
             pltpu.VMEM(recv.shape, F32),
             pltpu.VMEM((peers, LANES, 2 * hidden), BF16),
             pltpu.VMEM((peers, hidden, LANES), BF16),
             pltpu.VMEM((peers, LANES, 2 * hidden), BF16),
             pltpu.VMEM((peers, hidden, LANES), BF16),
-            pltpu.SemaphoreType.DMA((9, lines // LANES)),
+            pltpu.VMEM(recv.shape, BF16),
+            pltpu.SemaphoreType.DMA((peers, copies)),
+            pltpu.SemaphoreType.DMA((peers, copies)),
+            pltpu.SemaphoreType.DMA((1,)),
         ],
-        in_specs=[pl.BlockSpec(memory_space=pltpu.SMEM), vmem()]
-        + [pl.BlockSpec(memory_space=pl.ANY)] * 9,
+        interpret=INTERPRET,
         name="expert",
     )(place, recv, *pieces)
 
@@ -263,29 +283,22 @@
 
 
 def gather_ring(chunk):
-    half = far_half(chunk.shape[0])
     right, left = [chunk], [chunk]
+    for _ in range(4):
+        right.append(shifted(right[-1], 1))
     for _ in range(3):
-        right.append(shifted(right[-1], 1))
         left.append(shifted(left[-1], -1))
-    far = [shifted(right[-1][:half], 1), shifted(left[-1][half:], -1)]
-    return right + left[1:] + far
-
-
-def far_half(lines):
-    return lines // LANES // 2 * LANES + lines // LANES % 2 * LANES
+    return right + left[1:]
 
 
 def scatter_ring(terms):
-    own, near, two, three, far3, far2, far1, first, second = terms
-    half = first.shape[0]
-    right, left = shifted(first, 1), shifted(second, -1)
-    right = jnp.concatenate([three[:half] + right, three[half:]], axis=0)
-    left = jnp.concatenate([far3[:half], far3[half:] + left], axis=0)
-    right, left = shifted(right, 1), shifted(left, -1)
-    right, left = shifted(two + right, 1), shifted(far2 + left, -1)
-    right, left = shifted(near + right, 1), shifted(far1 + left, -1)
-    return own, right, left
+    right = shifted(terms[4], 1)
+    left = shifted(terms[5], -1)
+    for step in (1, 2, 3):
+        right = shifted(terms[4 - step] + right, 1)
+        if step < 3:
+            left = shifted(terms[5 + step] + left, -1)
+    return terms[0], right, left
 
 
 def combine(back, cotangent, ids, weights):
@@ -294,7 +307,6 @@
         [cotangent.shape, cotangent.shape, ids.shape],
         scratch=[pltpu.VMEM(back.shape, F32)],
         in_specs=[vmem()] * 4,
-        name="combine",
     )(back, cotangent, ids, weights)
 
 
@@ -303,13 +315,16 @@
         unpack_kernel,
         [(features, hidden), (features, hidden), (hidden, LANES)],
         in_specs=[vmem()] * 3,
-        name="unpack_grads",
     )(*parts)
 
 
 def exchange(lines, peers):
     out = lax.all_to_all(
-        lines.reshape(peers, -1, LANES), ("group", "local"), split_axis=0, concat_axis=0, tiled=True
+        lines.reshape(peers, -1, LANES),
+        ("group", "local"),
+        split_axis=0,
+        concat_axis=0,
+        tiled=True,
     )
     return out.reshape(lines.shape)
 

time: 153 us -> 150 us (0.980)
  starting transfers between devices: 97 us -> 84.4 us
  waiting for transfers between devices: 30.5 us -> 40.9 us
    ppermute x16 -> x14, starting transfers between devices: 58.9 us -> 46.3 us  [shifted(): lax.ppermute(value, 'dp', [(i, (i + by) % peers) for i in range(peers)])]
    ppermute x16 -> x14, waiting for transfers between devices: 30.5 us -> 40.9 us  [shifted(): lax.ppermute(value, 'dp', [(i, (i + by) % peers) for i in range(peers)])]
    unnamed x40 -> x36, local copies, waits for them, and re-layouts: 3.09 us -> 3.05 us
  transfers between devices with their start and end apart: 18 -> 16, of which waited for: 11 -> 8; matrix products, arithmetic and copies ran while one was open for 1% -> 0% of each run, Pallas kernels for 1% -> 1%
where the time goes in v3:
time: 150 us; the launch traced here: 149 us
  starting transfers between devices  84.4 us (56%)
  waiting for transfers between devices  40.9 us (27%)
  Pallas kernels  19 us (13%)
  local copies, waits for them, and re-layouts  3.05 us (2%)
    ppermute x14, starting transfers between devices, shifted(): lax.ppermute(value, 'dp', [(i, (i + by) % peers) for i in range(peers)])  46.3 us
    ppermute x14, waiting for transfers between devices, shifted(): lax.ppermute(value, 'dp', [(i, (i + by) % peers) for i in range(peers)])  40.9 us
    all_to_all x2, starting transfers between devices, exchange(): lax.all_to_all(lines.reshape(peers, -1, LANES), ('group', 'local'), split...  38.1 us
    pallas_call x1, Pallas kernels, expert(): pl.pallas_call(expert_kernel, out_shape=[jax.ShapeDtypeStruct(recv.shape,...  9.62 us
    pallas_call x1, Pallas kernels, combine(): call(combine_kernel, [cotangent.shape, cotangent.shape, ids.shape], scrat...  3.84 us
    pallas_call x1, Pallas kernels, prepare(): call(prepare_kernel, [(lines, LANES), (3 * gate.shape[1], LANES)], scratc...  3.66 us
    unnamed x36, local copies, waits for them, and re-layouts  3.05 us
  transfers between devices with their start and end apart: 16, of which 8 were waited for; matrix products, arithmetic and copies ran while one was open for 0% of the time, Pallas kernels for 1%

profile of v3, /device:TPU:24, one launch (start us, length us, event | category | flops | bytes accessed | tf_op | source)
XLA Modules:
  0.0 148.7 jit_solution(5201670050774832877)
XLA Ops:
  0.6 3.7 %shard_map.118 = (bf16[6144,128]{1,0:T(8,128)(2,1)}, bf16[1152,128]{1,0:T(8,128)(2,1)}) custom-call(bf16[16,1024]{1,0:T(8,128)(2,1)} %tokens.1, bf16[16,1024]{1,0:T(8,128)(2,1)} %cotangent.3, s32[8,16]{1,0:T(8,128)} %bitcast.21, bf16[8,16]{1,0:T(8,128)(2,1)} %bitcast.23, bf16[128,384]{1,0:T(8,128)(2,1)} %bitcast.18, bf16[128,384]{1,0:T(8,128)(2,1)} %bitcast.19, ...), custom_call_target="tpu_custom_call" | custom-call | tf_op jit(solution)/shard_map/pallas_call | solution.py:245
  4.3 24.2 %all-to-all-start = ((bf16[128,48,128]{2,1,0:T(8,128)(2,1)}), bf16[128,48,128]{2,1,0:T(8,128)(2,1)S(1)}, u32[]{:S(2)}, u32[]{:S(2)}) async-start(bf16[128,48,128]{2,1,0:T(8,128)(2,1)} %bitcast.17), calls=%async_computation | async-start | bytes 3145728 | tf_op jit(solution)/shard_map/all_to_all | solution.py:322
  28.5 0.0 copy-done.2
  28.5 2.5 %collective-permute-start = (bf16[1152,128]{1,0:T(8,128)(2,1)S(1)}, bf16[1152,128]{1,0:T(8,128)(2,1)S(1)}, u32[]{:S(2)}, u32[]{:S(2)}) collective-permute-start(bf16[1152,128]{1,0:T(8,128)(2,1)S(1)} %copy-done.2), channel_id=1, source_target_pairs={{0,128},{128,256},{256,384},{384,512},{512,640},{640,768},{768,896... | collective-permute-start | bytes 884744 | tf_op jit(solution)/shard_map/ppermute | solution.py:282
  31.0 4.6 %collective-permute-start.4 = (bf16[1152,128]{1,0:T(8,128)(2,1)S(1)}, bf16[1152,128]{1,0:T(8,128)(2,1)S(1)}, u32[]{:S(2)}, u32[]{:S(2)}) collective-permute-start(bf16[1152,128]{1,0:T(8,128)(2,1)S(1)} %copy-done.2), channel_id=1, source_target_pairs={{0,896},{128,0},{256,128},{384,256},{512,384},{640,512},{768,640},... | collective-permute-start | bytes 884744 | tf_op jit(solution)/shard_map/ppermute | solution.py:282
  35.6 5.1 %collective-permute-done.refs_1_ = bf16[1152,128]{1,0:T(8,128)(2,1)S(1)} collective-permute-done((bf16[1152,128]{1,0:T(8,128)(2,1)S(1)}, bf16[1152,128]{1,0:T(8,128)(2,1)S(1)}, u32[]{:S(2)}, u32[]{:S(2)}) %collective-permute-start) | collective-permute-done | bytes 294944 | tf_op jit(solution)/shard_map/ppermute | solution.py:282
  40.7 1.9 %collective-permute-start.1 = (bf16[1152,128]{1,0:T(8,128)(2,1)S(1)}, bf16[1152,128]{1,0:T(8,128)(2,1)S(1)}, u32[]{:S(2)}, u32[]{:S(2)}) collective-permute-start(bf16[1152,128]{1,0:T(8,128)(2,1)S(1)} %collective-permute-done.refs_1_), channel_id=1, source_target_pairs={{0,128},{128,256},{256,384},{384,512},{512,640},{640,768},{768,896... | collective-permute-start | bytes 884744 | tf_op jit(solution)/shard_map/ppermute | solution.py:282
  42.6 0.0 collective-permute-done.4.refs_5_
  42.6 0.0 copy-start.4
  42.6 5.1 %collective-permute-start.5 = (bf16[1152,128]{1,0:T(8,128)(2,1)S(1)}, bf16[1152,128]{1,0:T(8,128)(2,1)S(1)}, u32[]{:S(2)}, u32[]{:S(2)}) collective-permute-start(bf16[1152,128]{1,0:T(8,128)(2,1)S(1)} %collective-permute-done.4.refs_5_), channel_id=1, source_target_pairs={{0,896},{128,0},{256,128},{384,256},{512,384},{640,512},{768,640},... | collective-permute-start | bytes 884744 | tf_op jit(solution)/shard_map/ppermute | solution.py:282
  47.7 4.2 %collective-permute-done.1.refs_2_ = bf16[1152,128]{1,0:T(8,128)(2,1)S(1)} collective-permute-done((bf16[1152,128]{1,0:T(8,128)(2,1)S(1)}, bf16[1152,128]{1,0:T(8,128)(2,1)S(1)}, u32[]{:S(2)}, u32[]{:S(2)}) %collective-permute-start.1) | collective-permute-done | bytes 294944 | tf_op jit(solution)/shard_map/ppermute | solution.py:282
  51.9 1.9 %collective-permute-start.2 = (bf16[1152,128]{1,0:T(8,128)(2,1)S(1)}, bf16[1152,128]{1,0:T(8,128)(2,1)S(1)}, u32[]{:S(2)}, u32[]{:S(2)}) collective-permute-start(bf16[1152,128]{1,0:T(8,128)(2,1)S(1)} %collective-permute-done.1.refs_2_), channel_id=1, source_target_pairs={{0,128},{128,256},{256,384},{384,512},{512,640},{640,768},{768,896... | collective-permute-start | bytes 884744 | tf_op jit(solution)/shard_map/ppermute | solution.py:282
  53.8 0.0 collective-permute-done.5.refs_6_
  53.9 0.0 copy-start.6
  53.9 5.1 %collective-permute-start.6 = (bf16[1152,128]{1,0:T(8,128)(2,1)S(1)}, bf16[1152,128]{1,0:T(8,128)(2,1)S(1)}, u32[]{:S(2)}, u32[]{:S(2)}) collective-permute-start(bf16[1152,128]{1,0:T(8,128)(2,1)S(1)} %collective-permute-done.5.refs_6_), channel_id=1, source_target_pairs={{0,896},{128,0},{256,128},{384,256},{512,384},{640,512},{768,640},... | collective-permute-start | bytes 884744 | tf_op jit(solution)/shard_map/ppermute | solution.py:282
  59.0 3.3 %collective-permute-done.2.refs_3_ = bf16[1152,128]{1,0:T(8,128)(2,1)S(1)} collective-permute-done((bf16[1152,128]{1,0:T(8,128)(2,1)S(1)}, bf16[1152,128]{1,0:T(8,128)(2,1)S(1)}, u32[]{:S(2)}, u32[]{:S(2)}) %collective-permute-start.2) | collective-permute-done | bytes 294944 | tf_op jit(solution)/shard_map/ppermute | solution.py:282
  62.3 1.9 %collective-permute-start.3 = (bf16[1152,128]{1,0:T(8,128)(2,1)S(1)}, bf16[1152,128]{1,0:T(8,128)(2,1)}, u32[]{:S(2)}, u32[]{:S(2)}) collective-permute-start(bf16[1152,128]{1,0:T(8,128)(2,1)S(1)} %collective-permute-done.2.refs_3_), channel_id=1, source_target_pairs={{0,128},{128,256},{256,384},{384,512},{512,640},{640,768},{768,896... | collective-permute-start | bytes 884744 | tf_op jit(solution)/shard_map/ppermute | solution.py:282
  64.3 0.0 collective-permute-done.6.refs_7_
  64.3 0.0 copy-start.8
  64.3 8.0 %collective-permute-done.3.refs_4_ = bf16[1152,128]{1,0:T(8,128)(2,1)} collective-permute-done((bf16[1152,128]{1,0:T(8,128)(2,1)S(1)}, bf16[1152,128]{1,0:T(8,128)(2,1)}, u32[]{:S(2)}, u32[]{:S(2)}) %collective-permute-start.3) | collective-permute-done | bytes 294944 | tf_op jit(solution)/shard_map/ppermute | solution.py:282
  72.3 0.0 all-to-all-done
  72.3 0.0 copy-done.3
  72.3 0.0 copy-done.4
  72.3 0.0 copy-done.5
  72.3 0.0 copy-done.6
  72.3 0.0 copy-done.7
  72.3 0.0 copy-done.8
  72.3 1.1 copy-done.1
  73.4 9.6 %expert.1 = (bf16[6144,128]{1,0:T(8,128)(2,1)}, bf16[1152,128]{1,0:T(8,128)(2,1)}, bf16[1152,128]{1,0:T(8,128)(2,1)}, bf16[1152,128]{1,0:T(8,128)(2,1)}, bf16[11...) custom-call(s32[1]{0:T(128)} %bitcast.place, ...), custom_call_target="tpu_custom_call" | custom-call | tf_op jit(solution)/shard_map/expert/pallas_call | solution.py:258
  83.0 0.0 copy-start.17
  83.1 0.0 copy-start.16
  83.1 0.0 copy-start.13
  83.1 0.0 copy-start.12
  83.1 13.9 %all-to-all-start.1 = ((bf16[128,48,128]{2,1,0:T(8,128)(2,1)}), bf16[128,48,128]{2,1,0:T(8,128)(2,1)S(1)}, u32[]{:S(2)}, u32[]{:S(2)}) async-start(bf16[128,48,128]{2,1,0:T(8,128)(2,1)} %bitcast.16), calls=%async_computation.1 | async-start | bytes 3145728 | tf_op jit(solution)/shard_map/all_to_all | solution.py:322
  97.0 0.0 copy-start.11
  97.0 0.0 copy-start.10
  97.0 0.0 copy-done.17
  97.0 2.2 %collective-permute-start.7 = (bf16[1152,128]{1,0:T(8,128)(2,1)S(1)}, bf16[1152,128]{1,0:T(8,128)(2,1)S(1)}, u32[]{:S(2)}, u32[]{:S(2)}) collective-permute-start(bf16[1152,128]{1,0:T(8,128)(2,1)S(1)} %copy-done.17), channel_id=1, source_target_pairs={{0,128},{128,256},{256,384},{384,512},{512,640},{640,768},{768,896... | collective-permute-start | bytes 884744 | tf_op jit(solution)/shard_map/ppermute | solution.py:282
  99.3 5.0 %collective-permute-start.11 = (bf16[1152,128]{1,0:T(8,128)(2,1)S(1)}, bf16[1152,128]{1,0:T(8,128)(2,1)S(1)}, u32[]{:S(2)}, u32[]{:S(2)}) collective-permute-start(bf16[1152,128]{1,0:T(8,128)(2,1)S(1)} %copy-done.16), channel_id=1, source_target_pairs={{0,896},{128,0},{256,128},{384,256},{512,384},{640,512},{768,640},... | collective-permute-start | bytes 884744 | tf_op jit(solution)/shard_map/ppermute | solution.py:282
  104.2 5.1 %collective-permute-done.7 = bf16[1152,128]{1,0:T(8,128)(2,1)S(1)} collective-permute-done((bf16[1152,128]{1,0:T(8,128)(2,1)S(1)}, bf16[1152,128]{1,0:T(8,128)(2,1)S(1)}, u32[]{:S(2)}, u32[]{:S(2)}) %collective-permute-start.7) | collective-permute-done | bytes 294944 | tf_op jit(solution)/shard_map/ppermute | solution.py:282
  109.3 0.1 add.15
  109.4 1.9 %collective-permute-start.8 = (bf16[1152,128]{1,0:T(8,128)(2,1)S(1)}, bf16[1152,128]{1,0:T(8,128)(2,1)S(1)}, u32[]{:S(2)}, u32[]{:S(2)}) collective-permute-start(bf16[1152,128]{1,0:T(8,128)(2,1)S(1)} %add.15), channel_id=1, source_target_pairs={{0,128},{128,256},{256,384},{384,512},{512,640},{640,768},{768,896... | collective-permute-start | bytes 884744 | tf_op jit(solution)/shard_map/ppermute | solution.py:282
  111.3 0.0 collective-permute-done.11
  111.3 0.0 copy-done.12
  111.3 0.1 add.18
  111.4 5.1 %collective-permute-start.12 = (bf16[1152,128]{1,0:T(8,128)(2,1)S(1)}, bf16[1152,128]{1,0:T(8,128)(2,1)S(1)}, u32[]{:S(2)}, u32[]{:S(2)}) collective-permute-start(bf16[1152,128]{1,0:T(8,128)(2,1)S(1)} %add.18), channel_id=1, source_target_pairs={{0,896},{128,0},{256,128},{384,256},{512,384},{640,512},{768,640},... | collective-permute-start | bytes 884744 | tf_op jit(solution)/shard_map/ppermute | solution.py:282
  116.5 4.1 %collective-permute-done.8 = bf16[1152,128]{1,0:T(8,128)(2,1)S(1)} collective-permute-done((bf16[1152,128]{1,0:T(8,128)(2,1)S(1)}, bf16[1152,128]{1,0:T(8,128)(2,1)S(1)}, u32[]{:S(2)}, u32[]{:S(2)}) %collective-permute-start.8) | collective-permute-done | bytes 294944 | tf_op jit(solution)/shard_map/ppermute | solution.py:282
  120.6 0.0 copy-done.11
  120.6 0.1 add.16
  120.7 1.9 %collective-permute-start.9 = (bf16[1152,128]{1,0:T(8,128)(2,1)S(1)}, bf16[1152,128]{1,0:T(8,128)(2,1)S(1)}, u32[]{:S(2)}, u32[]{:S(2)}) collective-permute-start(bf16[1152,128]{1,0:T(8,128)(2,1)S(1)} %add.16), channel_id=1, source_target_pairs={{0,128},{128,256},{256,384},{384,512},{512,640},{640,768},{768,896... | collective-permute-start | bytes 884744 | tf_op jit(solution)/shard_map/ppermute | solution.py:282
  122.7 0.0 collective-permute-done.12
  122.7 0.1 add.19
  122.8 5.1 %collective-permute-start.13 = (bf16[1152,128]{1,0:T(8,128)(2,1)S(1)}, bf16[1152,128]{1,0:T(8,128)(2,1)S(1)}, u32[]{:S(2)}, u32[]{:S(2)}) collective-permute-start(bf16[1152,128]{1,0:T(8,128)(2,1)S(1)} %add.19), channel_id=1, source_target_pairs={{0,896},{128,0},{256,128},{384,256},{512,384},{640,512},{768,640},... | collective-permute-start | bytes 884744 | tf_op jit(solution)/shard_map/ppermute | solution.py:282
  127.9 3.2 %collective-permute-done.9 = bf16[1152,128]{1,0:T(8,128)(2,1)S(1)} collective-permute-done((bf16[1152,128]{1,0:T(8,128)(2,1)S(1)}, bf16[1152,128]{1,0:T(8,128)(2,1)S(1)}, u32[]{:S(2)}, u32[]{:S(2)}) %collective-permute-start.9) | collective-permute-done | bytes 294944 | tf_op jit(solution)/shard_map/ppermute | solution.py:282
  131.2 0.1 add.17
  131.2 1.9 %collective-permute-start.10 = (bf16[1152,128]{1,0:T(8,128)(2,1)S(1)}, bf16[1152,128]{1,0:T(8,128)(2,1)S(1)}, u32[]{:S(2)}, u32[]{:S(2)}) collective-permute-start(bf16[1152,128]{1,0:T(8,128)(2,1)S(1)} %add.17), channel_id=1, source_target_pairs={{0,128},{128,256},{256,384},{384,512},{512,640},{640,768},{768,896... | collective-permute-start | bytes 884744 | tf_op jit(solution)/shard_map/ppermute | solution.py:282
  133.2 0.0 collective-permute-done.13.left
  133.2 0.0 copy-start.14
  133.2 7.9 %collective-permute-done.10.right = bf16[1152,128]{1,0:T(8,128)(2,1)S(1)} collective-permute-done((bf16[1152,128]{1,0:T(8,128)(2,1)S(1)}, bf16[1152,128]{1,0:T(8,128)(2,1)S(1)}, u32[]{:S(2)}, u32[]{:S(2)}) %collective-permute-start.10) | collective-permute-done | bytes 294944 | tf_op jit(solution)/shard_map/ppermute | solution.py:282
  141.1 0.7 copy-done.15
  141.8 1.9 %shard_map.120 = (bf16[128,384]{1,0:T(8,128)(2,1)}, bf16[128,384]{1,0:T(8,128)(2,1)}, bf16[384,128]{1,0:T(8,128)(2,1)}) custom-call(bf16[1152,128]{1,0:T(8,128)(2,1)} %get-tuple-element.29.own, bf16[1152,128]{1,0:T(8,128)(2,1)} %copy-done.15, bf16[1152,128]{1,0:T(8,128)(2,1)} %copy-done.14), custom_call_target="tpu_custom_call" | custom-call | tf_op jit(solution)/shard_map/pallas_call | solution.py:314
  143.7 0.0 all-to-all-done.1
  143.7 1.2 copy-done
  144.9 3.8 %shard_map.119 = (bf16[16,1024]{1,0:T(8,128)(2,1)}, bf16[16,1024]{1,0:T(8,128)(2,1)}, bf16[8,16]{1,0:T(8,128)(2,1)}) custom-call(bf16[6144,128]{1,0:T(8,128)(2,1)} %bitcast.14, bf16[16,1024]{1,0:T(8,128)(2,1)} %cotangent.3, s32[8,16]{1,0:T(8,128)} %bitcast.22, bf16[8,16]{1,0:T(8,128)(2,1)} %bitcast.24), custom_call_target="tpu_custom_call" | custom-call | tf_op jit(solution)/shard_map/pallas_call | solution.py:305
  (13 shorter events, 0.0 us)
Async XLA Ops:
  4.3 24.2 %copy-start.2 = (bf16[1152,128]{1,0:T(8,128)(2,1)S(1)}, bf16[1152,128]{1,0:T(8,128)(2,1)}, u32[]{:S(2)}) copy-start(bf16[1152,128]{1,0:T(8,128)(2,1)} %get-tuple-element.24.refs_0_) | copy-start | bytes 884740
  4.3 68.0 %all-to-all-start = ((bf16[128,48,128]{2,1,0:T(8,128)(2,1)}), bf16[128,48,128]{2,1,0:T(8,128)(2,1)S(1)}, u32[]{:S(2)}, u32[]{:S(2)}) async-start(bf16[128,48,128]{2,1,0:T(8,128)(2,1)} %bitcast.17), calls=%async_computation | async-start | bytes 3145728 | tf_op jit(solution)/shard_map/all_to_all | solution.py:322
  28.5 12.1 %collective-permute-start = (bf16[1152,128]{1,0:T(8,128)(2,1)S(1)}, bf16[1152,128]{1,0:T(8,128)(2,1)S(1)}, u32[]{:S(2)}, u32[]{:S(2)}) collective-permute-start(bf16[1152,128]{1,0:T(8,128)(2,1)S(1)} %copy-done.2), channel_id=1, source_target_pairs={{0,128},{128,256},{256,384},{384,512},{512,640},{640,768},{768,896... | collective-permute-start | bytes 884744 | tf_op jit(solution)/shard_map/ppermute | solution.py:282
  31.0 11.5 %collective-permute-start.4 = (bf16[1152,128]{1,0:T(8,128)(2,1)S(1)}, bf16[1152,128]{1,0:T(8,128)(2,1)S(1)}, u32[]{:S(2)}, u32[]{:S(2)}) collective-permute-start(bf16[1152,128]{1,0:T(8,128)(2,1)S(1)} %copy-done.2), channel_id=1, source_target_pairs={{0,896},{128,0},{256,128},{384,256},{512,384},{640,512},{768,640},... | collective-permute-start | bytes 884744 | tf_op jit(solution)/shard_map/ppermute | solution.py:282
  40.7 31.6 %copy-start.3 = (bf16[1152,128]{1,0:T(8,128)(2,1)}, bf16[1152,128]{1,0:T(8,128)(2,1)S(1)}, u32[]{:S(2)}) copy-start(bf16[1152,128]{1,0:T(8,128)(2,1)S(1)} %collective-permute-done.refs_1_) | copy-start | bytes 884740
  40.7 11.3 %collective-permute-start.1 = (bf16[1152,128]{1,0:T(8,128)(2,1)S(1)}, bf16[1152,128]{1,0:T(8,128)(2,1)S(1)}, u32[]{:S(2)}, u32[]{:S(2)}) collective-permute-start(bf16[1152,128]{1,0:T(8,128)(2,1)S(1)} %collective-permute-done.refs_1_), channel_id=1, source_target_pairs={{0,128},{128,256},{256,384},{384,512},{512,640},{640,768},{768,896... | collective-permute-start | bytes 884744 | tf_op jit(solution)/shard_map/ppermute | solution.py:282
  42.6 29.7 %copy-start.4 = (bf16[1152,128]{1,0:T(8,128)(2,1)}, bf16[1152,128]{1,0:T(8,128)(2,1)S(1)}, u32[]{:S(2)}) copy-start(bf16[1152,128]{1,0:T(8,128)(2,1)S(1)} %collective-permute-done.4.refs_5_) | copy-start | bytes 884740
  42.6 11.2 %collective-permute-start.5 = (bf16[1152,128]{1,0:T(8,128)(2,1)S(1)}, bf16[1152,128]{1,0:T(8,128)(2,1)S(1)}, u32[]{:S(2)}, u32[]{:S(2)}) collective-permute-start(bf16[1152,128]{1,0:T(8,128)(2,1)S(1)} %collective-permute-done.4.refs_5_), channel_id=1, source_target_pairs={{0,896},{128,0},{256,128},{384,256},{512,384},{640,512},{768,640},... | collective-permute-start | bytes 884744 | tf_op jit(solution)/shard_map/ppermute | solution.py:282
  51.9 20.4 %copy-start.5 = (bf16[1152,128]{1,0:T(8,128)(2,1)}, bf16[1152,128]{1,0:T(8,128)(2,1)S(1)}, u32[]{:S(2)}) copy-start(bf16[1152,128]{1,0:T(8,128)(2,1)S(1)} %collective-permute-done.1.refs_2_) | copy-start | bytes 884740
  51.9 10.4 %collective-permute-start.2 = (bf16[1152,128]{1,0:T(8,128)(2,1)S(1)}, bf16[1152,128]{1,0:T(8,128)(2,1)S(1)}, u32[]{:S(2)}, u32[]{:S(2)}) collective-permute-start(bf16[1152,128]{1,0:T(8,128)(2,1)S(1)} %collective-permute-done.1.refs_2_), channel_id=1, source_target_pairs={{0,128},{128,256},{256,384},{384,512},{512,640},{640,768},{768,896... | collective-permute-start | bytes 884744 | tf_op jit(solution)/shard_map/ppermute | solution.py:282
  53.9 18.4 %copy-start.6 = (bf16[1152,128]{1,0:T(8,128)(2,1)}, bf16[1152,128]{1,0:T(8,128)(2,1)S(1)}, u32[]{:S(2)}) copy-start(bf16[1152,128]{1,0:T(8,128)(2,1)S(1)} %collective-permute-done.5.refs_6_) | copy-start | bytes 884740
  53.9 10.4 %collective-permute-start.6 = (bf16[1152,128]{1,0:T(8,128)(2,1)S(1)}, bf16[1152,128]{1,0:T(8,128)(2,1)S(1)}, u32[]{:S(2)}, u32[]{:S(2)}) collective-permute-start(bf16[1152,128]{1,0:T(8,128)(2,1)S(1)} %collective-permute-done.5.refs_6_), channel_id=1, source_target_pairs={{0,896},{128,0},{256,128},{384,256},{512,384},{640,512},{768,640},... | collective-permute-start | bytes 884744 | tf_op jit(solution)/shard_map/ppermute | solution.py:282
  62.3 10.0 %copy-start.7 = (bf16[1152,128]{1,0:T(8,128)(2,1)}, bf16[1152,128]{1,0:T(8,128)(2,1)S(1)}, u32[]{:S(2)}) copy-start(bf16[1152,128]{1,0:T(8,128)(2,1)S(1)} %collective-permute-done.2.refs_3_) | copy-start | bytes 884740
  62.3 9.9 %collective-permute-start.3 = (bf16[1152,128]{1,0:T(8,128)(2,1)S(1)}, bf16[1152,128]{1,0:T(8,128)(2,1)}, u32[]{:S(2)}, u32[]{:S(2)}) collective-permute-start(bf16[1152,128]{1,0:T(8,128)(2,1)S(1)} %collective-permute-done.2.refs_3_), channel_id=1, source_target_pairs={{0,128},{128,256},{256,384},{384,512},{512,640},{640,768},{768,896... | collective-permute-start | bytes 884744 | tf_op jit(solution)/shard_map/ppermute | solution.py:282
  64.3 8.0 %copy-start.8 = (bf16[1152,128]{1,0:T(8,128)(2,1)}, bf16[1152,128]{1,0:T(8,128)(2,1)S(1)}, u32[]{:S(2)}) copy-start(bf16[1152,128]{1,0:T(8,128)(2,1)S(1)} %collective-permute-done.6.refs_7_) | copy-start | bytes 884740
  72.3 1.1 copy-start.1
  83.0 14.0 %copy-start.17 = (bf16[1152,128]{1,0:T(8,128)(2,1)S(1)}, bf16[1152,128]{1,0:T(8,128)(2,1)}, u32[]{:S(2)}) copy-start(bf16[1152,128]{1,0:T(8,128)(2,1)} %get-tuple-element.33) | copy-start | bytes 884740
  83.1 16.2 %copy-start.16 = (bf16[1152,128]{1,0:T(8,128)(2,1)S(1)}, bf16[1152,128]{1,0:T(8,128)(2,1)}, u32[]{:S(2)}) copy-start(bf16[1152,128]{1,0:T(8,128)(2,1)} %get-tuple-element.36) | copy-start | bytes 884740
  83.1 26.2 %copy-start.13 = (bf16[1152,128]{1,0:T(8,128)(2,1)S(1)}, bf16[1152,128]{1,0:T(8,128)(2,1)}, u32[]{:S(2)}) copy-start(bf16[1152,128]{1,0:T(8,128)(2,1)} %get-tuple-element.32) | copy-start | bytes 884740
  83.1 28.2 %copy-start.12 = (bf16[1152,128]{1,0:T(8,128)(2,1)S(1)}, bf16[1152,128]{1,0:T(8,128)(2,1)}, u32[]{:S(2)}) copy-start(bf16[1152,128]{1,0:T(8,128)(2,1)} %get-tuple-element.35) | copy-start | bytes 884740
  83.1 60.6 %all-to-all-start.1 = ((bf16[128,48,128]{2,1,0:T(8,128)(2,1)}), bf16[128,48,128]{2,1,0:T(8,128)(2,1)S(1)}, u32[]{:S(2)}, u32[]{:S(2)}) async-start(bf16[128,48,128]{2,1,0:T(8,128)(2,1)} %bitcast.16), calls=%async_computation.1 | async-start | bytes 3145728 | tf_op jit(solution)/shard_map/all_to_all | solution.py:322
  97.0 23.7 %copy-start.11 = (bf16[1152,128]{1,0:T(8,128)(2,1)S(1)}, bf16[1152,128]{1,0:T(8,128)(2,1)}, u32[]{:S(2)}) copy-start(bf16[1152,128]{1,0:T(8,128)(2,1)} %get-tuple-element.31) | copy-start | bytes 884740
  97.0 25.7 %copy-start.10 = (bf16[1152,128]{1,0:T(8,128)(2,1)S(1)}, bf16[1152,128]{1,0:T(8,128)(2,1)}, u32[]{:S(2)}) copy-start(bf16[1152,128]{1,0:T(8,128)(2,1)} %get-tuple-element.34) | copy-start | bytes 884740
  97.0 12.3 %collective-permute-start.7 = (bf16[1152,128]{1,0:T(8,128)(2,1)S(1)}, bf16[1152,128]{1,0:T(8,128)(2,1)S(1)}, u32[]{:S(2)}, u32[]{:S(2)}) collective-permute-start(bf16[1152,128]{1,0:T(8,128)(2,1)S(1)} %copy-done.17), channel_id=1, source_target_pairs={{0,128},{128,256},{256,384},{384,512},{512,640},{640,768},{768,896... | collective-permute-start | bytes 884744 | tf_op jit(solution)/shard_map/ppermute | solution.py:282
  99.3 12.0 %collective-permute-start.11 = (bf16[1152,128]{1,0:T(8,128)(2,1)S(1)}, bf16[1152,128]{1,0:T(8,128)(2,1)S(1)}, u32[]{:S(2)}, u32[]{:S(2)}) collective-permute-start(bf16[1152,128]{1,0:T(8,128)(2,1)S(1)} %copy-done.16), channel_id=1, source_target_pairs={{0,896},{128,0},{256,128},{384,256},{512,384},{640,512},{768,640},... | collective-permute-start | bytes 884744 | tf_op jit(solution)/shard_map/ppermute | solution.py:282
  109.3 21.9 %copy-start.9 = (bf16[1152,128]{1,0:T(8,128)(2,1)S(1)}, bf16[1152,128]{1,0:T(8,128)(2,1)}, u32[]{:S(2)}) copy-start(bf16[1152,128]{1,0:T(8,128)(2,1)} %get-tuple-element.30) | copy-start | bytes 884740
  109.4 11.3 %collective-permute-start.8 = (bf16[1152,128]{1,0:T(8,128)(2,1)S(1)}, bf16[1152,128]{1,0:T(8,128)(2,1)S(1)}, u32[]{:S(2)}, u32[]{:S(2)}) collective-permute-start(bf16[1152,128]{1,0:T(8,128)(2,1)S(1)} %add.15), channel_id=1, source_target_pairs={{0,128},{128,256},{256,384},{384,512},{512,640},{640,768},{768,896... | collective-permute-start | bytes 884744 | tf_op jit(solution)/shard_map/ppermute | solution.py:282
  111.4 11.3 %collective-permute-start.12 = (bf16[1152,128]{1,0:T(8,128)(2,1)S(1)}, bf16[1152,128]{1,0:T(8,128)(2,1)S(1)}, u32[]{:S(2)}, u32[]{:S(2)}) collective-permute-start(bf16[1152,128]{1,0:T(8,128)(2,1)S(1)} %add.18), channel_id=1, source_target_pairs={{0,896},{128,0},{256,128},{384,256},{512,384},{640,512},{768,640},... | collective-permute-start | bytes 884744 | tf_op jit(solution)/shard_map/ppermute | solution.py:282
  120.7 10.4 %collective-permute-start.9 = (bf16[1152,128]{1,0:T(8,128)(2,1)S(1)}, bf16[1152,128]{1,0:T(8,128)(2,1)S(1)}, u32[]{:S(2)}, u32[]{:S(2)}) collective-permute-start(bf16[1152,128]{1,0:T(8,128)(2,1)S(1)} %add.16), channel_id=1, source_target_pairs={{0,128},{128,256},{256,384},{384,512},{512,640},{640,768},{768,896... | collective-permute-start | bytes 884744 | tf_op jit(solution)/shard_map/ppermute | solution.py:282
  122.8 10.4 %collective-permute-start.13 = (bf16[1152,128]{1,0:T(8,128)(2,1)S(1)}, bf16[1152,128]{1,0:T(8,128)(2,1)S(1)}, u32[]{:S(2)}, u32[]{:S(2)}) collective-permute-start(bf16[1152,128]{1,0:T(8,128)(2,1)S(1)} %add.19), channel_id=1, source_target_pairs={{0,896},{128,0},{256,128},{384,256},{512,384},{640,512},{768,640},... | collective-permute-start | bytes 884744 | tf_op jit(solution)/shard_map/ppermute | solution.py:282
  131.2 9.8 %collective-permute-start.10 = (bf16[1152,128]{1,0:T(8,128)(2,1)S(1)}, bf16[1152,128]{1,0:T(8,128)(2,1)S(1)}, u32[]{:S(2)}, u32[]{:S(2)}) collective-permute-start(bf16[1152,128]{1,0:T(8,128)(2,1)S(1)} %add.17), channel_id=1, source_target_pairs={{0,128},{128,256},{256,384},{384,512},{512,640},{640,768},{768,896... | collective-permute-start | bytes 884744 | tf_op jit(solution)/shard_map/ppermute | solution.py:282
  133.2 7.9 %copy-start.14 = (bf16[1152,128]{1,0:T(8,128)(2,1)}, bf16[1152,128]{1,0:T(8,128)(2,1)S(1)}, u32[]{:S(2)}) copy-start(bf16[1152,128]{1,0:T(8,128)(2,1)S(1)} %collective-permute-done.13.left) | copy-start | bytes 884740
  141.1 0.7 copy-start.15
  143.7 1.2 copy-start

commit v4 on v3

--- a/solution.py
+++ b/solution.py
@@ -217,9 +217,21 @@
     router_grads[...] = dot(routed.astype(BF16), eye, ((0,), (0,))).astype(BF16)
 
 
-def unpack_kernel(own, right, left, gate, up, down):
+def finish_kernel(back, own, right, left, cotangent, ids, weights, *refs):
+    layer, token_grads, router_grads, gate, up, down, lines, rows, sems = refs
+    copies = [
+        pltpu.make_async_copy(part, lines.at[i], sems.at[i])
+        for i, part in enumerate((own, right, left))
+    ]
+    for copy in copies:
+        copy.start()
+    combine_kernel(back, cotangent, ids, weights, layer, token_grads, router_grads, rows)
+    for copy in copies:
+        copy.wait()
     features, hidden = gate.shape
-    total = (own[...].astype(F32) + right[...].astype(F32) + left[...].astype(F32)).astype(BF16)
+    total = (
+        lines[0].astype(F32) + lines[1].astype(F32) + lines[2].astype(F32)
+    ).astype(BF16)
     for i, weight in enumerate((gate, up)):
         for c in range(hidden // LANES):
             at = i * hidden + c * LANES
@@ -301,21 +313,29 @@
     return terms[0], right, left
 
 
-def combine(back, cotangent, ids, weights):
+def finish(back, cotangent, ids, weights, parts, features, hidden):
+    anywhere = pl.BlockSpec(memory_space=pl.ANY)
     return call(
-        combine_kernel,
-        [cotangent.shape, cotangent.shape, ids.shape],
-        scratch=[pltpu.VMEM(back.shape, F32)],
-        in_specs=[vmem()] * 4,
-    )(back, cotangent, ids, weights)
-
-
-def unpack_grads(parts, features, hidden):
-    return call(
-        unpack_kernel,
-        [(features, hidden), (features, hidden), (hidden, LANES)],
-        in_specs=[vmem()] * 3,
-    )(*parts)
+        finish_kernel,
+        [
+            cotangent.shape,
+            cotangent.shape,
+            ids.shape,
+            (features, hidden),
+            (features, hidden),
+            (hidden, LANES),
+        ],
+        scratch=[
+            pltpu.VMEM((3,) + parts[0].shape, BF16),
+            pltpu.VMEM(back.shape, F32),
+            pltpu.SemaphoreType.DMA((3,)),
+        ],
+        in_specs=[vmem()] + [anywhere] * 3 + [vmem()] * 3,
+    )(back, *parts, cotangent, ids, weights)
+
+
+def on_chip(value):
+    return value if INTERPRET else pltpu.with_memory_space_constraint(value, pltpu.VMEM)
 
 
 def exchange(lines, peers):
@@ -340,11 +360,12 @@
     recv = exchange(sent, experts)
     pieces = gather_ring(packed)
     place = lax.axis_index("dp").astype(jnp.int32).reshape(1)
-    back, *terms = expert(place, recv, pieces, hidden, width)
+    back, *terms = expert(place, on_chip(recv), pieces, hidden, width)
     returned = exchange(back, experts)
     parts = scatter_ring(terms)
-    layer, token_grads, router_grads = combine(returned, cotangent, ids, weights)
-    gate, up, down = unpack_grads(parts, features, hidden)
+    layer, token_grads, router_grads, gate, up, down = finish(
+        on_chip(returned), cotangent, ids, weights, parts, features, hidden
+    )
     return layer, token_grads, router_grads.T, gate[None], up[None], down[None]
 
 

time: 150 us -> 144 us (0.960)
  Pallas kernels: 19 us -> 15.7 us
  local copies, waits for them, and re-layouts: 3.05 us -> 0.76 us
    unnamed x36 -> x32, local copies, waits for them, and re-layouts: 3.05 us -> 0.76 us
    pallas_call x2 -> x1, Pallas kernels: 5.74 us -> 3.88 us  [finish(): call(finish_kernel, [cotangent.shape, cotangent.shape, ids.shape, (featur...]
  transfers between devices with their start and end apart: 16 -> 16, of which waited for: 8 -> 8; matrix products, arithmetic and copies ran while one was open for 0% -> 0% of each run, Pallas kernels for 1% -> 0%
where the time goes in v4:
time: 144 us; the launch traced here: 143 us
  starting transfers between devices  84.5 us (59%)
  waiting for transfers between devices  40.7 us (28%)
  Pallas kernels  15.7 us (11%)
    ppermute x14, starting transfers between devices, shifted(): lax.ppermute(value, 'dp', [(i, (i + by) % peers) for i in range(peers)])  46.4 us
    ppermute x14, waiting for transfers between devices, shifted(): lax.ppermute(value, 'dp', [(i, (i + by) % peers) for i in range(peers)])  40.7 us
    all_to_all x2, starting transfers between devices, exchange(): lax.all_to_all(lines.reshape(peers, -1, LANES), ('group', 'local'), split...  38.1 us
    pallas_call x1, Pallas kernels, expert(): pl.pallas_call(expert_kernel, out_shape=[jax.ShapeDtypeStruct(recv.shape,...  8.21 us
    pallas_call x1, Pallas kernels, finish(): call(finish_kernel, [cotangent.shape, cotangent.shape, ids.shape, (featur...  3.88 us
    pallas_call x1, Pallas kernels, prepare(): call(prepare_kernel, [(lines, LANES), (3 * gate.shape[1], LANES)], scratc...  3.63 us
  transfers between devices with their start and end apart: 16, of which 8 were waited for; matrix products, arithmetic and copies ran while one was open for 0% of the time, Pallas kernels for 0%

profile of v4, /device:TPU:24, one launch (start us, length us, event | category | flops | bytes accessed | tf_op | source)
XLA Modules:
  0.0 143.3 jit_solution(5475922284466935871)
XLA Ops:
  0.6 3.6 %shard_map.118 = (bf16[6144,128]{1,0:T(8,128)(2,1)}, bf16[1152,128]{1,0:T(8,128)(2,1)}) custom-call(bf16[16,1024]{1,0:T(8,128)(2,1)} %tokens.1, bf16[16,1024]{1,0:T(8,128)(2,1)} %cotangent.3, s32[8,16]{1,0:T(8,128)} %bitcast.21, bf16[8,16]{1,0:T(8,128)(2,1)} %bitcast.23, bf16[128,384]{1,0:T(8,128)(2,1)} %bitcast.18, bf16[128,384]{1,0:T(8,128)(2,1)} %bitcast.19, ...), custom_call_target="tpu_custom_call" | custom-call | tf_op jit(solution)/shard_map/pallas_call | solution.py:257
  4.3 24.2 %all-to-all-start = ((bf16[128,48,128]{2,1,0:T(8,128)(2,1)}), bf16[128,48,128]{2,1,0:T(8,128)(2,1)S(1)}, u32[]{:S(2)}, u32[]{:S(2)}) async-start(bf16[128,48,128]{2,1,0:T(8,128)(2,1)} %bitcast.17), calls=%async_computation | async-start | bytes 3145728 | tf_op jit(solution)/shard_map/all_to_all | solution.py:342
  28.5 0.0 copy-done
  28.5 2.5 %collective-permute-start = (bf16[1152,128]{1,0:T(8,128)(2,1)S(1)}, bf16[1152,128]{1,0:T(8,128)(2,1)S(1)}, u32[]{:S(2)}, u32[]{:S(2)}) collective-permute-start(bf16[1152,128]{1,0:T(8,128)(2,1)S(1)} %copy-done), channel_id=1, source_target_pairs={{0,128},{128,256},{256,384},{384,512},{512,640},{640,768},{768,896... | collective-permute-start | bytes 884744 | tf_op jit(solution)/shard_map/ppermute | solution.py:294
  31.0 4.6 %collective-permute-start.4 = (bf16[1152,128]{1,0:T(8,128)(2,1)S(1)}, bf16[1152,128]{1,0:T(8,128)(2,1)S(1)}, u32[]{:S(2)}, u32[]{:S(2)}) collective-permute-start(bf16[1152,128]{1,0:T(8,128)(2,1)S(1)} %copy-done), channel_id=1, source_target_pairs={{0,896},{128,0},{256,128},{384,256},{512,384},{640,512},{768,640},... | collective-permute-start | bytes 884744 | tf_op jit(solution)/shard_map/ppermute | solution.py:294
  35.6 5.1 %collective-permute-done.refs_1_ = bf16[1152,128]{1,0:T(8,128)(2,1)S(1)} collective-permute-done((bf16[1152,128]{1,0:T(8,128)(2,1)S(1)}, bf16[1152,128]{1,0:T(8,128)(2,1)S(1)}, u32[]{:S(2)}, u32[]{:S(2)}) %collective-permute-start) | collective-permute-done | bytes 294944 | tf_op jit(solution)/shard_map/ppermute | solution.py:294
  40.6 1.9 %collective-permute-start.1 = (bf16[1152,128]{1,0:T(8,128)(2,1)S(1)}, bf16[1152,128]{1,0:T(8,128)(2,1)S(1)}, u32[]{:S(2)}, u32[]{:S(2)}) collective-permute-start(bf16[1152,128]{1,0:T(8,128)(2,1)S(1)} %collective-permute-done.refs_1_), channel_id=1, source_target_pairs={{0,128},{128,256},{256,384},{384,512},{512,640},{640,768},{768,896... | collective-permute-start | bytes 884744 | tf_op jit(solution)/shard_map/ppermute | solution.py:294
  42.6 0.0 collective-permute-done.4.refs_5_
  42.6 0.0 copy-start.2
  42.6 5.1 %collective-permute-start.5 = (bf16[1152,128]{1,0:T(8,128)(2,1)S(1)}, bf16[1152,128]{1,0:T(8,128)(2,1)S(1)}, u32[]{:S(2)}, u32[]{:S(2)}) collective-permute-start(bf16[1152,128]{1,0:T(8,128)(2,1)S(1)} %collective-permute-done.4.refs_5_), channel_id=1, source_target_pairs={{0,896},{128,0},{256,128},{384,256},{512,384},{640,512},{768,640},... | collective-permute-start | bytes 884744 | tf_op jit(solution)/shard_map/ppermute | solution.py:294
  47.7 4.2 %collective-permute-done.1.refs_2_ = bf16[1152,128]{1,0:T(8,128)(2,1)S(1)} collective-permute-done((bf16[1152,128]{1,0:T(8,128)(2,1)S(1)}, bf16[1152,128]{1,0:T(8,128)(2,1)S(1)}, u32[]{:S(2)}, u32[]{:S(2)}) %collective-permute-start.1) | collective-permute-done | bytes 294944 | tf_op jit(solution)/shard_map/ppermute | solution.py:294
  51.9 1.9 %collective-permute-start.2 = (bf16[1152,128]{1,0:T(8,128)(2,1)S(1)}, bf16[1152,128]{1,0:T(8,128)(2,1)S(1)}, u32[]{:S(2)}, u32[]{:S(2)}) collective-permute-start(bf16[1152,128]{1,0:T(8,128)(2,1)S(1)} %collective-permute-done.1.refs_2_), channel_id=1, source_target_pairs={{0,128},{128,256},{256,384},{384,512},{512,640},{640,768},{768,896... | collective-permute-start | bytes 884744 | tf_op jit(solution)/shard_map/ppermute | solution.py:294
  53.8 0.0 collective-permute-done.5.refs_6_
  53.8 0.0 copy-start.4
  53.8 5.1 %collective-permute-start.6 = (bf16[1152,128]{1,0:T(8,128)(2,1)S(1)}, bf16[1152,128]{1,0:T(8,128)(2,1)S(1)}, u32[]{:S(2)}, u32[]{:S(2)}) collective-permute-start(bf16[1152,128]{1,0:T(8,128)(2,1)S(1)} %collective-permute-done.5.refs_6_), channel_id=1, source_target_pairs={{0,896},{128,0},{256,128},{384,256},{512,384},{640,512},{768,640},... | collective-permute-start | bytes 884744 | tf_op jit(solution)/shard_map/ppermute | solution.py:294
  59.0 3.3 %collective-permute-done.2.refs_3_ = bf16[1152,128]{1,0:T(8,128)(2,1)S(1)} collective-permute-done((bf16[1152,128]{1,0:T(8,128)(2,1)S(1)}, bf16[1152,128]{1,0:T(8,128)(2,1)S(1)}, u32[]{:S(2)}, u32[]{:S(2)}) %collective-permute-start.2) | collective-permute-done | bytes 294944 | tf_op jit(solution)/shard_map/ppermute | solution.py:294
  62.3 1.9 %collective-permute-start.3 = (bf16[1152,128]{1,0:T(8,128)(2,1)S(1)}, bf16[1152,128]{1,0:T(8,128)(2,1)}, u32[]{:S(2)}, u32[]{:S(2)}) collective-permute-start(bf16[1152,128]{1,0:T(8,128)(2,1)S(1)} %collective-permute-done.2.refs_3_), channel_id=1, source_target_pairs={{0,128},{128,256},{256,384},{384,512},{512,640},{640,768},{768,896... | collective-permute-start | bytes 884744 | tf_op jit(solution)/shard_map/ppermute | solution.py:294
  64.2 0.0 collective-permute-done.6.refs_7_
  64.2 0.0 copy-start.6
  64.3 8.0 %collective-permute-done.3.refs_4_ = bf16[1152,128]{1,0:T(8,128)(2,1)} collective-permute-done((bf16[1152,128]{1,0:T(8,128)(2,1)S(1)}, bf16[1152,128]{1,0:T(8,128)(2,1)}, u32[]{:S(2)}, u32[]{:S(2)}) %collective-permute-start.3) | collective-permute-done | bytes 294944 | tf_op jit(solution)/shard_map/ppermute | solution.py:294
  72.2 0.0 all-to-all-done
  72.2 0.0 copy-done.1
  72.2 0.0 copy-done.2
  72.2 0.0 copy-done.3
  72.3 0.0 copy-done.4
  72.3 0.0 copy-done.5
  72.3 0.0 copy-done.6
  72.3 8.2 %expert.1 = (bf16[6144,128]{1,0:T(8,128)(2,1)}, bf16[1152,128]{1,0:T(8,128)(2,1)}, bf16[1152,128]{1,0:T(8,128)(2,1)}, bf16[1152,128]{1,0:T(8,128)(2,1)}, bf16[11...) custom-call(s32[1]{0:T(128)} %bitcast.place, ...), custom_call_target="tpu_custom_call" | custom-call | tf_op jit(solution)/shard_map/expert/pallas_call | solution.py:270
  80.5 0.0 copy-start.15
  80.5 0.0 copy-start.14
  80.5 0.0 copy-start.11
  80.5 0.0 copy-start.10
  80.5 13.9 %all-to-all-start.1 = ((bf16[128,48,128]{2,1,0:T(8,128)(2,1)}), bf16[128,48,128]{2,1,0:T(8,128)(2,1)S(1)}, u32[]{:S(2)}, u32[]{:S(2)}) async-start(bf16[128,48,128]{2,1,0:T(8,128)(2,1)} %bitcast.16), calls=%async_computation.1 | async-start | bytes 3145728 | tf_op jit(solution)/shard_map/all_to_all | solution.py:342
  94.4 0.0 copy-start.9
  94.5 0.0 copy-start.8
  94.5 0.0 copy-done.15
  94.5 2.2 %collective-permute-start.7 = (bf16[1152,128]{1,0:T(8,128)(2,1)S(1)}, bf16[1152,128]{1,0:T(8,128)(2,1)S(1)}, u32[]{:S(2)}, u32[]{:S(2)}) collective-permute-start(bf16[1152,128]{1,0:T(8,128)(2,1)S(1)} %copy-done.15), channel_id=1, source_target_pairs={{0,128},{128,256},{256,384},{384,512},{512,640},{640,768},{768,896... | collective-permute-start | bytes 884744 | tf_op jit(solution)/shard_map/ppermute | solution.py:294
  96.7 0.0 copy-done.14
  96.7 5.1 %collective-permute-start.11 = (bf16[1152,128]{1,0:T(8,128)(2,1)S(1)}, bf16[1152,128]{1,0:T(8,128)(2,1)S(1)}, u32[]{:S(2)}, u32[]{:S(2)}) collective-permute-start(bf16[1152,128]{1,0:T(8,128)(2,1)S(1)} %copy-done.14), channel_id=1, source_target_pairs={{0,896},{128,0},{256,128},{384,256},{512,384},{640,512},{768,640},... | collective-permute-start | bytes 884744 | tf_op jit(solution)/shard_map/ppermute | solution.py:294
  101.9 4.9 %collective-permute-done.7 = bf16[1152,128]{1,0:T(8,128)(2,1)S(1)} collective-permute-done((bf16[1152,128]{1,0:T(8,128)(2,1)S(1)}, bf16[1152,128]{1,0:T(8,128)(2,1)S(1)}, u32[]{:S(2)}, u32[]{:S(2)}) %collective-permute-start.7) | collective-permute-done | bytes 294944 | tf_op jit(solution)/shard_map/ppermute | solution.py:294
  106.7 0.0 copy-done.11
  106.7 0.1 add.15
  106.8 1.9 %collective-permute-start.8 = (bf16[1152,128]{1,0:T(8,128)(2,1)S(1)}, bf16[1152,128]{1,0:T(8,128)(2,1)S(1)}, u32[]{:S(2)}, u32[]{:S(2)}) collective-permute-start(bf16[1152,128]{1,0:T(8,128)(2,1)S(1)} %add.15), channel_id=1, source_target_pairs={{0,128},{128,256},{256,384},{384,512},{512,640},{640,768},{768,896... | collective-permute-start | bytes 884744 | tf_op jit(solution)/shard_map/ppermute | solution.py:294
  108.8 0.0 collective-permute-done.11
  108.8 0.0 copy-done.10
  108.8 0.1 add.18
  108.9 5.1 %collective-permute-start.12 = (bf16[1152,128]{1,0:T(8,128)(2,1)S(1)}, bf16[1152,128]{1,0:T(8,128)(2,1)S(1)}, u32[]{:S(2)}, u32[]{:S(2)}) collective-permute-start(bf16[1152,128]{1,0:T(8,128)(2,1)S(1)} %add.18), channel_id=1, source_target_pairs={{0,896},{128,0},{256,128},{384,256},{512,384},{640,512},{768,640},... | collective-permute-start | bytes 884744 | tf_op jit(solution)/shard_map/ppermute | solution.py:294
  114.0 4.1 %collective-permute-done.8 = bf16[1152,128]{1,0:T(8,128)(2,1)S(1)} collective-permute-done((bf16[1152,128]{1,0:T(8,128)(2,1)S(1)}, bf16[1152,128]{1,0:T(8,128)(2,1)S(1)}, u32[]{:S(2)}, u32[]{:S(2)}) %collective-permute-start.8) | collective-permute-done | bytes 294944 | tf_op jit(solution)/shard_map/ppermute | solution.py:294
  118.1 0.0 copy-done.9
  118.1 0.1 add.16
  118.2 1.9 %collective-permute-start.9 = (bf16[1152,128]{1,0:T(8,128)(2,1)S(1)}, bf16[1152,128]{1,0:T(8,128)(2,1)S(1)}, u32[]{:S(2)}, u32[]{:S(2)}) collective-permute-start(bf16[1152,128]{1,0:T(8,128)(2,1)S(1)} %add.16), channel_id=1, source_target_pairs={{0,128},{128,256},{256,384},{384,512},{512,640},{640,768},{768,896... | collective-permute-start | bytes 884744 | tf_op jit(solution)/shard_map/ppermute | solution.py:294
  120.1 0.0 collective-permute-done.12
  120.1 0.0 copy-done.8
  120.1 0.1 add.19
  120.2 5.1 %collective-permute-start.13 = (bf16[1152,128]{1,0:T(8,128)(2,1)S(1)}, bf16[1152,128]{1,0:T(8,128)(2,1)S(1)}, u32[]{:S(2)}, u32[]{:S(2)}) collective-permute-start(bf16[1152,128]{1,0:T(8,128)(2,1)S(1)} %add.19), channel_id=1, source_target_pairs={{0,896},{128,0},{256,128},{384,256},{512,384},{640,512},{768,640},... | collective-permute-start | bytes 884744 | tf_op jit(solution)/shard_map/ppermute | solution.py:294
  125.4 3.2 %collective-permute-done.9 = bf16[1152,128]{1,0:T(8,128)(2,1)S(1)} collective-permute-done((bf16[1152,128]{1,0:T(8,128)(2,1)S(1)}, bf16[1152,128]{1,0:T(8,128)(2,1)S(1)}, u32[]{:S(2)}, u32[]{:S(2)}) %collective-permute-start.9) | collective-permute-done | bytes 294944 | tf_op jit(solution)/shard_map/ppermute | solution.py:294
  128.6 0.1 add.17
  128.7 1.9 %collective-permute-start.10 = (bf16[1152,128]{1,0:T(8,128)(2,1)S(1)}, bf16[1152,128]{1,0:T(8,128)(2,1)S(1)}, u32[]{:S(2)}, u32[]{:S(2)}) collective-permute-start(bf16[1152,128]{1,0:T(8,128)(2,1)S(1)} %add.17), channel_id=1, source_target_pairs={{0,128},{128,256},{256,384},{384,512},{512,640},{640,768},{768,896... | collective-permute-start | bytes 884744 | tf_op jit(solution)/shard_map/ppermute | solution.py:294
  130.6 0.0 collective-permute-done.13.left
  130.7 7.9 %collective-permute-done.10.right = bf16[1152,128]{1,0:T(8,128)(2,1)S(1)} collective-permute-done((bf16[1152,128]{1,0:T(8,128)(2,1)S(1)}, bf16[1152,128]{1,0:T(8,128)(2,1)S(1)}, u32[]{:S(2)}, u32[]{:S(2)}) %collective-permute-start.10) | collective-permute-done | bytes 294944 | tf_op jit(solution)/shard_map/ppermute | solution.py:294
  138.5 0.0 all-to-all-done.1
  138.5 0.0 copy-done.12
  138.5 0.7 copy-done.13
  139.2 3.9 %shard_map.119 = (bf16[16,1024]{1,0:T(8,128)(2,1)}, bf16[16,1024]{1,0:T(8,128)(2,1)}, bf16[8,16]{1,0:T(8,128)(2,1)}, bf16[128,384]{1,0:T(8,128)(2,1)}, bf16[128,...) custom-call(bf16[6144,128]{1,0:T(8,128)(2,1)S(1)} %bitcast.14, bf16[1152,128]{1,0:T(8,128)(2,1)} %get-tuple-element.26.own, ...), custom_call_target="tpu_custom_call" | custom-call | tf_op jit(solution)/shard_map/pallas_call | solution.py:318
  (8 shorter events, 0.0 us)
Async XLA Ops:
  4.3 24.2 %copy-start = (bf16[1152,128]{1,0:T(8,128)(2,1)S(1)}, bf16[1152,128]{1,0:T(8,128)(2,1)}, u32[]{:S(2)}) copy-start(bf16[1152,128]{1,0:T(8,128)(2,1)} %get-tuple-element.24.refs_0_) | copy-start | bytes 884740
  4.3 68.0 %all-to-all-start = ((bf16[128,48,128]{2,1,0:T(8,128)(2,1)}), bf16[128,48,128]{2,1,0:T(8,128)(2,1)S(1)}, u32[]{:S(2)}, u32[]{:S(2)}) async-start(bf16[128,48,128]{2,1,0:T(8,128)(2,1)} %bitcast.17), calls=%async_computation | async-start | bytes 3145728 | tf_op jit(solution)/shard_map/all_to_all | solution.py:342
  28.5 12.1 %collective-permute-start = (bf16[1152,128]{1,0:T(8,128)(2,1)S(1)}, bf16[1152,128]{1,0:T(8,128)(2,1)S(1)}, u32[]{:S(2)}, u32[]{:S(2)}) collective-permute-start(bf16[1152,128]{1,0:T(8,128)(2,1)S(1)} %copy-done), channel_id=1, source_target_pairs={{0,128},{128,256},{256,384},{384,512},{512,640},{640,768},{768,896... | collective-permute-start | bytes 884744 | tf_op jit(solution)/shard_map/ppermute | solution.py:294
  31.0 11.5 %collective-permute-start.4 = (bf16[1152,128]{1,0:T(8,128)(2,1)S(1)}, bf16[1152,128]{1,0:T(8,128)(2,1)S(1)}, u32[]{:S(2)}, u32[]{:S(2)}) collective-permute-start(bf16[1152,128]{1,0:T(8,128)(2,1)S(1)} %copy-done), channel_id=1, source_target_pairs={{0,896},{128,0},{256,128},{384,256},{512,384},{640,512},{768,640},... | collective-permute-start | bytes 884744 | tf_op jit(solution)/shard_map/ppermute | solution.py:294
  40.6 31.6 %copy-start.1 = (bf16[1152,128]{1,0:T(8,128)(2,1)}, bf16[1152,128]{1,0:T(8,128)(2,1)S(1)}, u32[]{:S(2)}) copy-start(bf16[1152,128]{1,0:T(8,128)(2,1)S(1)} %collective-permute-done.refs_1_) | copy-start | bytes 884740
  40.6 11.3 %collective-permute-start.1 = (bf16[1152,128]{1,0:T(8,128)(2,1)S(1)}, bf16[1152,128]{1,0:T(8,128)(2,1)S(1)}, u32[]{:S(2)}, u32[]{:S(2)}) collective-permute-start(bf16[1152,128]{1,0:T(8,128)(2,1)S(1)} %collective-permute-done.refs_1_), channel_id=1, source_target_pairs={{0,128},{128,256},{256,384},{384,512},{512,640},{640,768},{768,896... | collective-permute-start | bytes 884744 | tf_op jit(solution)/shard_map/ppermute | solution.py:294
  42.6 29.7 %copy-start.2 = (bf16[1152,128]{1,0:T(8,128)(2,1)}, bf16[1152,128]{1,0:T(8,128)(2,1)S(1)}, u32[]{:S(2)}) copy-start(bf16[1152,128]{1,0:T(8,128)(2,1)S(1)} %collective-permute-done.4.refs_5_) | copy-start | bytes 884740
  42.6 11.2 %collective-permute-start.5 = (bf16[1152,128]{1,0:T(8,128)(2,1)S(1)}, bf16[1152,128]{1,0:T(8,128)(2,1)S(1)}, u32[]{:S(2)}, u32[]{:S(2)}) collective-permute-start(bf16[1152,128]{1,0:T(8,128)(2,1)S(1)} %collective-permute-done.4.refs_5_), channel_id=1, source_target_pairs={{0,896},{128,0},{256,128},{384,256},{512,384},{640,512},{768,640},... | collective-permute-start | bytes 884744 | tf_op jit(solution)/shard_map/ppermute | solution.py:294
  51.9 20.4 %copy-start.3 = (bf16[1152,128]{1,0:T(8,128)(2,1)}, bf16[1152,128]{1,0:T(8,128)(2,1)S(1)}, u32[]{:S(2)}) copy-start(bf16[1152,128]{1,0:T(8,128)(2,1)S(1)} %collective-permute-done.1.refs_2_) | copy-start | bytes 884740
  51.9 10.4 %collective-permute-start.2 = (bf16[1152,128]{1,0:T(8,128)(2,1)S(1)}, bf16[1152,128]{1,0:T(8,128)(2,1)S(1)}, u32[]{:S(2)}, u32[]{:S(2)}) collective-permute-start(bf16[1152,128]{1,0:T(8,128)(2,1)S(1)} %collective-permute-done.1.refs_2_), channel_id=1, source_target_pairs={{0,128},{128,256},{256,384},{384,512},{512,640},{640,768},{768,896... | collective-permute-start | bytes 884744 | tf_op jit(solution)/shard_map/ppermute | solution.py:294
  53.8 18.4 %copy-start.4 = (bf16[1152,128]{1,0:T(8,128)(2,1)}, bf16[1152,128]{1,0:T(8,128)(2,1)S(1)}, u32[]{:S(2)}) copy-start(bf16[1152,128]{1,0:T(8,128)(2,1)S(1)} %collective-permute-done.5.refs_6_) | copy-start | bytes 884740
  53.8 10.4 %collective-permute-start.6 = (bf16[1152,128]{1,0:T(8,128)(2,1)S(1)}, bf16[1152,128]{1,0:T(8,128)(2,1)S(1)}, u32[]{:S(2)}, u32[]{:S(2)}) collective-permute-start(bf16[1152,128]{1,0:T(8,128)(2,1)S(1)} %collective-permute-done.5.refs_6_), channel_id=1, source_target_pairs={{0,896},{128,0},{256,128},{384,256},{512,384},{640,512},{768,640},... | collective-permute-start | bytes 884744 | tf_op jit(solution)/shard_map/ppermute | solution.py:294
  62.3 10.0 %copy-start.5 = (bf16[1152,128]{1,0:T(8,128)(2,1)}, bf16[1152,128]{1,0:T(8,128)(2,1)S(1)}, u32[]{:S(2)}) copy-start(bf16[1152,128]{1,0:T(8,128)(2,1)S(1)} %collective-permute-done.2.refs_3_) | copy-start | bytes 884740
  62.3 9.9 %collective-permute-start.3 = (bf16[1152,128]{1,0:T(8,128)(2,1)S(1)}, bf16[1152,128]{1,0:T(8,128)(2,1)}, u32[]{:S(2)}, u32[]{:S(2)}) collective-permute-start(bf16[1152,128]{1,0:T(8,128)(2,1)S(1)} %collective-permute-done.2.refs_3_), channel_id=1, source_target_pairs={{0,128},{128,256},{256,384},{384,512},{512,640},{640,768},{768,896... | collective-permute-start | bytes 884744 | tf_op jit(solution)/shard_map/ppermute | solution.py:294
  64.2 8.0 %copy-start.6 = (bf16[1152,128]{1,0:T(8,128)(2,1)}, bf16[1152,128]{1,0:T(8,128)(2,1)S(1)}, u32[]{:S(2)}) copy-start(bf16[1152,128]{1,0:T(8,128)(2,1)S(1)} %collective-permute-done.6.refs_7_) | copy-start | bytes 884740
  80.5 14.0 %copy-start.15 = (bf16[1152,128]{1,0:T(8,128)(2,1)S(1)}, bf16[1152,128]{1,0:T(8,128)(2,1)}, u32[]{:S(2)}) copy-start(bf16[1152,128]{1,0:T(8,128)(2,1)} %get-tuple-element.30) | copy-start | bytes 884740
  80.5 16.2 %copy-start.14 = (bf16[1152,128]{1,0:T(8,128)(2,1)S(1)}, bf16[1152,128]{1,0:T(8,128)(2,1)}, u32[]{:S(2)}) copy-start(bf16[1152,128]{1,0:T(8,128)(2,1)} %get-tuple-element.33) | copy-start | bytes 884740
  80.5 26.2 %copy-start.11 = (bf16[1152,128]{1,0:T(8,128)(2,1)S(1)}, bf16[1152,128]{1,0:T(8,128)(2,1)}, u32[]{:S(2)}) copy-start(bf16[1152,128]{1,0:T(8,128)(2,1)} %get-tuple-element.29) | copy-start | bytes 884740
  80.5 28.2 %copy-start.10 = (bf16[1152,128]{1,0:T(8,128)(2,1)S(1)}, bf16[1152,128]{1,0:T(8,128)(2,1)}, u32[]{:S(2)}) copy-start(bf16[1152,128]{1,0:T(8,128)(2,1)} %get-tuple-element.32) | copy-start | bytes 884740
  80.5 58.0 %all-to-all-start.1 = ((bf16[128,48,128]{2,1,0:T(8,128)(2,1)}), bf16[128,48,128]{2,1,0:T(8,128)(2,1)S(1)}, u32[]{:S(2)}, u32[]{:S(2)}) async-start(bf16[128,48,128]{2,1,0:T(8,128)(2,1)} %bitcast.16), calls=%async_computation.1 | async-start | bytes 3145728 | tf_op jit(solution)/shard_map/all_to_all | solution.py:342
  94.4 23.7 %copy-start.9 = (bf16[1152,128]{1,0:T(8,128)(2,1)S(1)}, bf16[1152,128]{1,0:T(8,128)(2,1)}, u32[]{:S(2)}) copy-start(bf16[1152,128]{1,0:T(8,128)(2,1)} %get-tuple-element.28) | copy-start | bytes 884740
  94.5 25.7 %copy-start.8 = (bf16[1152,128]{1,0:T(8,128)(2,1)S(1)}, bf16[1152,128]{1,0:T(8,128)(2,1)}, u32[]{:S(2)}) copy-start(bf16[1152,128]{1,0:T(8,128)(2,1)} %get-tuple-element.31) | copy-start | bytes 884740
  94.5 12.3 %collective-permute-start.7 = (bf16[1152,128]{1,0:T(8,128)(2,1)S(1)}, bf16[1152,128]{1,0:T(8,128)(2,1)S(1)}, u32[]{:S(2)}, u32[]{:S(2)}) collective-permute-start(bf16[1152,128]{1,0:T(8,128)(2,1)S(1)} %copy-done.15), channel_id=1, source_target_pairs={{0,128},{128,256},{256,384},{384,512},{512,640},{640,768},{768,896... | collective-permute-start | bytes 884744 | tf_op jit(solution)/shard_map/ppermute | solution.py:294
  96.7 12.0 %collective-permute-start.11 = (bf16[1152,128]{1,0:T(8,128)(2,1)S(1)}, bf16[1152,128]{1,0:T(8,128)(2,1)S(1)}, u32[]{:S(2)}, u32[]{:S(2)}) collective-permute-start(bf16[1152,128]{1,0:T(8,128)(2,1)S(1)} %copy-done.14), channel_id=1, source_target_pairs={{0,896},{128,0},{256,128},{384,256},{512,384},{640,512},{768,640},... | collective-permute-start | bytes 884744 | tf_op jit(solution)/shard_map/ppermute | solution.py:294
  106.7 21.9 %copy-start.7 = (bf16[1152,128]{1,0:T(8,128)(2,1)S(1)}, bf16[1152,128]{1,0:T(8,128)(2,1)}, u32[]{:S(2)}) copy-start(bf16[1152,128]{1,0:T(8,128)(2,1)} %get-tuple-element.27) | copy-start | bytes 884740
  106.8 11.3 %collective-permute-start.8 = (bf16[1152,128]{1,0:T(8,128)(2,1)S(1)}, bf16[1152,128]{1,0:T(8,128)(2,1)S(1)}, u32[]{:S(2)}, u32[]{:S(2)}) collective-permute-start(bf16[1152,128]{1,0:T(8,128)(2,1)S(1)} %add.15), channel_id=1, source_target_pairs={{0,128},{128,256},{256,384},{384,512},{512,640},{640,768},{768,896... | collective-permute-start | bytes 884744 | tf_op jit(solution)/shard_map/ppermute | solution.py:294
  108.9 11.3 %collective-permute-start.12 = (bf16[1152,128]{1,0:T(8,128)(2,1)S(1)}, bf16[1152,128]{1,0:T(8,128)(2,1)S(1)}, u32[]{:S(2)}, u32[]{:S(2)}) collective-permute-start(bf16[1152,128]{1,0:T(8,128)(2,1)S(1)} %add.18), channel_id=1, source_target_pairs={{0,896},{128,0},{256,128},{384,256},{512,384},{640,512},{768,640},... | collective-permute-start | bytes 884744 | tf_op jit(solution)/shard_map/ppermute | solution.py:294
  118.2 10.4 %collective-permute-start.9 = (bf16[1152,128]{1,0:T(8,128)(2,1)S(1)}, bf16[1152,128]{1,0:T(8,128)(2,1)S(1)}, u32[]{:S(2)}, u32[]{:S(2)}) collective-permute-start(bf16[1152,128]{1,0:T(8,128)(2,1)S(1)} %add.16), channel_id=1, source_target_pairs={{0,128},{128,256},{256,384},{384,512},{512,640},{640,768},{768,896... | collective-permute-start | bytes 884744 | tf_op jit(solution)/shard_map/ppermute | solution.py:294
  120.2 10.4 %collective-permute-start.13 = (bf16[1152,128]{1,0:T(8,128)(2,1)S(1)}, bf16[1152,128]{1,0:T(8,128)(2,1)S(1)}, u32[]{:S(2)}, u32[]{:S(2)}) collective-permute-start(bf16[1152,128]{1,0:T(8,128)(2,1)S(1)} %add.19), channel_id=1, source_target_pairs={{0,896},{128,0},{256,128},{384,256},{512,384},{640,512},{768,640},... | collective-permute-start | bytes 884744 | tf_op jit(solution)/shard_map/ppermute | solution.py:294
  128.7 9.8 %collective-permute-start.10 = (bf16[1152,128]{1,0:T(8,128)(2,1)S(1)}, bf16[1152,128]{1,0:T(8,128)(2,1)S(1)}, u32[]{:S(2)}, u32[]{:S(2)}) collective-permute-start(bf16[1152,128]{1,0:T(8,128)(2,1)S(1)} %add.17), channel_id=1, source_target_pairs={{0,128},{128,256},{256,384},{384,512},{512,640},{640,768},{768,896... | collective-permute-start | bytes 884744 | tf_op jit(solution)/shard_map/ppermute | solution.py:294
  130.6 7.9 %copy-start.12 = (bf16[1152,128]{1,0:T(8,128)(2,1)}, bf16[1152,128]{1,0:T(8,128)(2,1)S(1)}, u32[]{:S(2)}) copy-start(bf16[1152,128]{1,0:T(8,128)(2,1)S(1)} %collective-permute-done.13.left) | copy-start | bytes 884740
  138.5 0.7 copy-start.13

commit v5 on v4

--- a/solution.py
+++ b/solution.py
@@ -46,12 +46,6 @@
     column = lax.broadcasted_iota(jnp.int32, (tokens, tokens), 1)
     earlier = (row < column).astype(F32).astype(BF16)
     return matches, named, dot(named.astype(BF16), earlier)
-
-
-def identity(size):
-    row = lax.broadcasted_iota(jnp.int32, (size, size), 0)
-    column = lax.broadcasted_iota(jnp.int32, (size, size), 1)
-    return (row == column).astype(F32).astype(BF16)
 
 
 def prepare_kernel(tokens, cotangent, ids, weights, gate, up, down, out, packed, rows):
@@ -177,12 +171,20 @@
     rows[...] = back[...].astype(F32)
     matches, _, rank = token_ranks(ids[...], experts)
     ranks = [rank == float(r) for r in range(CAP)]
-    pick = jnp.concatenate(
+    values = weights[...].astype(F32)
+    slots = [
+        jnp.concatenate([jnp.where(match & at, 1.0, 0.0) for at in ranks], axis=0)
+        for match in matches
+    ]
+    pairs = range(columns // 2)
+    plain = jnp.concatenate([slots[2 * j] + slots[2 * j + 1] for j in pairs], axis=1).astype(BF16)
+    scaled = jnp.concatenate(
         [
-            jnp.concatenate([jnp.where(match & at, 1.0, 0.0) for match in matches], axis=1)
-            for at in ranks
-        ],
-        axis=0,
+            slots[2 * j] * values[2 * j : 2 * j + 1, :]
+            + slots[2 * j + 1] * values[2 * j + 1 : 2 * j + 2, :]
+            for j in pairs
+        ],
+        axis=1,
     ).astype(BF16)
     outs = jnp.concatenate(
         [gather_rows(rows, experts, r * per, blocks, per).astype(BF16) for r in range(CAP)], axis=0
@@ -194,43 +196,32 @@
         ],
         axis=0,
     )
-    out = dot(pick, outs, ((0,), (0,)))
-    grad = dot(pick, grads, ((0,), (0,)))
-    eye = identity(tokens)
-    values = dot(eye, weights[...], ((1,), (1,)))
-    cot = cotangent[...].astype(F32)
-    lane = lax.broadcasted_iota(jnp.int32, (tokens, columns), 1)
-    total = jnp.zeros((tokens, width), F32)
-    total_grad = jnp.zeros((tokens, width), F32)
-    routed = jnp.zeros((tokens, columns), F32)
-    for j in range(columns // 2):
-        a, b = 2 * j, 2 * j + 1
-        first, second = out[a * tokens : (a + 1) * tokens], out[b * tokens : (b + 1) * tokens]
-        pair = values[:, a : a + 1] * first + values[:, b : b + 1] * second
-        total = total + pair.astype(BF16).astype(F32)
-        pair = grad[a * tokens : (a + 1) * tokens] + grad[b * tokens : (b + 1) * tokens]
-        total_grad = total_grad + pair.astype(BF16).astype(F32)
-        routed = jnp.where(lane == a, jnp.sum(cot * first, axis=1, keepdims=True), routed)
-        routed = jnp.where(lane == b, jnp.sum(cot * second, axis=1, keepdims=True), routed)
+    out = dot(scaled, outs, ((0,), (0,))).astype(BF16).astype(F32)
+    grad = dot(plain, grads, ((0,), (0,))).astype(BF16).astype(F32)
+    total, total_grad = out[:tokens], grad[:tokens]
+    for j in pairs[1:]:
+        total = total + out[j * tokens : (j + 1) * tokens]
+        total_grad = total_grad + grad[j * tokens : (j + 1) * tokens]
     layer[...] = total.astype(BF16)
     token_grads[...] = total_grad.astype(BF16)
-    router_grads[...] = dot(routed.astype(BF16), eye, ((0,), (0,))).astype(BF16)
-
-
-def finish_kernel(back, own, right, left, cotangent, ids, weights, *refs):
-    layer, token_grads, router_grads, gate, up, down, lines, rows, sems = refs
-    copies = [
-        pltpu.make_async_copy(part, lines.at[i], sems.at[i])
-        for i, part in enumerate((own, right, left))
-    ]
-    for copy in copies:
-        copy.start()
+    products = dot(outs, cotangent[...], ((1,), (1,)))
+    row = lax.broadcasted_iota(jnp.int32, (columns, tokens), 0)
+    routed = jnp.zeros((columns, tokens), F32)
+    for k, slot in enumerate(slots):
+        column = jnp.sum(slot * products, axis=0, keepdims=True)
+        routed = jnp.where(row == k, column, routed)
+    router_grads[...] = routed.astype(BF16)
+
+
+def finish_kernel(back, right, left, own, cotangent, ids, weights, *refs):
+    layer, token_grads, router_grads, gate, up, down, mine, rows, sem = refs
+    copy = pltpu.make_async_copy(own, mine, sem.at[0])
+    copy.start()
     combine_kernel(back, cotangent, ids, weights, layer, token_grads, router_grads, rows)
-    for copy in copies:
-        copy.wait()
+    copy.wait()
     features, hidden = gate.shape
     total = (
-        lines[0].astype(F32) + lines[1].astype(F32) + lines[2].astype(F32)
+        mine[...].astype(F32) + right[...].astype(F32) + left[...].astype(F32)
     ).astype(BF16)
     for i, weight in enumerate((gate, up)):
         for c in range(hidden // LANES):
@@ -326,12 +317,12 @@
             (hidden, LANES),
         ],
         scratch=[
-            pltpu.VMEM((3,) + parts[0].shape, BF16),
+            pltpu.VMEM(parts[0].shape, BF16),
             pltpu.VMEM(back.shape, F32),
-            pltpu.SemaphoreType.DMA((3,)),
-        ],
-        in_specs=[vmem()] + [anywhere] * 3 + [vmem()] * 3,
-    )(back, *parts, cotangent, ids, weights)
+            pltpu.SemaphoreType.DMA((1,)),
+        ],
+        in_specs=[vmem()] * 3 + [anywhere] + [vmem()] * 3,
+    )(on_chip(back), on_chip(parts[1]), on_chip(parts[2]), parts[0], cotangent, ids, weights)
 
 
 def on_chip(value):
@@ -364,7 +355,7 @@
     returned = exchange(back, experts)
     parts = scatter_ring(terms)
     layer, token_grads, router_grads, gate, up, down = finish(
-        on_chip(returned), cotangent, ids, weights, parts, features, hidden
+        returned, cotangent, ids, weights, parts, features, hidden
     )
     return layer, token_grads, router_grads.T, gate[None], up[None], down[None]
 

time: 144 us -> 143 us (level)
  the two profiles are of different devices: /device:TPU:24 before, /device:TPU:1 now
where the time goes in v5:
time: 143 us; the launch traced here: 141 us
  starting transfers between devices  85 us (59%)
  waiting for transfers between devices  38.5 us (27%)
  Pallas kernels  15.6 us (11%)
    ppermute x14, starting transfers between devices, shifted(): lax.ppermute(value, 'dp', [(i, (i + by) % peers) for i in range(peers)])  43.1 us
    all_to_all x2, starting transfers between devices, exchange(): lax.all_to_all(lines.reshape(peers, -1, LANES), ('group', 'local'), split...  41.9 us
    ppermute x14, waiting for transfers between devices, shifted(): lax.ppermute(value, 'dp', [(i, (i + by) % peers) for i in range(peers)])  34.1 us
    pallas_call x1, Pallas kernels, expert(): pl.pallas_call(expert_kernel, out_shape=[jax.ShapeDtypeStruct(recv.shape,...  8.26 us
    all_to_all x2, waiting for transfers between devices, exchange(): lax.all_to_all(lines.reshape(peers, -1, LANES), ('group', 'local'), split...  4.37 us
    pallas_call x1, Pallas kernels, finish(): call(finish_kernel, [cotangent.shape, cotangent.shape, ids.shape, (featur...  3.72 us
    pallas_call x1, Pallas kernels, prepare(): call(prepare_kernel, [(lines, LANES), (3 * gate.shape[1], LANES)], scratc...  3.64 us
  transfers between devices with their start and end apart: 16, of which 10 were waited for; matrix products, arithmetic and copies ran while one was open for 0% of the time, Pallas kernels for 0%

profile of v5, /device:TPU:1, one launch (start us, length us, event | category | flops | bytes accessed | tf_op | source)
XLA Modules:
  0.0 140.7 jit_solution(10887078078773901798)
XLA Ops:
  0.6 3.6 %shard_map.118 = (bf16[6144,128]{1,0:T(8,128)(2,1)}, bf16[1152,128]{1,0:T(8,128)(2,1)}) custom-call(bf16[16,1024]{1,0:T(8,128)(2,1)} %tokens.1, bf16[16,1024]{1,0:T(8,128)(2,1)} %cotangent.3, s32[8,16]{1,0:T(8,128)} %bitcast.21, bf16[8,16]{1,0:T(8,128)(2,1)} %bitcast.23, bf16[128,384]{1,0:T(8,128)(2,1)} %bitcast.18, bf16[128,384]{1,0:T(8,128)(2,1)} %bitcast.19, ...), custom_call_target="tpu_custom_call" | custom-call | tf_op jit(solution)/shard_map/pallas_call | solution.py:248
  4.3 0.0 copy-start
  4.3 25.4 %all-to-all-start = ((bf16[128,48,128]{2,1,0:T(8,128)(2,1)}), bf16[128,48,128]{2,1,0:T(8,128)(2,1)S(1)}, u32[]{:S(2)}, u32[]{:S(2)}) async-start(bf16[128,48,128]{2,1,0:T(8,128)(2,1)} %bitcast.17), calls=%async_computation | async-start | bytes 3145728 | tf_op jit(solution)/shard_map/all_to_all | solution.py:333
  29.6 0.0 copy-done
  29.7 3.1 %collective-permute-start = (bf16[1152,128]{1,0:T(8,128)(2,1)S(1)}, bf16[1152,128]{1,0:T(8,128)(2,1)S(1)}, u32[]{:S(2)}, u32[]{:S(2)}) collective-permute-start(bf16[1152,128]{1,0:T(8,128)(2,1)S(1)} %copy-done), channel_id=1, source_target_pairs={{0,128},{128,256},{256,384},{384,512},{512,640},{640,768},{768,896... | collective-permute-start | bytes 884744 | tf_op jit(solution)/shard_map/ppermute | solution.py:285
  32.8 3.4 %collective-permute-start.4 = (bf16[1152,128]{1,0:T(8,128)(2,1)S(1)}, bf16[1152,128]{1,0:T(8,128)(2,1)S(1)}, u32[]{:S(2)}, u32[]{:S(2)}) collective-permute-start(bf16[1152,128]{1,0:T(8,128)(2,1)S(1)} %copy-done), channel_id=1, source_target_pairs={{0,896},{128,0},{256,128},{384,256},{512,384},{640,512},{768,640},... | collective-permute-start | bytes 884744 | tf_op jit(solution)/shard_map/ppermute | solution.py:285
  36.2 4.3 %collective-permute-done.refs_1_ = bf16[1152,128]{1,0:T(8,128)(2,1)S(1)} collective-permute-done((bf16[1152,128]{1,0:T(8,128)(2,1)S(1)}, bf16[1152,128]{1,0:T(8,128)(2,1)S(1)}, u32[]{:S(2)}, u32[]{:S(2)}) %collective-permute-start) | collective-permute-done | bytes 294944 | tf_op jit(solution)/shard_map/ppermute | solution.py:285
  40.4 1.9 %collective-permute-start.1 = (bf16[1152,128]{1,0:T(8,128)(2,1)S(1)}, bf16[1152,128]{1,0:T(8,128)(2,1)S(1)}, u32[]{:S(2)}, u32[]{:S(2)}) collective-permute-start(bf16[1152,128]{1,0:T(8,128)(2,1)S(1)} %collective-permute-done.refs_1_), channel_id=1, source_target_pairs={{0,128},{128,256},{256,384},{384,512},{512,640},{640,768},{768,896... | collective-permute-start | bytes 884744 | tf_op jit(solution)/shard_map/ppermute | solution.py:285
  42.4 0.0 collective-permute-done.4.refs_5_
  42.4 0.0 copy-start.2
  42.4 4.6 %collective-permute-start.5 = (bf16[1152,128]{1,0:T(8,128)(2,1)S(1)}, bf16[1152,128]{1,0:T(8,128)(2,1)S(1)}, u32[]{:S(2)}, u32[]{:S(2)}) collective-permute-start(bf16[1152,128]{1,0:T(8,128)(2,1)S(1)} %collective-permute-done.4.refs_5_), channel_id=1, source_target_pairs={{0,896},{128,0},{256,128},{384,256},{512,384},{640,512},{768,640},... | collective-permute-start | bytes 884744 | tf_op jit(solution)/shard_map/ppermute | solution.py:285
  47.0 3.4 %collective-permute-done.1.refs_2_ = bf16[1152,128]{1,0:T(8,128)(2,1)S(1)} collective-permute-done((bf16[1152,128]{1,0:T(8,128)(2,1)S(1)}, bf16[1152,128]{1,0:T(8,128)(2,1)S(1)}, u32[]{:S(2)}, u32[]{:S(2)}) %collective-permute-start.1) | collective-permute-done | bytes 294944 | tf_op jit(solution)/shard_map/ppermute | solution.py:285
  50.4 1.9 %collective-permute-start.2 = (bf16[1152,128]{1,0:T(8,128)(2,1)S(1)}, bf16[1152,128]{1,0:T(8,128)(2,1)S(1)}, u32[]{:S(2)}, u32[]{:S(2)}) collective-permute-start(bf16[1152,128]{1,0:T(8,128)(2,1)S(1)} %collective-permute-done.1.refs_2_), channel_id=1, source_target_pairs={{0,128},{128,256},{256,384},{384,512},{512,640},{640,768},{768,896... | collective-permute-start | bytes 884744 | tf_op jit(solution)/shard_map/ppermute | solution.py:285
  52.3 0.0 collective-permute-done.5.refs_6_
  52.3 0.0 copy-start.4
  52.3 4.6 %collective-permute-start.6 = (bf16[1152,128]{1,0:T(8,128)(2,1)S(1)}, bf16[1152,128]{1,0:T(8,128)(2,1)S(1)}, u32[]{:S(2)}, u32[]{:S(2)}) collective-permute-start(bf16[1152,128]{1,0:T(8,128)(2,1)S(1)} %collective-permute-done.5.refs_6_), channel_id=1, source_target_pairs={{0,896},{128,0},{256,128},{384,256},{512,384},{640,512},{768,640},... | collective-permute-start | bytes 884744 | tf_op jit(solution)/shard_map/ppermute | solution.py:285
  56.9 2.5 %collective-permute-done.2.refs_3_ = bf16[1152,128]{1,0:T(8,128)(2,1)S(1)} collective-permute-done((bf16[1152,128]{1,0:T(8,128)(2,1)S(1)}, bf16[1152,128]{1,0:T(8,128)(2,1)S(1)}, u32[]{:S(2)}, u32[]{:S(2)}) %collective-permute-start.2) | collective-permute-done | bytes 294944 | tf_op jit(solution)/shard_map/ppermute | solution.py:285
  59.4 1.9 %collective-permute-start.3 = (bf16[1152,128]{1,0:T(8,128)(2,1)S(1)}, bf16[1152,128]{1,0:T(8,128)(2,1)}, u32[]{:S(2)}, u32[]{:S(2)}) collective-permute-start(bf16[1152,128]{1,0:T(8,128)(2,1)S(1)} %collective-permute-done.2.refs_3_), channel_id=1, source_target_pairs={{0,128},{128,256},{256,384},{384,512},{512,640},{640,768},{768,896... | collective-permute-start | bytes 884744 | tf_op jit(solution)/shard_map/ppermute | solution.py:285
  61.3 0.0 collective-permute-done.6.refs_7_
  61.3 0.0 copy-start.6
  61.4 7.0 %collective-permute-done.3.refs_4_ = bf16[1152,128]{1,0:T(8,128)(2,1)} collective-permute-done((bf16[1152,128]{1,0:T(8,128)(2,1)S(1)}, bf16[1152,128]{1,0:T(8,128)(2,1)}, u32[]{:S(2)}, u32[]{:S(2)}) %collective-permute-start.3) | collective-permute-done | bytes 294944 | tf_op jit(solution)/shard_map/ppermute | solution.py:285
  68.4 2.4 %all-to-all-done = bf16[128,48,128]{2,1,0:T(8,128)(2,1)S(1)} async-done(((bf16[128,48,128]{2,1,0:T(8,128)(2,1)}), bf16[128,48,128]{2,1,0:T(8,128)(2,1)S(1)}, u32[]{:S(2)}, u32[]{:S(2)}) %all-to-all-start) | async-done | bytes 1572896 | tf_op jit(solution)/shard_map/all_to_all | solution.py:333
  70.8 0.0 copy-done.1
  70.8 0.0 copy-done.2
  70.8 0.0 copy-done.3
  70.8 0.0 copy-done.4
  70.8 0.0 copy-done.5
  70.8 0.0 copy-done.6
  70.8 8.3 %expert.1 = (bf16[6144,128]{1,0:T(8,128)(2,1)}, bf16[1152,128]{1,0:T(8,128)(2,1)}, bf16[1152,128]{1,0:T(8,128)(2,1)}, bf16[1152,128]{1,0:T(8,128)(2,1)}, bf16[11...) custom-call(s32[1]{0:T(128)} %bitcast.place, ...), custom_call_target="tpu_custom_call" | custom-call | tf_op jit(solution)/shard_map/expert/pallas_call | solution.py:261
  79.1 0.0 copy-start.13
  79.1 0.0 copy-start.12
  79.1 0.0 copy-start.11
  79.1 0.0 copy-start.10
  79.1 16.5 %all-to-all-start.1 = ((bf16[128,48,128]{2,1,0:T(8,128)(2,1)}), bf16[128,48,128]{2,1,0:T(8,128)(2,1)S(1)}, u32[]{:S(2)}, u32[]{:S(2)}) async-start(bf16[128,48,128]{2,1,0:T(8,128)(2,1)} %bitcast.16), calls=%async_computation.1 | async-start | bytes 3145728 | tf_op jit(solution)/shard_map/all_to_all | solution.py:333
  95.7 0.0 copy-start.9
  95.7 0.0 copy-start.8
  95.7 0.0 copy-done.13
  95.7 2.2 %collective-permute-start.7 = (bf16[1152,128]{1,0:T(8,128)(2,1)S(1)}, bf16[1152,128]{1,0:T(8,128)(2,1)S(1)}, u32[]{:S(2)}, u32[]{:S(2)}) collective-permute-start(bf16[1152,128]{1,0:T(8,128)(2,1)S(1)} %copy-done.13), channel_id=1, source_target_pairs={{0,128},{128,256},{256,384},{384,512},{512,640},{640,768},{768,896... | collective-permute-start | bytes 884744 | tf_op jit(solution)/shard_map/ppermute | solution.py:285
  97.9 0.0 copy-done.12
  97.9 4.6 %collective-permute-start.11 = (bf16[1152,128]{1,0:T(8,128)(2,1)S(1)}, bf16[1152,128]{1,0:T(8,128)(2,1)S(1)}, u32[]{:S(2)}, u32[]{:S(2)}) collective-permute-start(bf16[1152,128]{1,0:T(8,128)(2,1)S(1)} %copy-done.12), channel_id=1, source_target_pairs={{0,896},{128,0},{256,128},{384,256},{512,384},{640,512},{768,640},... | collective-permute-start | bytes 884744 | tf_op jit(solution)/shard_map/ppermute | solution.py:285
  102.5 4.1 %collective-permute-done.7 = bf16[1152,128]{1,0:T(8,128)(2,1)S(1)} collective-permute-done((bf16[1152,128]{1,0:T(8,128)(2,1)S(1)}, bf16[1152,128]{1,0:T(8,128)(2,1)S(1)}, u32[]{:S(2)}, u32[]{:S(2)}) %collective-permute-start.7) | collective-permute-done | bytes 294944 | tf_op jit(solution)/shard_map/ppermute | solution.py:285
  106.6 0.0 copy-done.11
  106.6 0.1 add.15
  106.7 1.9 %collective-permute-start.8 = (bf16[1152,128]{1,0:T(8,128)(2,1)S(1)}, bf16[1152,128]{1,0:T(8,128)(2,1)S(1)}, u32[]{:S(2)}, u32[]{:S(2)}) collective-permute-start(bf16[1152,128]{1,0:T(8,128)(2,1)S(1)} %add.15), channel_id=1, source_target_pairs={{0,128},{128,256},{256,384},{384,512},{512,640},{640,768},{768,896... | collective-permute-start | bytes 884744 | tf_op jit(solution)/shard_map/ppermute | solution.py:285
  108.6 0.0 collective-permute-done.11
  108.6 0.0 copy-done.10
  108.6 0.1 add.18
  108.7 4.6 %collective-permute-start.12 = (bf16[1152,128]{1,0:T(8,128)(2,1)S(1)}, bf16[1152,128]{1,0:T(8,128)(2,1)S(1)}, u32[]{:S(2)}, u32[]{:S(2)}) collective-permute-start(bf16[1152,128]{1,0:T(8,128)(2,1)S(1)} %add.18), channel_id=1, source_target_pairs={{0,896},{128,0},{256,128},{384,256},{512,384},{640,512},{768,640},... | collective-permute-start | bytes 884744 | tf_op jit(solution)/shard_map/ppermute | solution.py:285
  113.3 3.3 %collective-permute-done.8 = bf16[1152,128]{1,0:T(8,128)(2,1)S(1)} collective-permute-done((bf16[1152,128]{1,0:T(8,128)(2,1)S(1)}, bf16[1152,128]{1,0:T(8,128)(2,1)S(1)}, u32[]{:S(2)}, u32[]{:S(2)}) %collective-permute-start.8) | collective-permute-done | bytes 294944 | tf_op jit(solution)/shard_map/ppermute | solution.py:285
  116.6 0.0 copy-done.9
  116.6 0.1 add.16
  116.7 1.9 %collective-permute-start.9 = (bf16[1152,128]{1,0:T(8,128)(2,1)S(1)}, bf16[1152,128]{1,0:T(8,128)(2,1)S(1)}, u32[]{:S(2)}, u32[]{:S(2)}) collective-permute-start(bf16[1152,128]{1,0:T(8,128)(2,1)S(1)} %add.16), channel_id=1, source_target_pairs={{0,128},{128,256},{256,384},{384,512},{512,640},{640,768},{768,896... | collective-permute-start | bytes 884744 | tf_op jit(solution)/shard_map/ppermute | solution.py:285
  118.6 0.0 collective-permute-done.12
  118.6 0.0 copy-done.8
  118.6 0.1 add.19
  118.7 4.6 %collective-permute-start.13 = (bf16[1152,128]{1,0:T(8,128)(2,1)S(1)}, bf16[1152,128]{1,0:T(8,128)(2,1)S(1)}, u32[]{:S(2)}, u32[]{:S(2)}) collective-permute-start(bf16[1152,128]{1,0:T(8,128)(2,1)S(1)} %add.19), channel_id=1, source_target_pairs={{0,896},{128,0},{256,128},{384,256},{512,384},{640,512},{768,640},... | collective-permute-start | bytes 884744 | tf_op jit(solution)/shard_map/ppermute | solution.py:285
  123.3 2.4 %collective-permute-done.9 = bf16[1152,128]{1,0:T(8,128)(2,1)S(1)} collective-permute-done((bf16[1152,128]{1,0:T(8,128)(2,1)S(1)}, bf16[1152,128]{1,0:T(8,128)(2,1)S(1)}, u32[]{:S(2)}, u32[]{:S(2)}) %collective-permute-start.9) | collective-permute-done | bytes 294944 | tf_op jit(solution)/shard_map/ppermute | solution.py:285
  125.8 0.0 copy-done.7
  125.8 0.1 add.17
  125.8 1.9 %collective-permute-start.10 = (bf16[1152,128]{1,0:T(8,128)(2,1)S(1)}, bf16[1152,128]{1,0:T(8,128)(2,1)S(1)}, u32[]{:S(2)}, u32[]{:S(2)}) collective-permute-start(bf16[1152,128]{1,0:T(8,128)(2,1)S(1)} %add.17), channel_id=1, source_target_pairs={{0,128},{128,256},{256,384},{384,512},{512,640},{640,768},{768,896... | collective-permute-start | bytes 884744 | tf_op jit(solution)/shard_map/ppermute | solution.py:285
  127.8 0.0 collective-permute-done.13.left
  127.8 7.0 %collective-permute-done.10.right = bf16[1152,128]{1,0:T(8,128)(2,1)S(1)} collective-permute-done((bf16[1152,128]{1,0:T(8,128)(2,1)S(1)}, bf16[1152,128]{1,0:T(8,128)(2,1)S(1)}, u32[]{:S(2)}, u32[]{:S(2)}) %collective-permute-start.10) | collective-permute-done | bytes 294944 | tf_op jit(solution)/shard_map/ppermute | solution.py:285
  134.8 2.0 %all-to-all-done.1 = bf16[128,48,128]{2,1,0:T(8,128)(2,1)S(1)} async-done(((bf16[128,48,128]{2,1,0:T(8,128)(2,1)}), bf16[128,48,128]{2,1,0:T(8,128)(2,1)S(1)}, u32[]{:S(2)}, u32[]{:S(2)}) %all-to-all-start.1) | async-done | bytes 1572896 | tf_op jit(solution)/shard_map/all_to_all | solution.py:333
  136.8 3.7 %shard_map.119 = (bf16[16,1024]{1,0:T(8,128)(2,1)}, bf16[16,1024]{1,0:T(8,128)(2,1)}, bf16[8,16]{1,0:T(8,128)(2,1)}, bf16[128,384]{1,0:T(8,128)(2,1)}, bf16[128,...) custom-call(bf16[6144,128]{1,0:T(8,128)(2,1)S(1)} %bitcast.14, bf16[1152,128]{1,0:T(8,128)(2,1)S(1)} %collective-permute-done.10.right, ...), custom_call_target="tpu_custom_call" | custom-call | tf_op jit(solution)/shard_map/pallas_call | solution.py:309
  (4 shorter events, 0.0 us)
Async XLA Ops:
  4.3 25.4 %copy-start = (bf16[1152,128]{1,0:T(8,128)(2,1)S(1)}, bf16[1152,128]{1,0:T(8,128)(2,1)}, u32[]{:S(2)}) copy-start(bf16[1152,128]{1,0:T(8,128)(2,1)} %get-tuple-element.24.refs_0_) | copy-start | bytes 884740
  4.3 66.5 %all-to-all-start = ((bf16[128,48,128]{2,1,0:T(8,128)(2,1)}), bf16[128,48,128]{2,1,0:T(8,128)(2,1)S(1)}, u32[]{:S(2)}, u32[]{:S(2)}) async-start(bf16[128,48,128]{2,1,0:T(8,128)(2,1)} %bitcast.17), calls=%async_computation | async-start | bytes 3145728 | tf_op jit(solution)/shard_map/all_to_all | solution.py:333
  29.7 10.8 %collective-permute-start = (bf16[1152,128]{1,0:T(8,128)(2,1)S(1)}, bf16[1152,128]{1,0:T(8,128)(2,1)S(1)}, u32[]{:S(2)}, u32[]{:S(2)}) collective-permute-start(bf16[1152,128]{1,0:T(8,128)(2,1)S(1)} %copy-done), channel_id=1, source_target_pairs={{0,128},{128,256},{256,384},{384,512},{512,640},{640,768},{768,896... | collective-permute-start | bytes 884744 | tf_op jit(solution)/shard_map/ppermute | solution.py:285
  32.8 9.6 %collective-permute-start.4 = (bf16[1152,128]{1,0:T(8,128)(2,1)S(1)}, bf16[1152,128]{1,0:T(8,128)(2,1)S(1)}, u32[]{:S(2)}, u32[]{:S(2)}) collective-permute-start(bf16[1152,128]{1,0:T(8,128)(2,1)S(1)} %copy-done), channel_id=1, source_target_pairs={{0,896},{128,0},{256,128},{384,256},{512,384},{640,512},{768,640},... | collective-permute-start | bytes 884744 | tf_op jit(solution)/shard_map/ppermute | solution.py:285
  40.4 30.3 %copy-start.1 = (bf16[1152,128]{1,0:T(8,128)(2,1)}, bf16[1152,128]{1,0:T(8,128)(2,1)S(1)}, u32[]{:S(2)}) copy-start(bf16[1152,128]{1,0:T(8,128)(2,1)S(1)} %collective-permute-done.refs_1_) | copy-start | bytes 884740
  40.4 9.9 %collective-permute-start.1 = (bf16[1152,128]{1,0:T(8,128)(2,1)S(1)}, bf16[1152,128]{1,0:T(8,128)(2,1)S(1)}, u32[]{:S(2)}, u32[]{:S(2)}) collective-permute-start(bf16[1152,128]{1,0:T(8,128)(2,1)S(1)} %collective-permute-done.refs_1_), channel_id=1, source_target_pairs={{0,128},{128,256},{256,384},{384,512},{512,640},{640,768},{768,896... | collective-permute-start | bytes 884744 | tf_op jit(solution)/shard_map/ppermute | solution.py:285
  42.4 28.4 %copy-start.2 = (bf16[1152,128]{1,0:T(8,128)(2,1)}, bf16[1152,128]{1,0:T(8,128)(2,1)S(1)}, u32[]{:S(2)}) copy-start(bf16[1152,128]{1,0:T(8,128)(2,1)S(1)} %collective-permute-done.4.refs_5_) | copy-start | bytes 884740
  42.4 9.9 %collective-permute-start.5 = (bf16[1152,128]{1,0:T(8,128)(2,1)S(1)}, bf16[1152,128]{1,0:T(8,128)(2,1)S(1)}, u32[]{:S(2)}, u32[]{:S(2)}) collective-permute-start(bf16[1152,128]{1,0:T(8,128)(2,1)S(1)} %collective-permute-done.4.refs_5_), channel_id=1, source_target_pairs={{0,896},{128,0},{256,128},{384,256},{512,384},{640,512},{768,640},... | collective-permute-start | bytes 884744 | tf_op jit(solution)/shard_map/ppermute | solution.py:285
  50.4 20.4 %copy-start.3 = (bf16[1152,128]{1,0:T(8,128)(2,1)}, bf16[1152,128]{1,0:T(8,128)(2,1)S(1)}, u32[]{:S(2)}) copy-start(bf16[1152,128]{1,0:T(8,128)(2,1)S(1)} %collective-permute-done.1.refs_2_) | copy-start | bytes 884740
  50.4 9.1 %collective-permute-start.2 = (bf16[1152,128]{1,0:T(8,128)(2,1)S(1)}, bf16[1152,128]{1,0:T(8,128)(2,1)S(1)}, u32[]{:S(2)}, u32[]{:S(2)}) collective-permute-start(bf16[1152,128]{1,0:T(8,128)(2,1)S(1)} %collective-permute-done.1.refs_2_), channel_id=1, source_target_pairs={{0,128},{128,256},{256,384},{384,512},{512,640},{640,768},{768,896... | collective-permute-start | bytes 884744 | tf_op jit(solution)/shard_map/ppermute | solution.py:285
  52.3 18.5 %copy-start.4 = (bf16[1152,128]{1,0:T(8,128)(2,1)}, bf16[1152,128]{1,0:T(8,128)(2,1)S(1)}, u32[]{:S(2)}) copy-start(bf16[1152,128]{1,0:T(8,128)(2,1)S(1)} %collective-permute-done.5.refs_6_) | copy-start | bytes 884740
  52.3 9.0 %collective-permute-start.6 = (bf16[1152,128]{1,0:T(8,128)(2,1)S(1)}, bf16[1152,128]{1,0:T(8,128)(2,1)S(1)}, u32[]{:S(2)}, u32[]{:S(2)}) collective-permute-start(bf16[1152,128]{1,0:T(8,128)(2,1)S(1)} %collective-permute-done.5.refs_6_), channel_id=1, source_target_pairs={{0,896},{128,0},{256,128},{384,256},{512,384},{640,512},{768,640},... | collective-permute-start | bytes 884744 | tf_op jit(solution)/shard_map/ppermute | solution.py:285
  59.4 11.4 %copy-start.5 = (bf16[1152,128]{1,0:T(8,128)(2,1)}, bf16[1152,128]{1,0:T(8,128)(2,1)S(1)}, u32[]{:S(2)}) copy-start(bf16[1152,128]{1,0:T(8,128)(2,1)S(1)} %collective-permute-done.2.refs_3_) | copy-start | bytes 884740
  59.4 9.0 %collective-permute-start.3 = (bf16[1152,128]{1,0:T(8,128)(2,1)S(1)}, bf16[1152,128]{1,0:T(8,128)(2,1)}, u32[]{:S(2)}, u32[]{:S(2)}) collective-permute-start(bf16[1152,128]{1,0:T(8,128)(2,1)S(1)} %collective-permute-done.2.refs_3_), channel_id=1, source_target_pairs={{0,128},{128,256},{256,384},{384,512},{512,640},{640,768},{768,896... | collective-permute-start | bytes 884744 | tf_op jit(solution)/shard_map/ppermute | solution.py:285
  61.3 9.5 %copy-start.6 = (bf16[1152,128]{1,0:T(8,128)(2,1)}, bf16[1152,128]{1,0:T(8,128)(2,1)S(1)}, u32[]{:S(2)}) copy-start(bf16[1152,128]{1,0:T(8,128)(2,1)S(1)} %collective-permute-done.6.refs_7_) | copy-start | bytes 884740
  79.1 16.6 %copy-start.13 = (bf16[1152,128]{1,0:T(8,128)(2,1)S(1)}, bf16[1152,128]{1,0:T(8,128)(2,1)}, u32[]{:S(2)}) copy-start(bf16[1152,128]{1,0:T(8,128)(2,1)} %get-tuple-element.29) | copy-start | bytes 884740
  79.1 18.8 %copy-start.12 = (bf16[1152,128]{1,0:T(8,128)(2,1)S(1)}, bf16[1152,128]{1,0:T(8,128)(2,1)}, u32[]{:S(2)}) copy-start(bf16[1152,128]{1,0:T(8,128)(2,1)} %get-tuple-element.32) | copy-start | bytes 884740
  79.1 27.5 %copy-start.11 = (bf16[1152,128]{1,0:T(8,128)(2,1)S(1)}, bf16[1152,128]{1,0:T(8,128)(2,1)}, u32[]{:S(2)}) copy-start(bf16[1152,128]{1,0:T(8,128)(2,1)} %get-tuple-element.28) | copy-start | bytes 884740
  79.1 29.5 %copy-start.10 = (bf16[1152,128]{1,0:T(8,128)(2,1)S(1)}, bf16[1152,128]{1,0:T(8,128)(2,1)}, u32[]{:S(2)}) copy-start(bf16[1152,128]{1,0:T(8,128)(2,1)} %get-tuple-element.31) | copy-start | bytes 884740
  79.1 57.7 %all-to-all-start.1 = ((bf16[128,48,128]{2,1,0:T(8,128)(2,1)}), bf16[128,48,128]{2,1,0:T(8,128)(2,1)S(1)}, u32[]{:S(2)}, u32[]{:S(2)}) async-start(bf16[128,48,128]{2,1,0:T(8,128)(2,1)} %bitcast.16), calls=%async_computation.1 | async-start | bytes 3145728 | tf_op jit(solution)/shard_map/all_to_all | solution.py:333
  95.7 21.0 %copy-start.9 = (bf16[1152,128]{1,0:T(8,128)(2,1)S(1)}, bf16[1152,128]{1,0:T(8,128)(2,1)}, u32[]{:S(2)}) copy-start(bf16[1152,128]{1,0:T(8,128)(2,1)} %get-tuple-element.27) | copy-start | bytes 884740
  95.7 23.0 %copy-start.8 = (bf16[1152,128]{1,0:T(8,128)(2,1)S(1)}, bf16[1152,128]{1,0:T(8,128)(2,1)}, u32[]{:S(2)}) copy-start(bf16[1152,128]{1,0:T(8,128)(2,1)} %get-tuple-element.30) | copy-start | bytes 884740
  95.7 10.9 %collective-permute-start.7 = (bf16[1152,128]{1,0:T(8,128)(2,1)S(1)}, bf16[1152,128]{1,0:T(8,128)(2,1)S(1)}, u32[]{:S(2)}, u32[]{:S(2)}) collective-permute-start(bf16[1152,128]{1,0:T(8,128)(2,1)S(1)} %copy-done.13), channel_id=1, source_target_pairs={{0,128},{128,256},{256,384},{384,512},{512,640},{640,768},{768,896... | collective-permute-start | bytes 884744 | tf_op jit(solution)/shard_map/ppermute | solution.py:285
  97.9 10.7 %collective-permute-start.11 = (bf16[1152,128]{1,0:T(8,128)(2,1)S(1)}, bf16[1152,128]{1,0:T(8,128)(2,1)S(1)}, u32[]{:S(2)}, u32[]{:S(2)}) collective-permute-start(bf16[1152,128]{1,0:T(8,128)(2,1)S(1)} %copy-done.12), channel_id=1, source_target_pairs={{0,896},{128,0},{256,128},{384,256},{512,384},{640,512},{768,640},... | collective-permute-start | bytes 884744 | tf_op jit(solution)/shard_map/ppermute | solution.py:285
  106.6 19.2 %copy-start.7 = (bf16[1152,128]{1,0:T(8,128)(2,1)S(1)}, bf16[1152,128]{1,0:T(8,128)(2,1)}, u32[]{:S(2)}) copy-start(bf16[1152,128]{1,0:T(8,128)(2,1)} %get-tuple-element.26) | copy-start | bytes 884740
  106.7 9.9 %collective-permute-start.8 = (bf16[1152,128]{1,0:T(8,128)(2,1)S(1)}, bf16[1152,128]{1,0:T(8,128)(2,1)S(1)}, u32[]{:S(2)}, u32[]{:S(2)}) collective-permute-start(bf16[1152,128]{1,0:T(8,128)(2,1)S(1)} %add.15), channel_id=1, source_target_pairs={{0,128},{128,256},{256,384},{384,512},{512,640},{640,768},{768,896... | collective-permute-start | bytes 884744 | tf_op jit(solution)/shard_map/ppermute | solution.py:285
  108.7 9.9 %collective-permute-start.12 = (bf16[1152,128]{1,0:T(8,128)(2,1)S(1)}, bf16[1152,128]{1,0:T(8,128)(2,1)S(1)}, u32[]{:S(2)}, u32[]{:S(2)}) collective-permute-start(bf16[1152,128]{1,0:T(8,128)(2,1)S(1)} %add.18), channel_id=1, source_target_pairs={{0,896},{128,0},{256,128},{384,256},{512,384},{640,512},{768,640},... | collective-permute-start | bytes 884744 | tf_op jit(solution)/shard_map/ppermute | solution.py:285
  116.7 9.1 %collective-permute-start.9 = (bf16[1152,128]{1,0:T(8,128)(2,1)S(1)}, bf16[1152,128]{1,0:T(8,128)(2,1)S(1)}, u32[]{:S(2)}, u32[]{:S(2)}) collective-permute-start(bf16[1152,128]{1,0:T(8,128)(2,1)S(1)} %add.16), channel_id=1, source_target_pairs={{0,128},{128,256},{256,384},{384,512},{512,640},{640,768},{768,896... | collective-permute-start | bytes 884744 | tf_op jit(solution)/shard_map/ppermute | solution.py:285
  118.7 9.0 %collective-permute-start.13 = (bf16[1152,128]{1,0:T(8,128)(2,1)S(1)}, bf16[1152,128]{1,0:T(8,128)(2,1)S(1)}, u32[]{:S(2)}, u32[]{:S(2)}) collective-permute-start(bf16[1152,128]{1,0:T(8,128)(2,1)S(1)} %add.19), channel_id=1, source_target_pairs={{0,896},{128,0},{256,128},{384,256},{512,384},{640,512},{768,640},... | collective-permute-start | bytes 884744 | tf_op jit(solution)/shard_map/ppermute | solution.py:285
  125.8 9.0 %collective-permute-start.10 = (bf16[1152,128]{1,0:T(8,128)(2,1)S(1)}, bf16[1152,128]{1,0:T(8,128)(2,1)S(1)}, u32[]{:S(2)}, u32[]{:S(2)}) collective-permute-start(bf16[1152,128]{1,0:T(8,128)(2,1)S(1)} %add.17), channel_id=1, source_target_pairs={{0,128},{128,256},{256,384},{384,512},{512,640},{640,768},{768,896... | collective-permute-start | bytes 884744 | tf_op jit(solution)/shard_map/ppermute | solution.py:285
